TPU v7x, 32 devices: a whole 2x2x4 slice. The times are simulated.
32 devices in a mesh: fourier: 8 (over y, x, core), mer: 4 (over z).
Axes of the slice: x: 2, y: 2, z: 4, core: 2. Of those that a mesh axis runs over, the one named last changes fastest.
Arguments:
- velocity: float32 [3, 256, 64, 1024], P(None, 'fourier', None, 'mer')
- metrics: float32 [4, 64, 1024], P(None, None, 'mer'), may hold values from -0.3 to 0.3
- lumped_mass: float32 [64, 1024], P(None, 'mer'), may hold values from 0.5 to 2
- element_ops: float32 [64, 64, 1024], P(None, None, 'mer'), may hold values from -0.75 to 0.75
- boundary_map: int32 [1024, 28], P('mer'), may hold values from 0 to 13311, as said below
- block_cols: int32 [104, 4], P('mer'), may hold values from 0 to 103, as said below
- schur_blocks: float32 [104, 4, 128, 128], P('mer'), may hold values from -0.25 to 0.25
Outputs:
- element_out: float32 [3, 256, 64, 1024], P(None, 'fourier', None, 'mer')
- boundary_out: float32 [3, 256, 13312], P(None, 'fourier', 'mer')
Inputs may be any that keep to these rules, and one draw needn't show every extreme that they name: `boundary_map`: every entry of an element of slab s (elements s * 256 to (s + 1) * 256 - 1) lies from s * 3328 to (s + 1) * 3328 + 127, and for the last slab below (s + 1) * 3328; both ends are taken in every slab. `block_cols`: entry s of row r differs from r by at most 2; entry 0 is r itself.
All inputs are finite; a program needn't handle non-finite values.
Results may differ from a plain program's by a relative error of at most 0.00014.
Values sent between devices are 32-bit elements; how exact they have to be, the bound alone decides.
No kernel may reach another device: no remote copies, remote signals or barrier semaphores. Data moves between devices by JAX's collectives and lax.ppermute only.
A program may use at most 192 MiB of HBM per device.

v0:
```python
import jax
import jax.numpy as jnp
import numpy as np
from jax import lax
from jax.sharding import PartitionSpec as P

PERIM = 28
K = 256
HB = 2


gauss_nodes = [
    -1.0,
    -0.8717401485096066,
    -0.5917001814331423,
    -0.2092992179024789,
    0.2092992179024789,
    0.5917001814331423,
    0.8717401485096066,
    1.0,
]
wave_scale = 1.0 / 32.0


def passed_along(value, axis, by):
    count = lax.axis_size(axis)
    pairs = [(i, i + by) for i in range(count) if 0 <= i + by < count]
    return lax.ppermute(value, axis, pairs)


def padded(value, sides, width):
    for axis, dim in sides:
        count, length = (lax.axis_size(axis), value.shape[dim])
        up = [(i, (i + 1) % count) for i in range(count - 1)]
        down = [(j, i) for i, j in up]
        last = lax.slice_in_dim(value, length - width, length, axis=dim)
        leading = lax.slice_in_dim(value, 0, width, axis=dim)
        before = lax.ppermute(last, axis, up)
        after = lax.ppermute(leading, axis, down)
        value = jnp.concatenate([before, value, after], axis=dim)
    return value


def node_tables():
    nodes = np.array(gauss_nodes)
    count = nodes.shape[0]
    barycentric = np.array(
        [1.0 / np.prod([nodes[i] - nodes[k] for k in range(count) if k != i]) for i in range(count)]
    )
    matrix = np.zeros((count, count))
    for i in range(count):
        for j in range(count):
            if i != j:
                matrix[i, j] = barycentric[j] / barycentric[i] / (nodes[i] - nodes[j])
        matrix[i, i] = -np.sum(matrix[i])
    return (np.kron(matrix, np.eye(count)), np.kron(np.eye(count), matrix))


def perimeter_points():
    points = [8 * a + b for a in range(8) for b in range(8) if a in (0, 7) or b in (0, 7)]
    return np.array(points, dtype=np.int32)


def spectral_tables(modes):
    planes = 3 * modes // 2
    index = np.arange(modes)
    wave = np.where(index == modes - 1, modes // 2, (index + 1) // 2)
    is_sine = (index % 2 == 0) & (index > 0) & (index < modes - 1)
    theta = 2.0 * np.pi * np.arange(planes) / planes
    angle = theta[:, None] * wave[None, :]
    basis = np.where(is_sine[None, :], np.sin(angle), np.cos(angle))
    deriv = wave_scale * wave[None, :] * np.where(is_sine[None, :], np.cos(angle), -np.sin(angle))
    weight = np.where(index == 0, 1.0, 2.0) / planes
    back = (basis * weight[None, :]).T
    return (basis, deriv, back, wave)


def per_device(velocity, metrics, lumped_mass, element_ops, boundary_map, block_cols, schur_blocks):
    high = lax.Precision.HIGHEST
    modes = velocity.shape[1]
    elems = velocity.shape[3]
    groups = lax.axis_size("fourier")
    sub_elems = elems // groups
    part = lax.axis_index("fourier")
    slab = lax.axis_index("mer")
    block_rows = schur_blocks.shape[0]
    block_size = schur_blocks.shape[2]
    owned_count = block_rows * block_size
    basis, deriv, back, wave = spectral_tables(K)
    forward_table = jnp.asarray(basis, jnp.float32)
    deriv_table = jnp.asarray(deriv, jnp.float32)
    back_table = jnp.asarray(back, jnp.float32)
    deriv_r_np, deriv_s_np = node_tables()
    deriv_r = jnp.asarray(deriv_r_np, jnp.float32)
    deriv_s = jnp.asarray(deriv_s_np, jnp.float32)
    incoming = lax.all_to_all(velocity, "fourier", split_axis=3, concat_axis=1, tiled=True)
    physical = jnp.einsum("jk,fkpe->fjpe", forward_table, incoming, precision=high)
    planes = physical[:3]
    grad_z = jnp.einsum("jk,fkpe->fjpe", deriv_table, incoming, precision=high)
    local_metrics = lax.dynamic_slice_in_dim(metrics, part * sub_elems, sub_elems, 2)
    along_r = jnp.einsum("qp,fjpe->fjqe", deriv_r, planes, precision=high)
    along_s = jnp.einsum("qp,fjpe->fjqe", deriv_s, planes, precision=high)
    grad_x = local_metrics[0] * along_r + local_metrics[2] * along_s
    grad_y = local_metrics[1] * along_r + local_metrics[3] * along_s
    advection = -(planes[0:1] * grad_x + planes[1:2] * grad_y + planes[2:3] * grad_z)
    projected = jnp.einsum("kj,fjpe->fkpe", back_table, advection, precision=high)
    returned = lax.all_to_all(projected, "fourier", split_axis=1, concat_axis=3, tiled=True)
    forcing = velocity + returned
    wave_all = jnp.asarray(wave, jnp.float32)
    local_wave = lax.dynamic_slice_in_dim(wave_all, part * modes, modes)
    helm = 1.0 + 4.0 * (local_wave / (K / 2)) ** 2
    element_out = jnp.einsum("ije,fkje->fkie", element_ops, forcing, precision=high)
    element_out = element_out + helm[None, :, None, None] * lumped_mass[None, None] * forcing
    perim = perimeter_points()
    values = element_out[:, :, perim, :]
    values = jnp.transpose(values, (3, 2, 0, 1)).reshape(elems * PERIM, 3 * modes)
    local_ids = boundary_map.reshape(-1) - slab * owned_count
    partial_sums = jax.ops.segment_sum(values, local_ids, num_segments=owned_count + block_size)
    partial_sums = partial_sums.T.reshape(3, modes, owned_count + block_size)
    reach_rows = HB * block_size
    owned = partial_sums[:, :, :owned_count]
    shared = partial_sums[:, :, owned_count:]
    arrived = passed_along(shared, "mer", 1)
    owned = owned.at[:, :, :block_size].add(arrived)
    extended = padded(owned, (("mer", 2),), reach_rows)
    blocked = extended.reshape(3 * modes, block_rows + 2 * HB, block_size)
    local_cols = block_cols - slab * block_rows + HB
    picked = blocked[:, local_cols, :]
    result = jnp.einsum("rsab,frsb->fra", schur_blocks, picked, precision=high)
    boundary_out = result.reshape(3, modes, owned_count)
    return (element_out, boundary_out)


def solution(mesh):
    in_specs = (
        P(None, "fourier", None, "mer"),
        P(None, None, "mer"),
        P(None, "mer"),
        P(None, None, "mer"),
        P("mer", None),
        P("mer", None),
        P("mer", None, None, None),
    )
    out_specs = (P(None, "fourier", None, "mer"), P(None, "fourier", "mer"))
    return jax.shard_map(
        per_device, mesh=mesh, in_specs=in_specs, out_specs=out_specs, check_vma=False
    )
```

profile of v0, /device:TPU:0, one launch (start us, length us, event | category | flops | bytes accessed | tf_op | source)
XLA Modules:
  0.0 565.5 jit_solution(6990238287051673647)
XLA Ops:
  0.6 12.7 %copy.110 = f32[3,32,64,256]{2,1,0,3:T(8,128)} copy(f32[3,32,64,256]{3,2,1,0:T(8,128)} %param.17) | data formatting | bytes 12582912 | tf_op args[0]
  13.4 12.6 %reshape.114 = f32[8,1,196608]{2,1,0:T(1,128)} reshape(f32[256,3,32,64]{3,2,1,0:T(8,128)} %bitcast.101) | data formatting | bytes 12582912
  26.0 5.3 all-to-all-start
  33.5 69.6 %all-to-all-done = f32[8,1,196608]{2,1,0:T(1,128)} async-done(((f32[8,1,196608]{2,1,0:T(1,128)}), f32[8,1,196608]{2,1,0:T(1,128)}, u32[]{:S(2)}, u32[]{:S(2)}) %all-to-all-start) | async-done | bytes 6291488 | tf_op jit(solution)/shard_map/all_to_all | solution.py:96
  103.7 19.7 %reduce.2 = f32[8,196608]{1,0:T(8,128)} reduce(f32[8,1,196608]{2,1,0:T(1,128)} %all-to-all-done, f32[]{:T(128)} %broadcast.68), dimensions={1}, to_apply=%all_to_all.26.reduce_sub_computation | reduce | bytes 12582916 | tf_op jit(solution)/shard_map/all_to_all | solution.py:96
  123.4 12.2 %reshape.115 = f32[256,3,32,64]{3,2,1,0:T(8,128)} reshape(f32[8,196608]{1,0:T(8,128)} %reduce.2) | data formatting | bytes 12582912
  135.6 20.4 %copy.99 = f32[3,8,32,64,32]{3,4,2,1,0:T(8,128)} copy(f32[3,8,32,64,32]{3,2,0,4,1:T(8,128)} %bitcast.104) | data formatting | bytes 12582912 | tf_op jit(solution)/shard_map/all_to_all | solution.py:96
  155.9 11.0 %copy.100 = f32[3,256,64,32]{1,2,3,0:T(8,128)} copy(f32[3,256,64,32]{2,3,1,0:T(8,128)} %bitcast.105) | data formatting | bytes 12582912 | tf_op jit(solution)/shard_map/all_to_all | solution.py:96
  167.0 13.4 %convolution_bitcast_fusion = f32[3,384,64,32]{1,2,3,0:T(8,128)S(1)} fusion(f32[384,256,1,1]{1,0,3,2:T(8,128)S(1)} %copy-done.3, f32[3,256,64,32]{1,2,3,0:T(8,128)} %copy.100), kind=kOutput, calls=%fused_computation.18 | convolution fusion | flops 7247757312 | bytes 16121856 | tf_op jit(solution)/shard_map/jk,fkpe->fjpe/dot_general | solution.py:97
  180.4 3.7 slice_bitcast_fusion.2
  186.9 11.4 %fusion.15 = f32[3,384,32,64]{1,3,2,0:T(8,128)} fusion(f32[3,384,64,32]{1,2,3,0:T(8,128)S(1)} %convolution_bitcast_fusion, f32[64,64,1,1]{1,0,3,2:T(8,128)S(1)} %copy-done.6), kind=kOutput, calls=%fused_computation.40 | convolution fusion | flops 1811939328 | bytes 18890752 | tf_op jit(solution)/shard_map/qp,fjpe->fjqe/dot_general | solution.py:101
  198.3 12.5 %fusion.16 = f32[384,3,64,32]{0,2,3,1:T(8,128)} fusion(f32[384,256,1,1]{1,0,3,2:T(8,128)S(1)} %copy-done.2, f32[3,256,64,32]{1,2,3,0:T(8,128)S(1)} %bitcast.103), kind=kOutput, calls=%fused_computation.41 | convolution fusion | flops 7247757312 | bytes 16121856 | tf_op jit(solution)/shard_map/jk,fkpe->fjpe/dot_general | solution.py:99
  210.8 21.6 %fusion = f32[3,384,64,32]{1,2,3,0:T(8,128)} fusion(f32[3,384,32,64]{1,3,2,0:T(8,128)} %fusion.15, f32[384,3,64,32]{0,2,3,1:T(8,128)} %fusion.16, f32[384,64,32]{0,1,2:T(8,128)} %get-tuple-element.25, f32[64,32]{0,1:T(8,128)S(1)} %copy.104, f32[64,32]{0,1:T(8,128)} %copy.103, f32[384,64,32]{0,1,2:T(8,128)} %get-tuple-element.26, f32[64,32]{0,1:T(8,128)} %copy.102, ...), kind=kOutput, calls=%fused_computation.6 | convolution fusion | flops 1840250880 | bytes 47235072 | tf_op jit(solution)/shard_map/qp,fjpe->fjqe/dot_general | solution.py:102
  232.5 20.0 %fusion.8 = f32[3,256,64,32]{1,3,2,0:T(8,128)} fusion(f32[256,384,1,1]{1,0,3,2:T(8,128)S(1)} %copy-done.1, f32[3,384,64,32]{1,2,3,0:T(8,128)} %fusion), kind=kOutput, calls=%fused_computation.22 | convolution fusion | flops 7247757312 | bytes 16121856 | tf_op jit(solution)/shard_map/kj,fjpe->fkpe/dot_general | solution.py:106
  252.5 12.8 %copy.107 = f32[3,256,64,32]{2,3,0,1:T(8,128)} copy(f32[3,256,64,32]{1,3,2,0:T(8,128)} %fusion.8) | data formatting | bytes 12582912 | tf_op jit(solution)/shard_map/kj,fjpe->fkpe/transpose | solution.py:106
  265.2 12.6 %reshape.116 = f32[8,1,196608]{2,1,0:T(1,128)} reshape(f32[256,3,32,64]{3,2,1,0:T(8,128)} %bitcast.106) | data formatting | bytes 12582912
  277.9 4.9 all-to-all-start.1
  283.0 9.2 %copy.127 = f32[64,64,256,1]{1,0,3,2:T(8,128)} copy(f32[64,64,256,1]{2,1,0,3:T(8,128)} %bitcast.114) | data formatting | bytes 8388608 | tf_op args[3]
  295.0 59.4 %all-to-all-done.1 = f32[8,1,196608]{2,1,0:T(1,128)} async-done(((f32[8,1,196608]{2,1,0:T(1,128)}), f32[8,1,196608]{2,1,0:T(1,128)}, u32[]{:S(2)}, u32[]{:S(2)}) %all-to-all-start.1) | async-done | bytes 6291488 | tf_op jit(solution)/shard_map/all_to_all | solution.py:107
  354.4 19.7 %reduce.3 = f32[8,196608]{1,0:T(8,128)} reduce(f32[8,1,196608]{2,1,0:T(1,128)} %all-to-all-done.1, f32[]{:T(128)} %broadcast.68), dimensions={1}, to_apply=%all_to_all.30.reduce_sub_computation | reduce | bytes 12582916 | tf_op jit(solution)/shard_map/all_to_all | solution.py:107
  374.1 12.3 %reshape.117 = f32[256,3,32,64]{3,2,1,0:T(8,128)} reshape(f32[8,196608]{1,0:T(8,128)} %reduce.3) | data formatting | bytes 12582912
  386.3 16.4 %copy.109 = f32[3,32,64,8,32]{2,1,0,4,3:T(8,128)} copy(f32[3,32,64,8,32]{2,4,0,1,3:T(8,128)} %bitcast.107) | data formatting | bytes 12582912 | tf_op jit(solution)/shard_map/all_to_all | solution.py:107
  402.7 14.6 %bitcast_add_fusion.1 = f32[3,32,64,256]{2,1,0,3:T(8,128)} fusion(f32[3,32,64,256]{2,1,0,3:T(8,128)} %copy.110, f32[3,32,64,8,32]{2,1,0,4,3:T(8,128)} %copy.109), kind=kLoop, calls=%fused_computation.4 | loop fusion | flops 1572864 | bytes 18874368 | tf_op jit(solution)/shard_map/add | solution.py:108
  417.3 25.5 %bitcast_add_fusion = f32[3,32,64,256]{2,1,0,3:T(8,128)} fusion(f32[3,32,64,256]{2,1,0,3:T(8,128)} %bitcast_add_fusion.1, f32[32,64,256]{1,0,2:T(8,128)} %broadcast_multiply_fusion, f32[64,64,256,1]{1,0,3,2:T(8,128)} %copy.127), kind=kOutput, calls=%fused_computation.3 | convolution fusion | flops 1211105280 | bytes 18874368 | tf_op jit(solution)/shard_map/ije,fkje->fkie/dot_general | solution.py:112
  442.9 12.1 %copy.114 = f32[3,32,64,256]{3,1,0,2:T(8,128)} copy(f32[3,32,64,256]{2,1,0,3:T(8,128)} %bitcast_add_fusion) | data formatting | bytes 12582912 | tf_op jit(solution)/shard_map/add | solution.py:113
  458.5 10.0 %copy.133 = f32[256,28,3,32]{3,2,1,0:T(4,128)} copy(f32[256,28,3,32]{0,3,2,1:T(8,128)S(1)} %bitcast.109) | data formatting | bytes 5505024 | tf_op jit(solution)/shard_map/reshape | solution.py:116
  468.4 14.7 %reshape.111 = f32[7168,96]{1,0:T(8,128)} reshape(f32[256,28,3,32]{3,2,1,0:T(4,128)} %copy.133) | data formatting | bytes 5505024 | tf_op jit(solution)/shard_map/reshape | solution.py:116
  483.1 39.3 %scatter_custom_fusion = f32[3456,96]{1,0:T(8,128)S(1)} fusion(s32[7168]{0:T(1024)S(1)} %reshape.95, f32[7168,96]{1,0:T(8,128)} %reshape.111, f32[]{:T(128)} %constant.71.clone.1), kind=kCustom, calls=%fused_computation.26 | custom fusion | flops 688128 | bytes 1327616 | tf_op jit(solution)/shard_map/scatter-add | solution.py:118
  523.0 4.4 collective-permute-start
  530.7 4.9 collective-permute-start.1
  535.6 11.0 %copy.121 = f32[3,32,64,256]{3,2,1,0:T(8,128)} copy(f32[3,32,64,256]{2,1,0,3:T(8,128)} %bitcast_add_fusion) | data formatting | bytes 12582912
  553.4 9.8 %convolution_bitcast_fusion.1 = f32[96,26,128]{2,0,1:T(8,128)S(1)} fusion(f32[96,26,4,128]{3,0,2,1:T(8,128)} %bitcast.108, f32[26,4,128,128]{3,2,1,0:T(8,128)} %param.23), kind=kOutput, calls=%fused_computation.25 | convolution fusion | flops 1962934272 | bytes 13205504 | tf_op jit(solution)/shard_map/rsab,frsb->fra/dot_general | solution.py:129
  (60 shorter events, 24.9 us)
Async XLA Ops:
  26.0 5.3 copy-start.5
  26.0 77.1 %all-to-all-start = ((f32[8,1,196608]{2,1,0:T(1,128)}), f32[8,1,196608]{2,1,0:T(1,128)}, u32[]{:S(2)}, u32[]{:S(2)}) async-start(f32[8,1,196608]{2,1,0:T(1,128)} %reshape.114), calls=%async_computation | async-start | bytes 12582912 | tf_op jit(solution)/shard_map/all_to_all | solution.py:96
  155.9 11.0 %copy-start.3 = (f32[384,256,1,1]{1,0,3,2:T(8,128)S(1)}, f32[384,256,1,1]{1,0,3,2:T(8,128)}, u32[]{:S(2)}) copy-start(f32[384,256,1,1]{1,0,3,2:T(8,128)} %constant.89) | copy-start | bytes 1179652
  180.3 6.6 %copy-start = (f32[3,384,64,32]{1,2,3,0:T(8,128)}, f32[3,384,64,32]{1,2,3,0:T(8,128)S(1)}, u32[]{:S(2)}) copy-start(f32[3,384,64,32]{1,2,3,0:T(8,128)S(1)} %convolution_bitcast_fusion) | copy-start | bytes 28311556
  180.4 6.6 %copy-start.6 = (f32[64,64,1,1]{1,0,3,2:T(8,128)S(1)}, f32[64,64,1,1]{1,0,3,2:T(8,128)}, u32[]{:S(2)}) copy-start(f32[64,64,1,1]{1,0,3,2:T(8,128)} %constant.90) | copy-start | bytes 49156
  180.4 17.9 %slice-start = ((s8[6291456]{0:T(1024)(128)(4,1)}), s8[4194304]{0:T(1024)(128)(4,1)S(1)}, s32[]{:S(2)}) async-start(s8[6291456]{0:T(1024)(128)(4,1)} %bitcast.102), calls=%async_computation.2 | async-start | bytes 8388608
  186.9 11.4 %slice-start.1 = ((s8[6291456]{0:T(1024)(128)(4,1)}), s8[2097152]{0:T(1024)(128)(4,1)S(1)}, s32[]{:S(2)}) async-start(s8[6291456]{0:T(1024)(128)(4,1)} %bitcast.102), calls=%async_computation.3 | async-start | bytes 4194304
  186.9 11.4 %copy-start.2 = (f32[384,256,1,1]{1,0,3,2:T(8,128)S(1)}, f32[384,256,1,1]{1,0,3,2:T(8,128)}, u32[]{:S(2)}) copy-start(f32[384,256,1,1]{1,0,3,2:T(8,128)} %constant.92) | copy-start | bytes 1179652
  210.8 21.7 %copy-start.1 = (f32[256,384,1,1]{1,0,3,2:T(8,128)S(1)}, f32[256,384,1,1]{1,0,3,2:T(8,128)}, u32[]{:S(2)}) copy-start(f32[256,384,1,1]{1,0,3,2:T(8,128)} %constant.93) | copy-start | bytes 1179652
  277.9 5.0 copy-start.4
  277.9 76.5 %all-to-all-start.1 = ((f32[8,1,196608]{2,1,0:T(1,128)}), f32[8,1,196608]{2,1,0:T(1,128)}, u32[]{:S(2)}, u32[]{:S(2)}) async-start(f32[8,1,196608]{2,1,0:T(1,128)} %reshape.116), calls=%async_computation.1 | async-start | bytes 12582912 | tf_op jit(solution)/shard_map/all_to_all | solution.py:107
  282.9 9.2 %copy-start.7 = (s32[256,28]{0,1:T(8,128)S(1)}, s32[256,28]{0,1:T(8,128)}, u32[]{:S(2)}) copy-start(s32[256,28]{0,1:T(8,128)} %param.21) | copy-start | bytes 86020
  282.9 9.4 %copy-start.10 = (f32[256]{0:T(256)S(1)}, f32[256]{0:T(256)}, u32[]{:S(2)}) copy-start(f32[256]{0:T(256)} %constant.82.clone) | copy-start | bytes 3076
  283.0 9.5 %copy-start.9 = (s32[28]{0:T(128)S(1)}, s32[28]{0:T(128)}, u32[]{:S(2)}) copy-start(s32[28]{0:T(128)} %constant.88) | copy-start | bytes 340
  468.4 58.9 %copy-start.8 = (s32[26,4]{0,1:T(4,128)S(1)}, s32[26,4]{0,1:T(4,128)}, u32[]{:S(2)}) copy-start(s32[26,4]{0,1:T(4,128)} %param.22) | copy-start | bytes 1252
  523.0 6.1 %collective-permute-start = (f32[3,32,128]{2,1,0:T(8,128)S(1)}, f32[3,32,128]{2,1,0:T(8,128)S(1)}, u32[]{:S(2)}, u32[]{:S(2)}) collective-permute-start(f32[3,32,128]{2,1,0:T(8,128)S(1)} %slice.79), channel_id=1, source_target_pairs={{0,1},{1,2},{2,3},{4,5},{5,6},{6,7},{8,9},{9,10},{10,11},{12,13},{... | collective-permute-start | bytes 147464 | tf_op jit(solution)/shard_map/ppermute | solution.py:28
  529.1 17.4 %collective-permute-start.2 = (f32[3,32,256]{2,1,0:T(8,128)S(1)}, f32[3,32,256]{2,1,0:T(8,128)S(1)}, u32[]{:S(2)}, u32[]{:S(2)}) collective-permute-start(f32[3,32,256]{2,1,0:T(8,128)S(1)} %get-tuple-element.28), channel_id=1, source_target_pairs={{1,0},{2,1},{3,2},{5,4},{6,5},{7,6},{9,8},{10,9},{11,10},{13,12},{... | collective-permute-start | bytes 294920 | tf_op jit(solution)/shard_map/ppermute | solution.py:39
  530.7 15.9 %collective-permute-start.1 = (f32[3,32,256]{2,1,0:T(8,128)S(1)}, f32[3,32,256]{2,1,0:T(8,128)S(1)}, u32[]{:S(2)}, u32[]{:S(2)}) collective-permute-start(f32[3,32,256]{2,1,0:T(8,128)S(1)} %get-tuple-element.27), channel_id=1, source_target_pairs={{0,1},{1,2},{2,3},{4,5},{5,6},{6,7},{8,9},{9,10},{10,11},{12,13},{... | collective-permute-start | bytes 294920 | tf_op jit(solution)/shard_map/ppermute | solution.py:38
where the time goes:
time: 571 us; the launch traced here: 566 us
  local copies, waits for them, and re-layouts  202 us (35%)
  waiting for transfers between devices  130 us (23%)
  matrix products  114 us (20%)
  other arithmetic  97.2 us (17%)
  starting transfers between devices  21 us (4%)
    unnamed x34, local copies, waits for them, and re-layouts  85.6 us
    all_to_all x1, waiting for transfers between devices, per_device(): lax.all_to_all(velocity, 'fourier', split_axis=3, concat_axis=1, tiled=True)  69.6 us
    all_to_all x1, waiting for transfers between devices, per_device(): lax.all_to_all(projected, 'fourier', split_axis=1, concat_axis=3, tiled=T...  59.4 us
    scatter-add x1, other arithmetic, per_device(): jax.ops.segment_sum(values, local_ids, num_segments=owned_count + block_s...  39.3 us
    all_to_all x3, local copies, waits for them, and re-layouts, per_device(): lax.all_to_all(velocity, 'fourier', split_axis=3, concat_axis=1, tiled=True)  32 us
    dot_general x1, matrix products, per_device(): jnp.einsum('ije,fkje->fkie', element_ops, forcing, precision=high)  25.5 us
    reshape x2, local copies, waits for them, and re-layouts, per_device(): jnp.transpose(values, (3, 2, 0, 1)).reshape(elems * PERIM, 3 * modes)  24.7 us
    dot_general x1, matrix products, per_device(): along_s = jnp.einsum('qp,fjpe->fjqe', deriv_s, planes, precision=high)  21.6 us
  transfers between devices with their start and end apart: 5, of which 3 were waited for; matrix products, arithmetic and copies ran while one was open for 5% of the time, Pallas kernels for 0%

commit v1 on v0

v1 whole, which is shorter than its diff:
```python
import functools

import jax
import jax.numpy as jnp
import numpy as np
from jax import lax
from jax.experimental import pallas as pl
from jax.experimental.pallas import tpu as pltpu
from jax.sharding import PartitionSpec as P

K = 256
HB = 2
NP = 64
ORDER = 8
LANES = 128
SUB = LANES // ORDER
WIDE = 256
COLS = NP * SUB


gauss_nodes = [
    -1.0,
    -0.8717401485096066,
    -0.5917001814331423,
    -0.2092992179024789,
    0.2092992179024789,
    0.5917001814331423,
    0.8717401485096066,
    1.0,
]
wave_scale = 1.0 / 32.0


def node_matrix():
    nodes = np.array(gauss_nodes)
    count = nodes.shape[0]
    barycentric = np.array(
        [1.0 / np.prod([nodes[i] - nodes[k] for k in range(count) if k != i]) for i in range(count)]
    )
    matrix = np.zeros((count, count))
    for i in range(count):
        for j in range(count):
            if i != j:
                matrix[i, j] = barycentric[j] / barycentric[i] / (nodes[i] - nodes[j])
        matrix[i, i] = -np.sum(matrix[i])
    return matrix


perimeter = [8 * a + b for a in range(8) for b in range(8) if a in (0, 7) or b in (0, 7)]
PERIM = len(perimeter)


def spectral_tables(modes):
    planes = 3 * modes // 2
    index = np.arange(modes)
    wave = np.where(index == modes - 1, modes // 2, (index + 1) // 2)
    is_sine = (index % 2 == 0) & (index > 0) & (index < modes - 1)
    theta = 2.0 * np.pi * np.arange(planes) / planes
    angle = theta[:, None] * wave[None, :]
    basis = np.where(is_sine[None, :], np.sin(angle), np.cos(angle))
    deriv = wave_scale * wave[None, :] * np.where(is_sine[None, :], np.cos(angle), -np.sin(angle))
    weight = np.where(index == 0, 1.0, 2.0) / planes
    back = (basis * weight[None, :]).T
    return (basis, deriv, back, wave)


def halves(table):
    table = np.asarray(table, np.float32)
    high = table.astype(jnp.bfloat16)
    low = (table - high.astype(np.float32)).astype(jnp.bfloat16)
    return jnp.asarray(high), jnp.asarray(low)


def split(value):
    high = value.astype(jnp.bfloat16)
    low = (value - high.astype(jnp.float32)).astype(jnp.bfloat16)
    return high, low


def dot(left, right):
    return jnp.dot(left, right, preferred_element_type=jnp.float32)


def dot_nt(left, right):
    return lax.dot_general(left, right, (((1,), (1,)), ((), ())), preferred_element_type=jnp.float32)


def lane_groups_swapped(rows):
    rows = list(rows)
    lane = lax.broadcasted_iota(jnp.int32, rows[0].shape, 1)
    for step in (4, 2, 1):
        lower = (lane & (step * SUB)) == 0
        for i in range(ORDER):
            if i & step:
                continue
            top, bottom = rows[i], rows[i + step]
            rows[i] = jnp.where(lower, top, pltpu.roll(bottom, step * SUB, 1))
            rows[i + step] = jnp.where(lower, pltpu.roll(top, LANES - step * SUB, 1), bottom)
    return rows


def pack_kernel(modes, v_ref, o_ref):
    for a in range(ORDER):
        rows = [v_ref[pl.ds(ORDER * a + b, modes, stride=NP), :] for b in range(ORDER)]
        for g, row in enumerate(lane_groups_swapped(rows)):
            o_ref[g, :, a * LANES : (a + 1) * LANES] = row


def pack(v2, chunk, tiles, modes, groups):
    return pl.pallas_call(
        functools.partial(pack_kernel, modes),
        out_shape=jax.ShapeDtypeStruct((groups, modes, 3 * COLS), jnp.float32),
        grid=(3, tiles),
        in_specs=[pl.BlockSpec((modes * NP, LANES), lambda f, t: (f, chunk * tiles + t))],
        out_specs=pl.BlockSpec((ORDER, modes, COLS), lambda f, t: (t, 0, f)),
        compiler_params=pltpu.CompilerParams(vmem_limit_bytes=24 << 20),
        cost_estimate=pl.CostEstimate(flops=0, transcendentals=0, bytes_accessed=8 * 3 * tiles * modes * NP * LANES),
        name="pack",
    )(v2)


def physics_kernel(planes, even, odd, x_ref, fh_ref, fl_ref, wh_ref, wl_ref, bh_ref, bl_ref, m_ref, y_ref,
                   p_ref, z_ref, s_ref, ah_ref, al_ref):
    width = 3 * COLS

    def forward(tile, carry):
        cols = pl.ds(pl.multiple_of(tile * WIDE, WIDE), WIDE)
        xh, xl = split(x_ref[:, cols])
        fh = fh_ref[...]
        both = dot(fh, xh) + dot(fl_ref[...], xh) + dot(fh, xl)
        values = both[:planes]
        p_ref[:, cols] = values
        z_ref[:, cols] = both[planes:]
        ph, plo = split(values)
        wh = wh_ref[...]
        s_ref[:, cols] = dot(ph, wh) + dot(plo, wh) + dot(ph, wl_ref[...])
        return carry

    lax.fori_loop(0, width // WIDE, forward, 0)

    step = 16

    def products(tile, carry):
        rows = pl.ds(pl.multiple_of(tile * step, step), step)

        def piece(ref, f, a):
            start = f * COLS + a * LANES
            return ref[rows, start : start + LANES]

        speed_r, speed_s, speed_z = [], [], []
        for a in range(ORDER):
            p0, p1, p2 = (piece(p_ref, f, a) for f in range(3))
            m0, m1, m2, m3 = (m_ref[ORDER * q + a : ORDER * q + a + 1, :] for q in range(4))
            speed_r.append(p0 * m0 + p1 * m1)
            speed_s.append(p0 * m2 + p1 * m3)
            speed_z.append(p2)
        for f in range(3):
            values = [piece(p_ref, f, a) for a in range(ORDER)]
            total = [values[j] + values[7 - j] for j in range(4)]
            diff = [values[j] - values[7 - j] for j in range(4)]
            for i in range(4):
                e = even[i][0] * total[0]
                o = odd[i][0] * diff[0]
                for j in range(1, 4):
                    e = e + even[i][j] * total[j]
                    o = o + odd[i][j] * diff[j]
                for a, along in ((i, o + e), (7 - i, o - e)):
                    out = speed_r[a] * along + speed_s[a] * piece(s_ref, f, a) + speed_z[a] * piece(z_ref, f, a)
                    high, low = split(out)
                    start = f * COLS + a * LANES
                    ah_ref[rows, start : start + LANES] = high
                    al_ref[rows, start : start + LANES] = low
        return carry

    lax.fori_loop(0, planes // step, products, 0)

    def backward(tile, carry):
        cols = pl.ds(pl.multiple_of(tile * WIDE, WIDE), WIDE)
        ah = ah_ref[:, cols]
        bh = bh_ref[...]
        y_ref[:, cols] = dot(bh, ah) + dot(bl_ref[...], ah) + dot(bh, al_ref[:, cols])
        return carry

    lax.fori_loop(0, width // WIDE, backward, 0)


def physics(received, metrics):
    basis, deriv, back, _ = spectral_tables(K)
    planes = basis.shape[0]
    width = 3 * COLS
    fh, fl = halves(np.concatenate([basis, deriv], axis=0))
    bh, bl = halves(-back)
    matrix = node_matrix()
    wh, wl = halves(np.kron(np.eye(WIDE // LANES), np.kron(matrix.T, np.eye(SUB))))
    flipped = matrix[:, ::-1]
    even = ((matrix + flipped) / 2)[:4, :4].astype(np.float32).tolist()
    odd = ((matrix - flipped) / 2)[:4, :4].astype(np.float32).tolist()
    return pl.pallas_call(
        functools.partial(physics_kernel, planes, even, odd),
        out_shape=jax.ShapeDtypeStruct((K, width), jnp.float32),
        in_specs=[pl.BlockSpec(memory_space=pltpu.VMEM)] * 8,
        out_specs=pl.BlockSpec(memory_space=pltpu.VMEM),
        scratch_shapes=[pltpu.VMEM((planes, width), jnp.float32)] * 3
        + [pltpu.VMEM((planes, width), jnp.bfloat16)] * 2,
        compiler_params=pltpu.CompilerParams(vmem_limit_bytes=48 << 20),
        cost_estimate=pl.CostEstimate(
            flops=6 * planes * width * (3 * K + WIDE), transcendentals=0, bytes_accessed=8 * K * width
        ),
        name="physics",
    )(received, fh, fl, wh, wl, bh, bl, metrics)


def element_kernel(modes, aliased, v_ref, r_ref, a_ref, mass_ref, helm_ref, *refs):
    o_ref, pv_ref, f_ref = refs[1:] if aliased else refs
    for a in range(ORDER):
        rows = [r_ref[g, :, a * LANES : (a + 1) * LANES] for g in range(ORDER)]
        for b, row in enumerate(lane_groups_swapped(rows)):
            p = ORDER * a + b
            f_ref[p] = v_ref[pl.ds(p, modes, stride=NP), :] + row

    block = 4

    def op_rows(tile, carry):
        first = tile * block
        sums = []
        for q in range(block):
            i = first + q
            sums.append(helm_ref[...] * mass_ref[pl.ds(i, 1), :] * f_ref[i])
        for j in range(NP):
            value = f_ref[j]
            for q in range(block):
                sums[q] = sums[q] + a_ref[pl.ds((first + q) * NP + j, 1), :] * value
        for q in range(block):
            o_ref[pl.ds(first + q, modes, stride=NP), :] = sums[q]
        return carry

    lax.fori_loop(0, NP // block, op_rows, 0)
    for t, p in enumerate(perimeter):
        pv_ref[:, t * LANES : (t + 1) * LANES] = o_ref[pl.ds(p, modes, stride=NP), :]


def element_stage(v2, received, ops2, mass, helm, previous, chunk, tiles, modes):
    aliased = previous is not None
    in_specs = [
        pl.BlockSpec((modes * NP, LANES), lambda t, f: (f, chunk * tiles + t)),
        pl.BlockSpec((ORDER, modes, COLS), lambda t, f: (t, 0, f)),
        pl.BlockSpec((NP * NP, LANES), lambda t, f: (0, chunk * tiles + t)),
        pl.BlockSpec((NP, LANES), lambda t, f: (0, chunk * tiles + t)),
        pl.BlockSpec((modes, LANES), lambda t, f: (0, 0)),
    ]
    args = [v2, received, ops2, mass, helm]
    if aliased:
        in_specs.append(pl.BlockSpec(memory_space=pl.ANY))
        args.append(previous)
    return pl.pallas_call(
        functools.partial(element_kernel, modes, aliased),
        out_shape=(
            jax.ShapeDtypeStruct(v2.shape, jnp.float32),
            jax.ShapeDtypeStruct((3 * modes, tiles * PERIM * LANES), jnp.float32),
        ),
        grid=(tiles, 3),
        in_specs=in_specs,
        out_specs=(
            pl.BlockSpec((modes * NP, LANES), lambda t, f: (f, chunk * tiles + t)),
            pl.BlockSpec((modes, PERIM * LANES), lambda t, f: (f, t)),
        ),
        scratch_shapes=[pltpu.VMEM((NP, modes, LANES), jnp.float32)],
        input_output_aliases={5: 0} if aliased else {},
        compiler_params=pltpu.CompilerParams(vmem_limit_bytes=32 << 20),
        cost_estimate=pl.CostEstimate(
            flops=2 * 3 * tiles * modes * NP * NP * LANES, transcendentals=0,
            bytes_accessed=4 * 4 * 3 * tiles * modes * NP * LANES,
        ),
        name="element",
    )(*args)


def assemble_kernel(rows, first, *refs):
    if first:
        pv_ref, ids_ref, o_ref, lhs_ref = refs
    else:
        pv_ref, ids_ref, before_ref, o_ref, lhs_ref = refs

    @pl.when(pl.program_id(0) == 0)
    def _():
        high, low = split(pv_ref[...])
        lhs_ref[:rows] = high
        lhs_ref[rows:] = low

    depth = pv_ref.shape[1]
    wanted = lax.broadcasted_iota(jnp.int32, (WIDE, LANES), 1) + pl.program_id(0) * WIDE
    total = jnp.zeros((2 * rows, WIDE), jnp.float32)
    for start in range(0, depth, WIDE):
        ids = ids_ref[start : start + WIDE, :]
        hot = [
            jnp.where(ids == wanted + LANES * h, 1.0, 0.0).astype(jnp.bfloat16)
            for h in range(WIDE // LANES)
        ]
        total = total + dot(lhs_ref[:, start : start + WIDE], jnp.concatenate(hot, axis=1))
    total = total[:rows] + total[rows:]
    o_ref[...] = total if first else before_ref[...] + total


def assemble(values, ids, before, width):
    rows, depth = values.shape
    first = before is None
    in_specs = [pl.BlockSpec(memory_space=pltpu.VMEM)] * 2
    args = [values, ids]
    if not first:
        in_specs.append(pl.BlockSpec((rows, WIDE), lambda n: (0, n)))
        args.append(before)
    return pl.pallas_call(
        functools.partial(assemble_kernel, rows, first),
        out_shape=jax.ShapeDtypeStruct((rows, width), jnp.float32),
        grid=(width // WIDE,),
        in_specs=in_specs,
        out_specs=pl.BlockSpec((rows, WIDE), lambda n: (0, n)),
        scratch_shapes=[pltpu.VMEM((2 * rows, depth), jnp.bfloat16)],
        compiler_params=pltpu.CompilerParams(vmem_limit_bytes=32 << 20),
        cost_estimate=pl.CostEstimate(
            flops=4 * rows * depth * width, transcendentals=0, bytes_accessed=4 * (2 * rows + LANES) * depth
        ),
        name="assemble",
    )(*args)


def coupling_kernel(cols_ref, x_ref, b_ref, o_ref, xh_ref, xl_ref):
    r = pl.program_id(0)

    @pl.when(r == 0)
    def _():
        high, low = split(x_ref[...])
        xh_ref[...] = high
        xl_ref[...] = low

    total = jnp.zeros(o_ref.shape, jnp.float32)
    for s in range(b_ref.shape[1]):
        at = pl.ds(pl.multiple_of(cols_ref[r, s] * LANES, LANES), LANES)
        bh, bl = split(b_ref[0, s])
        xh = xh_ref[:, at]
        total = total + dot_nt(xh, bh) + dot_nt(xl_ref[:, at], bh) + dot_nt(xh, bl)
    o_ref[...] = total


def coupling(extended, local_cols, blocks):
    rows = extended.shape[0]
    count, slots, size, _ = blocks.shape
    return pl.pallas_call(
        coupling_kernel,
        out_shape=jax.ShapeDtypeStruct((rows, count * size), jnp.float32),
        grid_spec=pltpu.PrefetchScalarGridSpec(
            num_scalar_prefetch=1,
            grid=(count,),
            in_specs=[
                pl.BlockSpec(extended.shape, lambda r, c: (0, 0)),
                pl.BlockSpec((1, slots, size, size), lambda r, c: (r, 0, 0, 0)),
            ],
            out_specs=pl.BlockSpec((rows, size), lambda r, c: (0, r)),
            scratch_shapes=[pltpu.VMEM(extended.shape, jnp.bfloat16)] * 2,
        ),
        compiler_params=pltpu.CompilerParams(vmem_limit_bytes=32 << 20),
        cost_estimate=pl.CostEstimate(
            flops=6 * rows * slots * size * size * count, transcendentals=0,
            bytes_accessed=4 * slots * size * size * count,
        ),
        name="coupling",
    )(local_cols, extended, blocks)


def per_device(velocity, metrics, lumped_mass, element_ops, boundary_map, block_cols, schur_blocks):
    modes, elems = velocity.shape[1], velocity.shape[3]
    groups = lax.axis_size("fourier")
    part = lax.axis_index("fourier")
    slab = lax.axis_index("mer")
    slabs = lax.axis_size("mer")
    block_rows, block_size = schur_blocks.shape[0], schur_blocks.shape[2]
    owned_count = block_rows * block_size
    tiles = groups // ORDER
    chunks = elems // (tiles * LANES)

    v2 = velocity.reshape(3 * modes * NP, elems)
    ops2 = element_ops.reshape(NP * NP, elems)
    wave = jnp.asarray(spectral_tables(K)[3], jnp.float32)
    local_wave = lax.dynamic_slice_in_dim(wave, part * modes, modes)
    helm = 1.0 + 4.0 * (local_wave / (K / 2)) ** 2
    helm = jnp.broadcast_to(helm[:, None], (modes, LANES))
    ids = boundary_map - slab * owned_count
    ids = ids.reshape(chunks, tiles, LANES, PERIM).transpose(0, 1, 3, 2).reshape(chunks, -1)
    ids = jnp.broadcast_to(ids[:, :, None], ids.shape + (LANES,))
    width = -(-(owned_count + block_size) // WIDE) * WIDE

    returned = []
    for chunk in range(chunks):
        sent = pack(v2, chunk, tiles, modes, groups)
        got = lax.all_to_all(sent, "fourier", split_axis=0, concat_axis=0, tiled=True)
        first = (chunk * tiles + part // ORDER) * LANES + (part % ORDER) * SUB
        local_metrics = lax.dynamic_slice_in_dim(metrics, first, SUB, 2).reshape(4 * ORDER, LANES)
        projected = physics(got.reshape(K, 3 * COLS), local_metrics)
        back = lax.all_to_all(
            projected.reshape(groups, modes, 3 * COLS), "fourier", split_axis=0, concat_axis=0, tiled=True
        )
        returned.append(back)

    out, sums = None, None
    for chunk in range(chunks):
        out, values = element_stage(v2, returned[chunk], ops2, lumped_mass, helm, out, chunk, tiles, modes)
        sums = assemble(values, ids[chunk], sums, width)

    reach = HB * block_size
    up = [(i, i + 1) for i in range(slabs - 1)]
    down = [(i + 1, i) for i in range(slabs - 1)]
    from_below = lax.ppermute(sums[:, owned_count - reach : owned_count + block_size], "mer", up)
    from_above = lax.ppermute(sums[:, :reach], "mer", down)
    start = sums[:, :block_size] + from_below[:, reach:]
    after = from_above[:, :block_size] + sums[:, owned_count : owned_count + block_size]
    extended = jnp.concatenate(
        [from_below[:, :reach], start, sums[:, block_size:owned_count], after, from_above[:, block_size:]], axis=1
    )
    local_cols = block_cols - slab * block_rows + HB
    boundary_out = coupling(extended, local_cols, schur_blocks)
    return (out.reshape(velocity.shape), boundary_out.reshape(3, modes, owned_count))


def solution(mesh):
    in_specs = (
        P(None, "fourier", None, "mer"),
        P(None, None, "mer"),
        P(None, "mer"),
        P(None, None, "mer"),
        P("mer", None),
        P("mer", None),
        P("mer", None, None, None),
    )
    out_specs = (P(None, "fourier", None, "mer"), P(None, "fourier", "mer"))
    return jax.shard_map(
        per_device, mesh=mesh, in_specs=in_specs, out_specs=out_specs, check_vma=False
    )
```

time: 571 us -> 248 us (0.43)
  local copies, waits for them, and re-layouts: 202 us -> 27.4 us
  Pallas kernels: 0 us -> 134 us
  matrix products: 114 us -> 0 us
  other arithmetic: 97.2 us -> 0.11 us
  waiting for transfers between devices: 130 us -> 60.2 us
    pallas_call x0 -> x9, Pallas kernels: none -> 134 us  [the longest x2 51.6 us: element_stage(): pl.pallas_call(functools.partial(element_kernel, modes, aliased), out_sha...]
    dot_general x7 -> x0, matrix products: 114 us -> none  [the longest x1 25.5 us: per_device(): jnp.einsum('ije,fkje->fkie', element_ops, forcing, precision=high)]
    all_to_all x2 -> x4, waiting for transfers between devices: 129 us -> 55.1 us  [the longest x2 44.3 us: per_device(): lax.all_to_all(sent, 'fourier', split_axis=0, concat_axis=0, tiled=True)]
    unnamed x34 -> x56, local copies, waits for them, and re-layouts: 85.6 us -> 23.6 us
    all_to_all x4 -> x0, local copies, waits for them, and re-layouts: 48.3 us -> none  [the longest x3 32 us: per_device(): lax.all_to_all(velocity, 'fourier', split_axis=3, concat_axis=1, tiled=True)]
    scatter-add x2 -> x0, other arithmetic: 39.3 us -> none  [the longest x1 39.3 us: per_device(): jax.ops.segment_sum(values, local_ids, num_segments=owned_count + block_s...]
    all_to_all x2 -> x0, other arithmetic: 39.3 us -> none  [the longest x1 19.7 us: per_device(): lax.all_to_all(velocity, 'fourier', split_axis=3, concat_axis=1, tiled=True)]
    reshape x5 -> x3, local copies, waits for them, and re-layouts: 28.4 us -> 1.11 us  [the longest x2 1.09 us: per_device(): lax.dynamic_slice_in_dim(metrics, first, SUB, 2).reshape(4 * ORDER, LANES)]
  transfers between devices with their start and end apart: 5 -> 6, of which waited for: 3 -> 5; matrix products, arithmetic and copies ran while one was open for 5% -> 1% of each run, Pallas kernels for 0% -> 32%
where the time goes in v1:
time: 248 us; the launch traced here: 247 us
  Pallas kernels  134 us (54%)
  waiting for transfers between devices  60.2 us (24%)
  local copies, waits for them, and re-layouts  27.4 us (11%)
  starting transfers between devices  23.5 us (9%)
    pallas_call x2, Pallas kernels, element_stage(): pl.pallas_call(functools.partial(element_kernel, modes, aliased), out_sha...  51.6 us
    all_to_all x2, waiting for transfers between devices, per_device(): lax.all_to_all(sent, 'fourier', split_axis=0, concat_axis=0, tiled=True)  44.3 us
    pallas_call x2, Pallas kernels, physics(): pl.pallas_call(functools.partial(physics_kernel, planes, even, odd), out_...  39.3 us
    unnamed x56, local copies, waits for them, and re-layouts  23.6 us
    pallas_call x2, Pallas kernels, assemble(): pl.pallas_call(functools.partial(assemble_kernel, rows, first), out_shape...  16.2 us
    pallas_call x1, Pallas kernels, coupling(): pl.pallas_call(coupling_kernel, out_shape=jax.ShapeDtypeStruct((rows, cou...  14.5 us
    pallas_call x2, Pallas kernels, pack(): pl.pallas_call(functools.partial(pack_kernel, modes), out_shape=jax.Shape...  12.9 us
    all_to_all x2, waiting for transfers between devices, per_device(): lax.all_to_all(projected.reshape(groups, modes, 3 * COLS), 'fourier', spl...  10.8 us
  transfers between devices with their start and end apart: 6, of which 5 were waited for; matrix products, arithmetic and copies ran while one was open for 1% of the time, Pallas kernels for 32%

profile of v1, /device:TPU:0, one launch (start us, length us, event | category | flops | bytes accessed | tf_op | source)
XLA Modules:
  0.0 246.7 jit_solution(5371583769590348977)
XLA Ops:
  0.6 2.8 %copy-done = f32[3,32,64,256]{3,2,1,0:T(8,128)S(1)} copy-done((f32[3,32,64,256]{3,2,1,0:T(8,128)S(1)}, f32[3,32,64,256]{3,2,1,0:T(8,128)}, u32[]{:S(2)}) %copy-start) | copy-done | bytes 6291480
  3.4 6.4 %pack.3 = f32[8,32,3072]{2,1,0:T(8,128)} custom-call(f32[6144,256]{1,0:T(8,128)S(1)} %bitcast.13), custom_call_target="tpu_custom_call" | custom-call | bytes 6291456 | tf_op jit(solution)/shard_map/pack/pallas_call | solution.py:110
  9.9 5.2 %all-to-all-start.2 = ((f32[8,32,3072]{2,1,0:T(8,128)}), f32[8,32,3072]{2,1,0:T(8,128)}, u32[]{:S(2)}, u32[]{:S(2)}) async-start(f32[8,32,3072]{2,1,0:T(8,128)} %pack.3), calls=%async_computation.2 | async-start | bytes 6291456 | tf_op jit(solution)/shard_map/all_to_all | solution.py:395
  15.0 2.8 %copy-done.1 = f32[3,32,64,256]{3,2,1,0:T(8,128)S(1)} copy-done((f32[3,32,64,256]{3,2,1,0:T(8,128)S(1)}, f32[3,32,64,256]{3,2,1,0:T(8,128)}, u32[]{:S(2)}) %copy-start.1) | copy-done | bytes 6291480
  17.8 6.4 %pack.2 = f32[8,32,3072]{2,1,0:T(8,128)} custom-call(f32[6144,256]{1,0:T(8,128)S(1)} %bitcast.14), custom_call_target="tpu_custom_call" | custom-call | bytes 6291456 | tf_op jit(solution)/shard_map/pack/pallas_call | solution.py:110
  24.3 28.7 %all-to-all-done.2 = f32[8,32,3072]{2,1,0:T(8,128)} async-done(((f32[8,32,3072]{2,1,0:T(8,128)}), f32[8,32,3072]{2,1,0:T(8,128)}, u32[]{:S(2)}, u32[]{:S(2)}) %all-to-all-start.2) | async-done | bytes 3145760 | tf_op jit(solution)/shard_map/all_to_all | solution.py:395
  53.0 4.4 %all-to-all-start = ((f32[8,32,3072]{2,1,0:T(8,128)}), f32[8,32,3072]{2,1,0:T(8,128)}, u32[]{:S(2)}, u32[]{:S(2)}) async-start(f32[8,32,3072]{2,1,0:T(8,128)} %pack.2), calls=%async_computation | async-start | bytes 6291456 | tf_op jit(solution)/shard_map/all_to_all | solution.py:395
  58.5 19.6 %physics.3 = f32[256,3072]{1,0:T(8,128)S(1)} custom-call(f32[256,3072]{1,0:T(8,128)} %bitcast.4.x_ref, bf16[768,256]{1,0:T(8,128)(2,1)S(1)} %copy-done.9, bf16[768,256]{1,0:T(8,128)(2,1)S(1)} %copy-done.10, bf16[256,256]{1,0:T(8,128)(2,1)S(1)} %copy-done.16, bf16[256,256]{1,0:T(8,128)(2,1)S(1)} %copy-done.18, bf16[256,384]{1,0:T(8,128)(2,1)S(1)} %copy-done.12, ...), custom_call_target="tpu_custom_call" | custom-call | flops 7247757312 | bytes 6291456 | tf_op jit(solution)/shard_map/physics/pallas_call | solution.py:198
  78.1 1.7 copy-done.7
  79.8 15.6 %all-to-all-done = f32[8,32,3072]{2,1,0:T(8,128)} async-done(((f32[8,32,3072]{2,1,0:T(8,128)}), f32[8,32,3072]{2,1,0:T(8,128)}, u32[]{:S(2)}, u32[]{:S(2)}) %all-to-all-start) | async-done | bytes 3145760 | tf_op jit(solution)/shard_map/all_to_all | solution.py:395
  95.4 3.6 %all-to-all-start.3 = ((f32[8,32,3072]{2,1,0:T(8,128)}), f32[8,32,3072]{2,1,0:T(8,128)S(1)}, u32[]{:S(2)}, u32[]{:S(2)}) async-start(f32[8,32,3072]{2,1,0:T(8,128)} %bitcast.22), calls=%async_computation.3 | async-start | bytes 6291456 | tf_op jit(solution)/shard_map/all_to_all | solution.py:399
  99.0 1.0 reshape.47.m_ref
  100.0 1.0 copy-done.11
  101.0 0.9 copy-done.13
  102.0 0.9 copy-done.15
  104.7 19.6 %physics.2 = f32[256,3072]{1,0:T(8,128)S(1)} custom-call(f32[256,3072]{1,0:T(8,128)} %bitcast.1.x_ref, bf16[768,256]{1,0:T(8,128)(2,1)S(1)} %copy-done.9, bf16[768,256]{1,0:T(8,128)(2,1)S(1)} %copy-done.11, bf16[256,256]{1,0:T(8,128)(2,1)S(1)} %copy-done.17, bf16[256,256]{1,0:T(8,128)(2,1)S(1)} %copy-done.19, bf16[256,384]{1,0:T(8,128)(2,1)S(1)} %copy-done.13, ...), custom_call_target="tpu_custom_call" | custom-call | flops 7247757312 | bytes 6291456 | tf_op jit(solution)/shard_map/physics/pallas_call | solution.py:198
  124.4 1.6 copy-done.6
  126.0 10.8 %all-to-all-done.3.r_ref = f32[8,32,3072]{2,1,0:T(8,128)S(1)} async-done(((f32[8,32,3072]{2,1,0:T(8,128)}), f32[8,32,3072]{2,1,0:T(8,128)S(1)}, u32[]{:S(2)}, u32[]{:S(2)}) %all-to-all-start.3) | async-done | bytes 3145760 | tf_op jit(solution)/shard_map/all_to_all | solution.py:399
  136.8 4.8 %all-to-all-start.1 = ((f32[8,32,3072]{2,1,0:T(8,128)}), f32[8,32,3072]{2,1,0:T(8,128)}, u32[]{:S(2)}, u32[]{:S(2)}) async-start(f32[8,32,3072]{2,1,0:T(8,128)} %bitcast.21), calls=%async_computation.1 | async-start | bytes 6291456 | tf_op jit(solution)/shard_map/all_to_all | solution.py:399
  142.6 2.8 %copy-done.2 = f32[3,32,64,256]{3,2,1,0:T(8,128)S(1)} copy-done((f32[3,32,64,256]{3,2,1,0:T(8,128)S(1)}, f32[3,32,64,256]{3,2,1,0:T(8,128)}, u32[]{:S(2)}) %copy-start.2) | copy-done | bytes 6291480
  145.4 2.2 copy-done.4
  147.6 25.4 %element.2 = (f32[6144,256]{1,0:T(8,128)}, f32[96,3584]{1,0:T(8,128)S(1)}) custom-call(f32[6144,256]{1,0:T(8,128)S(1)} %bitcast.15, f32[8,32,3072]{2,1,0:T(8,128)S(1)} %all-to-all-done.3.r_ref, f32[4096,256]{1,0:T(8,128)S(1)} %bitcast.17, f32[64,256]{1,0:T(8,128)S(1)} %copy-done.8, f32[32,128]{1,0:T(8,128)S(1)} %broadcast_in_dim.17.helm_ref), custom_call_target="tpu_custom_call" | custom-call | flops 100663296 | bytes 12582912 | tf_op jit(solution)/shard_map/element/pallas_call | solution.py:255
  173.5 8.0 %assemble.2.refs_2_ = f32[96,3584]{1,0:T(8,128)S(1)} custom-call(f32[96,3584]{1,0:T(8,128)S(1)} %get-tuple-element.9.refs_0_, s32[3584,128]{1,0:T(8,128)S(1)} %broadcast_in_dim.21.refs_1_), custom_call_target="tpu_custom_call" | custom-call | flops 4932501504 | bytes 4587520 | tf_op jit(solution)/shard_map/assemble/pallas_call | solution.py:312
  181.6 2.8 %copy-done.3 = f32[3,32,64,256]{3,2,1,0:T(8,128)S(1)} copy-done((f32[3,32,64,256]{3,2,1,0:T(8,128)S(1)}, f32[3,32,64,256]{3,2,1,0:T(8,128)}, u32[]{:S(2)}) %copy-start.3) | copy-done | bytes 6291480
  184.3 2.2 copy-done.5
  186.5 26.2 %element.3 = (f32[6144,256]{1,0:T(8,128)}, f32[96,3584]{1,0:T(8,128)S(1)}) custom-call(f32[6144,256]{1,0:T(8,128)S(1)} %bitcast.16, f32[8,32,3072]{2,1,0:T(8,128)} %all-to-all-done.1.r_ref, f32[4096,256]{1,0:T(8,128)S(1)} %bitcast.18, f32[64,256]{1,0:T(8,128)S(1)} %copy-done.8, ...), custom_call_target="tpu_custom_call", output_to_operand_aliasing={{0}: (5, {})} | custom-call | flops 100663296 | bytes 12582912 | tf_op jit(solution)/shard_map/element/pallas_call | solution.py:255
  213.3 8.2 %assemble.3 = f32[96,3584]{1,0:T(8,128)S(1)} custom-call(f32[96,3584]{1,0:T(8,128)S(1)} %get-tuple-element.8.refs_0_, s32[3584,128]{1,0:T(8,128)S(1)} %broadcast_in_dim.19.refs_1_, f32[96,3584]{1,0:T(8,128)S(1)} %assemble.2.refs_2_), custom_call_target="tpu_custom_call" | custom-call | flops 4932501504 | bytes 4587520 | tf_op jit(solution)/shard_map/assemble/pallas_call | solution.py:312
  221.5 4.1 %collective-permute-start = (f32[96,384]{1,0:T(8,128)S(1)}, f32[96,384]{1,0:T(8,128)S(1)}, u32[]{:S(2)}, u32[]{:S(2)}) collective-permute-start(f32[96,384]{1,0:T(8,128)S(1)} %slice.50), channel_id=1, source_target_pairs={{0,1},{1,2},{2,3},{4,5},{5,6},{6,7},{8,9},{9,10},{10,11},{12,13},{... | collective-permute-start | bytes 442376 | tf_op jit(solution)/shard_map/ppermute | solution.py:412
  225.7 1.3 collective-permute-start.1
  227.0 2.1 collective-permute-done
  229.2 3.0 %collective-permute-done.1 = f32[96,256]{1,0:T(8,128)S(1)} collective-permute-done((f32[96,256]{1,0:T(8,128)S(1)}, f32[96,256]{1,0:T(8,128)S(1)}, u32[]{:S(2)}, u32[]{:S(2)}) %collective-permute-start.1) | collective-permute-done | bytes 98336 | tf_op jit(solution)/shard_map/ppermute | solution.py:413
  232.2 14.5 %coupling.1 = f32[96,3328]{1,0:T(8,128)} custom-call(s32[26,4]{1,0:T(8,128)S(1)} %broadcast_add_fusion.cols_ref, f32[96,3840]{1,0:T(8,128)S(1)} %slice_dynamic-update-slice_fusion.2.x_ref, f32[26,4,128,128]{3,2,1,0:T(8,128)S(1)} %bitcast.20), custom_call_target="tpu_custom_call" | custom-call | flops 981467136 | bytes 6815744 | tf_op jit(solution)/shard_map/coupling/pallas_call | solution.py:348
  (64 shorter events, 4.9 us)
Async XLA Ops:
  0.6 2.8 %copy-start = (f32[3,32,64,256]{3,2,1,0:T(8,128)S(1)}, f32[3,32,64,256]{3,2,1,0:T(8,128)}, u32[]{:S(2)}) copy-start(f32[3,32,64,256]{3,2,1,0:T(8,128)} %param.20) | copy-start | bytes 18874372
  9.9 43.2 %all-to-all-start.2 = ((f32[8,32,3072]{2,1,0:T(8,128)}), f32[8,32,3072]{2,1,0:T(8,128)}, u32[]{:S(2)}, u32[]{:S(2)}) async-start(f32[8,32,3072]{2,1,0:T(8,128)} %pack.3), calls=%async_computation.2 | async-start | bytes 6291456 | tf_op jit(solution)/shard_map/all_to_all | solution.py:395
  15.0 2.8 %copy-start.1 = (f32[3,32,64,256]{3,2,1,0:T(8,128)S(1)}, f32[3,32,64,256]{3,2,1,0:T(8,128)}, u32[]{:S(2)}) copy-start(f32[3,32,64,256]{3,2,1,0:T(8,128)} %param.20) | copy-start | bytes 18874372
  24.2 33.3 %copy-start.20 = (f32[4,64,256]{2,1,0:T(8,128)S(1)}, f32[4,64,256]{2,1,0:T(8,128)}, u32[]{:S(2)}) copy-start(f32[4,64,256]{2,1,0:T(8,128)} %param.21) | copy-start | bytes 786436
  24.2 34.2 %copy-start.9 = (bf16[768,256]{1,0:T(8,128)(2,1)S(1)}, bf16[768,256]{1,0:T(8,128)(2,1)}, u32[]{:S(2)}) copy-start(bf16[768,256]{1,0:T(8,128)(2,1)} %constant.77.clone.fh_ref) | copy-start | bytes 1179652
  24.2 34.2 %copy-start.10 = (bf16[768,256]{1,0:T(8,128)(2,1)S(1)}, bf16[768,256]{1,0:T(8,128)(2,1)}, u32[]{:S(2)}) copy-start(bf16[768,256]{1,0:T(8,128)(2,1)} %constant.78.clone.fl_ref) | copy-start | bytes 1179652
  24.2 34.2 %copy-start.12 = (bf16[256,384]{1,0:T(8,128)(2,1)S(1)}, bf16[256,384]{1,0:T(8,128)(2,1)}, u32[]{:S(2)}) copy-start(bf16[256,384]{1,0:T(8,128)(2,1)} %constant.79.clone.bh_ref) | copy-start | bytes 589828
  24.2 34.2 %copy-start.14 = (bf16[256,384]{1,0:T(8,128)(2,1)S(1)}, bf16[256,384]{1,0:T(8,128)(2,1)}, u32[]{:S(2)}) copy-start(bf16[256,384]{1,0:T(8,128)(2,1)} %constant.80.clone.bl_ref) | copy-start | bytes 589828
  24.3 34.2 %copy-start.16 = (bf16[256,256]{1,0:T(8,128)(2,1)S(1)}, bf16[256,256]{1,0:T(8,128)(2,1)}, u32[]{:S(2)}) copy-start(bf16[256,256]{1,0:T(8,128)(2,1)} %constant.81.clone.wh_ref) | copy-start | bytes 393220
  24.3 34.2 %copy-start.18 = (bf16[256,256]{1,0:T(8,128)(2,1)S(1)}, bf16[256,256]{1,0:T(8,128)(2,1)}, u32[]{:S(2)}) copy-start(bf16[256,256]{1,0:T(8,128)(2,1)} %constant.82.clone.wl_ref) | copy-start | bytes 393220
  53.0 42.3 %all-to-all-start = ((f32[8,32,3072]{2,1,0:T(8,128)}), f32[8,32,3072]{2,1,0:T(8,128)}, u32[]{:S(2)}, u32[]{:S(2)}) async-start(f32[8,32,3072]{2,1,0:T(8,128)} %pack.2), calls=%async_computation | async-start | bytes 6291456 | tf_op jit(solution)/shard_map/all_to_all | solution.py:395
  78.1 1.7 copy-start.7
  95.4 41.5 %all-to-all-start.3 = ((f32[8,32,3072]{2,1,0:T(8,128)}), f32[8,32,3072]{2,1,0:T(8,128)S(1)}, u32[]{:S(2)}, u32[]{:S(2)}) async-start(f32[8,32,3072]{2,1,0:T(8,128)} %bitcast.22), calls=%async_computation.3 | async-start | bytes 6291456 | tf_op jit(solution)/shard_map/all_to_all | solution.py:399
  100.0 1.0 copy-start.11
  101.0 0.9 copy-start.13
  102.0 0.9 copy-start.15
  102.9 0.9 copy-start.17
  124.3 1.6 copy-start.6
  136.8 4.8 %copy-start.22 = (s32[256,28]{0,1:T(8,128)S(1)}, s32[256,28]{0,1:T(8,128)}, u32[]{:S(2)}) copy-start(s32[256,28]{0,1:T(8,128)} %param.24) | copy-start | bytes 86020
  136.8 4.9 %copy-start.23 = (s32[26,4]{0,1:T(4,128)S(1)}, s32[26,4]{0,1:T(4,128)}, u32[]{:S(2)}) copy-start(s32[26,4]{0,1:T(4,128)} %param.25) | copy-start | bytes 1252
  136.8 5.6 %copy-start.24 = (f32[256]{0:T(256)S(1)}, f32[256]{0:T(256)}, u32[]{:S(2)}) copy-start(f32[256]{0:T(256)} %constant.76.clone) | copy-start | bytes 3076
  136.8 5.8 %copy-start.8 = (f32[64,256]{1,0:T(8,128)S(1)}, f32[64,256]{1,0:T(8,128)}, u32[]{:S(2)}) copy-start(f32[64,256]{1,0:T(8,128)} %mass_ref.3) | copy-start | bytes 196612
  136.8 44.7 %all-to-all-start.1 = ((f32[8,32,3072]{2,1,0:T(8,128)}), f32[8,32,3072]{2,1,0:T(8,128)}, u32[]{:S(2)}, u32[]{:S(2)}) async-start(f32[8,32,3072]{2,1,0:T(8,128)} %bitcast.21), calls=%async_computation.1 | async-start | bytes 6291456 | tf_op jit(solution)/shard_map/all_to_all | solution.py:399
  142.6 2.8 %copy-start.2 = (f32[3,32,64,256]{3,2,1,0:T(8,128)S(1)}, f32[3,32,64,256]{3,2,1,0:T(8,128)}, u32[]{:S(2)}) copy-start(f32[3,32,64,256]{3,2,1,0:T(8,128)} %param.20) | copy-start | bytes 18874372
  145.4 2.2 copy-start.4
  181.6 2.8 %copy-start.3 = (f32[3,32,64,256]{3,2,1,0:T(8,128)S(1)}, f32[3,32,64,256]{3,2,1,0:T(8,128)}, u32[]{:S(2)}) copy-start(f32[3,32,64,256]{3,2,1,0:T(8,128)} %param.20) | copy-start | bytes 18874372
  184.3 2.2 copy-start.5
  212.7 19.5 %slice-start = ((s8[6815744]{0:T(1024)(128)(4,1)}), s8[4194304]{0:T(1024)(128)(4,1)S(1)}, s32[]{:S(2)}) async-start(s8[6815744]{0:T(1024)(128)(4,1)} %bitcast.19), calls=%async_computation.4 | async-start | bytes 8388608
  213.3 12.4 %copy-start.21 = (s32[26,4]{1,0:T(8,128)S(1)}, s32[26,4]{1,0:T(8,128)}, u32[]{:S(2)}) copy-start(s32[26,4]{1,0:T(8,128)} %copy.27) | copy-start | bytes 1252
  213.3 18.9 %slice-start.1 = ((s8[6815744]{0:T(1024)(128)(4,1)}), s8[2621440]{0:T(1024)(128)(4,1)S(1)}, s32[]{:S(2)}) async-start(s8[6815744]{0:T(1024)(128)(4,1)} %bitcast.19), calls=%async_computation.5 | async-start | bytes 5242880
  221.5 7.6 %collective-permute-start = (f32[96,384]{1,0:T(8,128)S(1)}, f32[96,384]{1,0:T(8,128)S(1)}, u32[]{:S(2)}, u32[]{:S(2)}) collective-permute-start(f32[96,384]{1,0:T(8,128)S(1)} %slice.50), channel_id=1, source_target_pairs={{0,1},{1,2},{2,3},{4,5},{5,6},{6,7},{8,9},{9,10},{10,11},{12,13},{... | collective-permute-start | bytes 442376 | tf_op jit(solution)/shard_map/ppermute | solution.py:412
  225.7 6.5 %collective-permute-start.1 = (f32[96,256]{1,0:T(8,128)S(1)}, f32[96,256]{1,0:T(8,128)S(1)}, u32[]{:S(2)}, u32[]{:S(2)}) collective-permute-start(f32[96,256]{1,0:T(8,128)S(1)} %slice.55), channel_id=1, source_target_pairs={{1,0},{2,1},{3,2},{5,4},{6,5},{7,6},{9,8},{10,9},{11,10},{13,12},{... | collective-permute-start | bytes 294920 | tf_op jit(solution)/shard_map/ppermute | solution.py:413
  (1 other events, 0.9 us)

commit v2 on v1

v2 whole, which is shorter than its diff:
```python
import functools

import jax
import jax.numpy as jnp
import numpy as np
from jax import lax
from jax.experimental import pallas as pl
from jax.experimental.pallas import tpu as pltpu
from jax.sharding import PartitionSpec as P

K = 256
HB = 2
NP = 64
ORDER = 8
LANES = 128
SUB = LANES // ORDER
WIDE = 256
COLS = NP * SUB
PERIM = 28
VMEM_LIMIT = 61 << 20
ASSEMBLED = 512


gauss_nodes = [
    -1.0,
    -0.8717401485096066,
    -0.5917001814331423,
    -0.2092992179024789,
    0.2092992179024789,
    0.5917001814331423,
    0.8717401485096066,
    1.0,
]
wave_scale = 1.0 / 32.0


def node_matrix():
    nodes = np.array(gauss_nodes)
    count = nodes.shape[0]
    barycentric = np.array(
        [1.0 / np.prod([nodes[i] - nodes[k] for k in range(count) if k != i]) for i in range(count)]
    )
    matrix = np.zeros((count, count))
    for i in range(count):
        for j in range(count):
            if i != j:
                matrix[i, j] = barycentric[j] / barycentric[i] / (nodes[i] - nodes[j])
        matrix[i, i] = -np.sum(matrix[i])
    return matrix


def spectral_tables(modes):
    planes = 3 * modes // 2
    index = np.arange(modes)
    wave = np.where(index == modes - 1, modes // 2, (index + 1) // 2)
    is_sine = (index % 2 == 0) & (index > 0) & (index < modes - 1)
    theta = 2.0 * np.pi * np.arange(planes) / planes
    angle = theta[:, None] * wave[None, :]
    basis = np.where(is_sine[None, :], np.sin(angle), np.cos(angle))
    deriv = wave_scale * wave[None, :] * np.where(is_sine[None, :], np.cos(angle), -np.sin(angle))
    weight = np.where(index == 0, 1.0, 2.0) / planes
    back = (basis * weight[None, :]).T
    return (basis, deriv, back, wave)


def halves(table):
    table = np.asarray(table, np.float32)
    high = table.astype(jnp.bfloat16)
    low = (table - high.astype(np.float32)).astype(jnp.bfloat16)
    return jnp.asarray(high), jnp.asarray(low)


def split(value):
    high = value.astype(jnp.bfloat16)
    low = (value - high.astype(jnp.float32)).astype(jnp.bfloat16)
    return high, low


def dot(left, right):
    return jnp.dot(left, right, preferred_element_type=jnp.float32)


def dot_nt(left, right):
    return lax.dot_general(left, right, (((1,), (1,)), ((), ())), preferred_element_type=jnp.float32)


def groups_picked(rows):
    lane = lax.broadcasted_iota(jnp.int32, rows[0].shape, 1)
    for step in (4, 2, 1):
        upper = (lane & (step * SUB)) != 0
        rows = [jnp.where(upper, rows[(i + step) % ORDER], rows[i]) for i in range(ORDER)]
    return [rows[-g % ORDER] for g in range(ORDER)]


def rolled(row, groups):
    shift = groups % ORDER * SUB
    return pltpu.roll(row, shift, 1) if shift else row


def pack_kernel(modes, v_ref, o_ref):
    for a in range(ORDER):
        rows = [v_ref[pl.ds(ORDER * a + b, modes, stride=NP), :] for b in range(ORDER)]
        rows = groups_picked([rolled(row, b) for b, row in enumerate(rows)])
        for g, row in enumerate(rows):
            o_ref[g, :, a * LANES : (a + 1) * LANES] = row


def pack(v2, chunk, tiles, modes, groups):
    return pl.pallas_call(
        functools.partial(pack_kernel, modes),
        out_shape=jax.ShapeDtypeStruct((groups, modes, 3 * COLS), jnp.float32),
        grid=(3, tiles),
        in_specs=[pl.BlockSpec((modes * NP, LANES), lambda f, t: (f, chunk * tiles + t))],
        out_specs=pl.BlockSpec((ORDER, modes, COLS), lambda f, t: (t, 0, f)),
        compiler_params=pltpu.CompilerParams(vmem_limit_bytes=VMEM_LIMIT),
        cost_estimate=pl.CostEstimate(flops=0, transcendentals=0, bytes_accessed=8 * 3 * tiles * modes * NP * LANES),
        name="pack",
    )(v2)


def physics_kernel(planes, even, odd, counts, fh_ref, fl_ref, wh_ref, wl_ref, bh_ref, bl_ref, m_ref, x_hbm, *refs):
    outs = refs[: len(counts)]
    x_ref, y_ref, p_ref, z_ref, s_ref, ah_ref, al_ref, in_sem, out_sem = refs[len(counts) :]
    width = 3 * COLS

    def arriving(tile):
        cols = pl.ds(pl.multiple_of(tile * WIDE, WIDE), WIDE)
        return pltpu.make_async_copy(x_hbm.at[:, cols], x_ref.at[:, cols], in_sem.at[tile])

    for tile in range(width // WIDE):
        arriving(tile).start()

    def forward(tile, carry):
        cols = pl.ds(pl.multiple_of(tile * WIDE, WIDE), WIDE)
        arriving(tile).wait()
        xh, xl = split(x_ref[:, cols])
        fh = fh_ref[...]
        both = dot(fh, xh) + dot(fl_ref[...], xh) + dot(fh, xl)
        values = both[:planes]
        p_ref[:, cols] = values
        z_ref[:, cols] = both[planes:]
        ph, plo = split(values)
        wh = wh_ref[...]
        s_ref[:, cols] = dot(ph, wh) + dot(plo, wh) + dot(ph, wl_ref[...])
        return carry

    lax.fori_loop(0, width // WIDE, forward, 0)

    step = 16

    def products(tile, carry):
        rows = pl.ds(pl.multiple_of(tile * step, step), step)

        def piece(ref, f, a):
            start = f * COLS + a * LANES
            return ref[rows, start : start + LANES]

        speed_r, speed_s, speed_z = [], [], []
        for a in range(ORDER):
            p0, p1, p2 = (piece(p_ref, f, a) for f in range(3))
            m0, m1, m2, m3 = (m_ref[ORDER * q + a : ORDER * q + a + 1, :] for q in range(4))
            speed_r.append(p0 * m0 + p1 * m1)
            speed_s.append(p0 * m2 + p1 * m3)
            speed_z.append(p2)
        for f in range(3):
            values = [piece(p_ref, f, a) for a in range(ORDER)]
            total = [values[j] + values[7 - j] for j in range(4)]
            diff = [values[j] - values[7 - j] for j in range(4)]
            for i in range(4):
                e = even[i][0] * total[0]
                o = odd[i][0] * diff[0]
                for j in range(1, 4):
                    e = e + even[i][j] * total[j]
                    o = o + odd[i][j] * diff[j]
                for a, along in ((i, o + e), (7 - i, o - e)):
                    out = speed_r[a] * along + speed_s[a] * piece(s_ref, f, a) + speed_z[a] * piece(z_ref, f, a)
                    high, low = split(out)
                    start = f * COLS + a * LANES
                    ah_ref[rows, start : start + LANES] = high
                    al_ref[rows, start : start + LANES] = low
        return carry

    lax.fori_loop(0, planes // step, products, 0)

    def backward(tile, carry):
        cols = pl.ds(pl.multiple_of(tile * WIDE, WIDE), WIDE)
        ah = ah_ref[:, cols]
        bh = bh_ref[...]
        y_ref[:, cols] = dot(bh, ah) + dot(bl_ref[...], ah) + dot(bh, al_ref[:, cols])
        return carry

    start, leaving = 0, []
    for n, count in enumerate(counts):
        stop = start + count * COLS
        lax.fori_loop(start // WIDE, stop // WIDE, backward, 0)
        leaving.append(pltpu.make_async_copy(y_ref.at[:, start:stop], outs[n], out_sem.at[n]))
        leaving[-1].start()
        start = stop
    for copy in leaving:
        copy.wait()


def physics(received, turn, metrics, counts):
    basis, deriv, back, _ = spectral_tables(K)
    planes = basis.shape[0]
    width = 3 * COLS
    fh, fl = halves(np.concatenate([basis, deriv], axis=0))
    bh, bl = halves(-back)
    matrix = node_matrix()
    metrics = jnp.roll(metrics, turn * SUB, 1)
    wh, wl = (jnp.roll(table, (turn, turn), (0, 1)) for table in halves(matrix.T))
    spread = [jnp.eye(n, dtype=jnp.bfloat16) for n in (WIDE // LANES, SUB)]
    wh, wl = (
        jnp.einsum("xy,bc,ef->xbeycf", spread[0], table, spread[1]).reshape(WIDE, WIDE) for table in (wh, wl)
    )
    flipped = matrix[:, ::-1]
    even = ((matrix + flipped) / 2)[:4, :4].astype(np.float32).tolist()
    odd = ((matrix - flipped) / 2)[:4, :4].astype(np.float32).tolist()
    return pl.pallas_call(
        functools.partial(physics_kernel, planes, even, odd, counts),
        out_shape=[jax.ShapeDtypeStruct((K, count * COLS), jnp.float32) for count in counts],
        in_specs=[pl.BlockSpec(memory_space=pltpu.VMEM)] * 7 + [pl.BlockSpec(memory_space=pl.ANY)],
        out_specs=[pl.BlockSpec(memory_space=pl.ANY)] * len(counts),
        scratch_shapes=[pltpu.VMEM((K, width), jnp.float32)] * 2
        + [pltpu.VMEM((planes, width), jnp.float32)] * 3
        + [pltpu.VMEM((planes, width), jnp.bfloat16)] * 2
        + [pltpu.SemaphoreType.DMA((width // WIDE,)), pltpu.SemaphoreType.DMA((len(counts),))],
        compiler_params=pltpu.CompilerParams(vmem_limit_bytes=VMEM_LIMIT),
        cost_estimate=pl.CostEstimate(
            flops=6 * planes * width * (3 * K + WIDE), transcendentals=0, bytes_accessed=8 * K * width
        ),
        name="physics",
    )(fh, fl, wh, wl, bh, bl, metrics, received)


def sublane_groups_swapped(rows):
    rows = list(rows)
    line = lax.broadcasted_iota(jnp.int32, (ORDER, LANES), 0)
    for step in (4, 2, 1):
        lower = (line & step) == 0
        for i in range(ORDER):
            if i & step:
                continue
            top, bottom = rows[i], rows[i + step]
            rows[i] = jnp.where(lower, top, pltpu.roll(bottom, step, 0))
            rows[i + step] = jnp.where(lower, pltpu.roll(top, ORDER - step, 0), bottom)
    return rows


def element_kernel(modes, aliased, v_ref, r_ref, a_ref, mass_ref, helm_ref, *refs):
    o_ref, high_ref, low_ref, f_ref = refs[1:] if aliased else refs
    bands = modes // ORDER
    for a in range(ORDER):
        rows = groups_picked([r_ref[g, :, a * LANES : (a + 1) * LANES] for g in range(ORDER)])
        rows = [rolled(row, -b) for b, row in enumerate(rows)]
        for u in range(bands):
            own = sublane_groups_swapped([v_ref[ORDER * u + k, a * ORDER : (a + 1) * ORDER, :] for k in range(ORDER)])
            for b in range(ORDER):
                f_ref[ORDER * a + b, ORDER * u : ORDER * (u + 1), :] = own[b] + rows[b][ORDER * u : ORDER * (u + 1), :]

    def op_rows(a, carry):
        first = pl.multiple_of(a * ORDER, ORDER)
        sums = []
        for b in range(ORDER):
            weight = helm_ref[...] * mass_ref[a, b : b + 1, :]
            own = f_ref[first + b]
            sums.append([(weight * own)[ORDER * u : ORDER * (u + 1), :] for u in range(bands)])
        for j in range(NP):
            value = f_ref[j]
            for b in range(ORDER):
                weight = a_ref[first + b, j : j + 1, :]
                for u in range(bands):
                    sums[b][u] = sums[b][u] + weight * value[ORDER * u : ORDER * (u + 1), :]

        def keep(b, slot):
            at = pl.ds(pl.multiple_of(slot * LANES, LANES), LANES)
            high, low = split(jnp.concatenate(sums[b], axis=0))
            high_ref[:, at] = high
            low_ref[:, at] = low

        keep(0, 2 * a)
        keep(ORDER - 1, 2 * a + 1)

        @pl.when((a == 0) | (a == ORDER - 1))
        def _():
            for b in range(1, ORDER - 1):
                keep(b, 2 * ORDER + jnp.where(a == 0, 0, ORDER - 2) + b - 1)

        for u in range(bands):
            rows = sublane_groups_swapped([sums[b][u] for b in range(ORDER)])
            for k in range(ORDER):
                o_ref[ORDER * u + k, pl.ds(first, ORDER), :] = rows[k]
        return carry

    lax.fori_loop(0, ORDER, op_rows, 0)


kept = [8 * a + b for a in range(8) for b in (0, 7)] + [8 * a + b for a in (0, 7) for b in range(1, 7)]


def element_stage(v3, received, ops, mass, helm, previous, chunk, tiles, modes, first):
    count = received.shape[2] // COLS
    aliased = previous is not None
    in_specs = [
        pl.BlockSpec((modes, NP, LANES), lambda t, f: (first + f, 0, chunk * tiles + t)),
        pl.BlockSpec((ORDER, modes, COLS), lambda t, f: (t, 0, f)),
        pl.BlockSpec((NP, NP, LANES), lambda t, f: (0, 0, chunk * tiles + t)),
        pl.BlockSpec((ORDER, ORDER, LANES), lambda t, f: (0, 0, chunk * tiles + t)),
        pl.BlockSpec((modes, LANES), lambda t, f: (0, 0)),
    ]
    args = [v3, received, ops, mass, helm]
    if aliased:
        in_specs.append(pl.BlockSpec(memory_space=pl.ANY))
        args.append(previous)
    values = jax.ShapeDtypeStruct((count * modes, tiles * PERIM * LANES), jnp.bfloat16)
    values_spec = pl.BlockSpec((modes, PERIM * LANES), lambda t, f: (f, t))
    return pl.pallas_call(
        functools.partial(element_kernel, modes, aliased),
        out_shape=(jax.ShapeDtypeStruct(v3.shape, jnp.float32), values, values),
        grid=(tiles, count),
        in_specs=in_specs,
        out_specs=(
            pl.BlockSpec((modes, NP, LANES), lambda t, f: (first + f, 0, chunk * tiles + t)),
            values_spec,
            values_spec,
        ),
        scratch_shapes=[pltpu.VMEM((NP, modes, LANES), jnp.float32)],
        input_output_aliases={5: 0} if aliased else {},
        compiler_params=pltpu.CompilerParams(vmem_limit_bytes=VMEM_LIMIT),
        cost_estimate=pl.CostEstimate(
            flops=2 * count * tiles * modes * NP * NP * LANES, transcendentals=0,
            bytes_accessed=4 * 4 * count * tiles * modes * NP * LANES,
        ),
        name="element",
    )(*args)


def assemble_kernel(parts, block, *refs):
    ids_ref, o_ref = refs[2 * parts], refs[-1]
    rows, depth = o_ref.shape[0], refs[0].shape[1]
    wanted = lax.broadcasted_iota(jnp.int32, (WIDE, LANES), 1) + pl.program_id(0) * block
    total = jnp.zeros((2 * rows, block), jnp.float32)
    for start in range(0, depth, WIDE):
        ids = ids_ref[start : start + WIDE, :] - wanted
        hot = [jnp.where(ids == LANES * h, 1.0, 0.0).astype(jnp.bfloat16) for h in range(block // LANES)]
        values = jnp.concatenate([ref[:, start : start + WIDE] for ref in refs[: 2 * parts]], axis=0)
        total = total + dot(values, jnp.concatenate(hot, axis=1))
    total = total[:rows] + total[rows:]
    o_ref[...] = total if len(refs) == 2 * parts + 2 else refs[-2][...] + total


def assemble(values, ids, before, width, block=ASSEMBLED):
    highs, lows = zip(*values)
    rows, depth = sum(high.shape[0] for high in highs), highs[0].shape[1]
    in_specs = [pl.BlockSpec(memory_space=pltpu.VMEM)] * (2 * len(values) + 1)
    args = [*highs, *lows, ids]
    if before is not None:
        in_specs.append(pl.BlockSpec((rows, block), lambda n: (0, n)))
        args.append(before)
    return pl.pallas_call(
        functools.partial(assemble_kernel, len(values), block),
        out_shape=jax.ShapeDtypeStruct((rows, width), jnp.float32),
        grid=(width // block,),
        in_specs=in_specs,
        out_specs=pl.BlockSpec((rows, block), lambda n: (0, n)),
        compiler_params=pltpu.CompilerParams(vmem_limit_bytes=32 << 20),
        cost_estimate=pl.CostEstimate(
            flops=4 * rows * depth * width, transcendentals=0, bytes_accessed=4 * (2 * rows + LANES) * depth
        ),
        name="assemble",
    )(*args)


def coupling_kernel(pair, cols_ref, at_ref, x_ref, b_ref, *refs):
    o_ref, both_ref = refs[-2:]
    step = pl.program_id(0)
    rows = x_ref.shape[0]
    slots = b_ref.shape[1]

    @pl.when(step == 0)
    def _():
        high, low = split(x_ref[...])
        both_ref[:rows] = high
        both_ref[rows:] = low

    for q in range(pair):
        r = at_ref[step] * pair + q
        total = jnp.zeros((rows, LANES), jnp.float32)
        for s in range(0, slots, 2):
            picks = [pl.ds(pl.multiple_of(cols_ref[r, s + h] * LANES, LANES), LANES) for h in range(2)]
            values = jnp.concatenate([both_ref[:, at] for at in picks], axis=1)
            bh, bl = split(jnp.concatenate([b_ref[q, s + h] for h in range(2)], axis=1))
            first = dot_nt(values, bh)
            total = total + first[:rows] + first[rows:] + dot_nt(values[:rows], bl)
        o_ref[:, q * LANES : (q + 1) * LANES] = total


def coupling(extended, local_cols, blocks, order, previous):
    rows = extended.shape[0]
    count, slots, size, _ = blocks.shape
    pair = 2
    in_specs = [
        pl.BlockSpec(extended.shape, lambda n, c, at: (0, 0)),
        pl.BlockSpec((pair, slots, size, size), lambda n, c, at: (at[n], 0, 0, 0)),
    ]
    args = [extended, blocks]
    if previous is not None:
        in_specs.append(pl.BlockSpec(memory_space=pl.ANY))
        args.append(previous)
    return pl.pallas_call(
        functools.partial(coupling_kernel, pair),
        out_shape=jax.ShapeDtypeStruct((rows, count * size), jnp.float32),
        grid_spec=pltpu.PrefetchScalarGridSpec(
            num_scalar_prefetch=2,
            grid=(len(order),),
            in_specs=in_specs,
            out_specs=pl.BlockSpec((rows, pair * size), lambda n, c, at: (0, at[n])),
            scratch_shapes=[pltpu.VMEM((2 * rows, extended.shape[1]), jnp.bfloat16)],
        ),
        input_output_aliases={4: 0} if previous is not None else {},
        compiler_params=pltpu.CompilerParams(vmem_limit_bytes=32 << 20),
        cost_estimate=pl.CostEstimate(
            flops=6 * rows * slots * size * size * pair * len(order), transcendentals=0,
            bytes_accessed=4 * slots * size * size * pair * len(order),
        ),
        name="coupling",
    )(local_cols, jnp.asarray(order, jnp.int32), *args)


def swapped(value, earlier):
    if earlier:
        value, earlier[-1] = lax.optimization_barrier((value, earlier[-1]))
    return lax.all_to_all(value, "fourier", split_axis=0, concat_axis=0, tiled=True)


def per_device(velocity, metrics, lumped_mass, element_ops, boundary_map, block_cols, schur_blocks):
    modes, elems = velocity.shape[1], velocity.shape[3]
    groups = lax.axis_size("fourier")
    part = lax.axis_index("fourier")
    slab = lax.axis_index("mer")
    slabs = lax.axis_size("mer")
    block_rows, block_size = schur_blocks.shape[0], schur_blocks.shape[2]
    owned_count = block_rows * block_size
    tiles = groups // ORDER
    chunks = elems // (tiles * LANES)

    v2 = velocity.reshape(3 * modes * NP, elems)
    v3 = velocity.reshape(3 * modes, NP, elems)
    mass = lumped_mass.reshape(ORDER, ORDER, elems)
    wave = jnp.asarray(spectral_tables(K)[3], jnp.float32)
    local_wave = lax.dynamic_slice_in_dim(wave, part * modes, modes)
    helm = 1.0 + 4.0 * (local_wave / (K / 2)) ** 2
    helm = jnp.broadcast_to(helm[:, None], (modes, LANES))
    order = np.argsort(np.argsort(kept))
    ids = jnp.stack([boundary_map[:, n] for n in order], axis=1) - slab * owned_count
    ids = ids.reshape(chunks, tiles, LANES, PERIM).transpose(0, 1, 3, 2).reshape(chunks, -1)
    ids = jnp.broadcast_to(ids[:, :, None], ids.shape + (LANES,))
    width = -(-(owned_count + block_size) // ASSEMBLED) * ASSEMBLED

    arrived = []
    for chunk in range(chunks):
        arrived.append(swapped(pack(v2, chunk, tiles, modes, groups), arrived))
    projected, order = [], []
    for chunk in range(chunks):
        first = (chunk * tiles + part // ORDER) * LANES + (part % ORDER) * SUB
        local_metrics = lax.dynamic_slice_in_dim(metrics, first, SUB, 2).reshape(4 * ORDER, LANES)
        counts = (3,) if chunk + 1 < chunks else (2, 1)
        pieces = physics(arrived[chunk].reshape(K, 3 * COLS), part % ORDER, local_metrics, counts)
        projected.append([piece.reshape(groups, modes, piece.shape[1]) for piece in pieces])
        order = [swapped(projected[chunk][0], order)]
        projected[chunk][0] = order[0]

    out, sums = None, None
    for chunk in range(chunks):
        values, first = [], 0
        if chunk + 1 == chunks:
            last = projected[chunk]
            if sums is not None:
                last[1], sums = lax.optimization_barrier((last[1], sums))
            last[1] = swapped(last[1], last[:1])
        for back in projected[chunk]:
            out, high, low = element_stage(
                v3, back, element_ops, mass, helm, out, chunk, tiles, modes, first
            )
            values.append((high, low))
            first += back.shape[2] // COLS
        sums = assemble(values, ids[chunk], sums, width)

    reach = HB * block_size
    up = [(i, i + 1) for i in range(slabs - 1)]
    down = [(i + 1, i) for i in range(slabs - 1)]
    from_below = lax.ppermute(sums[:, owned_count - reach : owned_count + block_size], "mer", up)
    from_above = lax.ppermute(sums[:, :reach], "mer", down)
    start = sums[:, :block_size] + from_below[:, reach:]
    after = from_above[:, :block_size] + sums[:, owned_count : owned_count + block_size]
    extended = jnp.concatenate(
        [from_below[:, :reach], start, sums[:, block_size:owned_count], after, from_above[:, block_size:]], axis=1
    )
    local_cols = block_cols - slab * block_rows
    pairs = block_rows // 2
    boundary_out = coupling(sums, local_cols, schur_blocks, range(2, pairs - 1), None)
    boundary_out = coupling(extended, local_cols + HB, schur_blocks, (0, 1, pairs - 1), boundary_out)
    return (out.reshape(velocity.shape), boundary_out.reshape(3, modes, owned_count))


def solution(mesh):
    in_specs = (
        P(None, "fourier", None, "mer"),
        P(None, None, "mer"),
        P(None, "mer"),
        P(None, None, "mer"),
        P("mer", None),
        P("mer", None),
        P("mer", None, None, None),
    )
    out_specs = (P(None, "fourier", None, "mer"), P(None, "fourier", "mer"))
    return jax.shard_map(
        per_device, mesh=mesh, in_specs=in_specs, out_specs=out_specs, check_vma=False
    )
```

time: 248 us -> 220 us (0.89)
  local copies, waits for them, and re-layouts: 27.4 us -> 8.82 us
  Pallas kernels: 134 us -> 118 us
  starting transfers between devices: 23.5 us -> 28.2 us
    unnamed x56 -> x41, local copies, waits for them, and re-layouts: 23.6 us -> 3.22 us
    pallas_call x2 -> x3, Pallas kernels: 51.6 us -> 42.4 us  [element_stage(): pl.pallas_call(functools.partial(element_kernel, modes, aliased), out_sha...]
    all_to_all x4 -> x5, waiting for transfers between devices: 55.1 us -> 61.1 us  [swapped(): lax.all_to_all(value, 'fourier', split_axis=0, concat_axis=0, tiled=True)]
    pallas_call x5 -> x6, Pallas kernels: 69.9 us -> 65.2 us  [the longest x2 42.9 us: physics(): pl.pallas_call(functools.partial(physics_kernel, planes, even, odd, count...]
    all_to_all x4 -> x5, starting transfers between devices: 18.1 us -> 22.8 us  [swapped(): lax.all_to_all(value, 'fourier', split_axis=0, concat_axis=0, tiled=True)]
    reshape x1 -> x2, local copies, waits for them, and re-layouts: 0.02 us -> 3.29 us  [physics(): jnp.einsum('xy,bc,ef->xbeycf', spread[0], table, spread[1])]
    ppermute x1, waiting for transfers between devices: 3.01 us -> 0.01 us  [per_device(): from_above = lax.ppermute(sums[:, :reach], 'mer', down)]
    pallas_call x2, Pallas kernels: 12.9 us -> 10.3 us  [pack(): pl.pallas_call(functools.partial(pack_kernel, modes), out_shape=jax.Shape...]
  transfers between devices with their start and end apart: 6 -> 7, of which waited for: 5 -> 4; matrix products, arithmetic and copies ran while one was open for 1% -> 3% of each run, Pallas kernels for 32% -> 43%
where the time goes in v2:
time: 220 us; the launch traced here: 219 us
  Pallas kernels  118 us (54%)
  waiting for transfers between devices  61.1 us (28%)
  starting transfers between devices  28.2 us (13%)
  local copies, waits for them, and re-layouts  8.82 us (4%)
    all_to_all x5, waiting for transfers between devices, swapped(): lax.all_to_all(value, 'fourier', split_axis=0, concat_axis=0, tiled=True)  61.1 us
    pallas_call x2, Pallas kernels, physics(): pl.pallas_call(functools.partial(physics_kernel, planes, even, odd, count...  42.9 us
    pallas_call x3, Pallas kernels, element_stage(): pl.pallas_call(functools.partial(element_kernel, modes, aliased), out_sha...  42.4 us
    all_to_all x5, starting transfers between devices, swapped(): lax.all_to_all(value, 'fourier', split_axis=0, concat_axis=0, tiled=True)  22.8 us
    pallas_call x2, Pallas kernels, assemble(): pl.pallas_call(functools.partial(assemble_kernel, len(values), block), ou...  12.9 us
    pallas_call x2, Pallas kernels, pack(): pl.pallas_call(functools.partial(pack_kernel, modes), out_shape=jax.Shape...  10.3 us
    pallas_call x2, Pallas kernels, coupling(): pl.pallas_call(functools.partial(coupling_kernel, pair), out_shape=jax.Sh...  9.33 us
  transfers between devices with their start and end apart: 7, of which 4 were waited for; matrix products, arithmetic and copies ran while one was open for 3% of the time, Pallas kernels for 43%

profile of v2, /device:TPU:0, one launch (start us, length us, event | category | flops | bytes accessed | tf_op | source)
XLA Modules:
  0.0 219.1 jit_solution(14862304721163660289)
XLA Ops:
  0.6 5.2 %pack.3 = f32[8,32,3072]{2,1,0:T(8,128)} custom-call(f32[6144,256]{1,0:T(8,128)} %bitcast.33), custom_call_target="tpu_custom_call" | custom-call | bytes 6291456 | tf_op jit(solution)/shard_map/pack/pallas_call | solution.py:109
  5.8 5.2 %all-to-all-start = ((f32[8,32,3072]{2,1,0:T(8,128)}), f32[8,32,3072]{2,1,0:T(8,128)}, u32[]{:S(2)}, u32[]{:S(2)}) async-start(f32[8,32,3072]{2,1,0:T(8,128)} %pack.3), calls=%async_computation | async-start | bytes 6291456 | tf_op jit(solution)/shard_map/all_to_all | solution.py:433
  11.0 5.2 %pack.2 = f32[8,32,3072]{2,1,0:T(8,128)} custom-call(f32[6144,256]{1,0:T(8,128)} %bitcast.34), custom_call_target="tpu_custom_call" | custom-call | bytes 6291456 | tf_op jit(solution)/shard_map/pack/pallas_call | solution.py:109
  16.1 32.8 %all-to-all-done = f32[8,32,3072]{2,1,0:T(8,128)} async-done(((f32[8,32,3072]{2,1,0:T(8,128)}), f32[8,32,3072]{2,1,0:T(8,128)}, u32[]{:S(2)}, u32[]{:S(2)}) %all-to-all-start) | async-done | bytes 3145760 | tf_op jit(solution)/shard_map/all_to_all | solution.py:433
  49.0 4.5 %all-to-all-start.1 = ((f32[8,32,3072]{2,1,0:T(8,128)}), f32[8,32,3072]{2,1,0:T(8,128)}, u32[]{:S(2)}, u32[]{:S(2)}) async-start(f32[8,32,3072]{2,1,0:T(8,128)} %pack.2), calls=%async_computation.1 | async-start | bytes 6291456 | tf_op jit(solution)/shard_map/all_to_all | solution.py:433
  54.1 1.6 reshape.130.wh_ref
  55.8 1.6 reshape.131.wl_ref
  57.7 0.7 fusion.2.m_ref
  58.4 21.8 %physics.3 = f32[256,3072]{1,0:T(8,128)} custom-call(bf16[768,256]{1,0:T(8,128)(2,1)} %constant.122.clone.fh_ref, bf16[768,256]{1,0:T(8,128)(2,1)} %constant.123.clone.fl_ref, bf16[256,256]{1,0:T(8,128)(2,1)} %reshape.130.wh_ref, bf16[256,256]{1,0:T(8,128)(2,1)} %reshape.131.wl_ref, bf16[256,384]{1,0:T(8,128)(2,1)} %constant.124.clone.bh_ref, ...), custom_call_target="tpu_custom_call" | custom-call | flops 7247757312 | bytes 6291456 | tf_op jit(solution)/shard_map/physics/pallas_call | solution.py:219
  80.2 11.1 %all-to-all-done.1 = f32[8,32,3072]{2,1,0:T(8,128)} async-done(((f32[8,32,3072]{2,1,0:T(8,128)}), f32[8,32,3072]{2,1,0:T(8,128)}, u32[]{:S(2)}, u32[]{:S(2)}) %all-to-all-start.1) | async-done | bytes 3145760 | tf_op jit(solution)/shard_map/all_to_all | solution.py:433
  91.3 4.6 %all-to-all-start.2 = ((f32[8,32,3072]{2,1,0:T(8,128)}), f32[8,32,3072]{2,1,0:T(8,128)}, u32[]{:S(2)}, u32[]{:S(2)}) async-start(f32[8,32,3072]{2,1,0:T(8,128)} %bitcast.40), calls=%async_computation.2 | async-start | bytes 6291456 | tf_op jit(solution)/shard_map/all_to_all | solution.py:433
  96.1 0.7 fusion.3.m_ref
  96.7 21.1 %physics.2 = (f32[256,2048]{1,0:T(8,128)}, f32[256,1024]{1,0:T(8,128)}) custom-call(bf16[768,256]{1,0:T(8,128)(2,1)} %constant.122.clone.fh_ref, bf16[768,256]{1,0:T(8,128)(2,1)} %constant.123.clone.fl_ref, bf16[256,256]{1,0:T(8,128)(2,1)} %reshape.130.wh_ref, bf16[256,256]{1,0:T(8,128)(2,1)} %reshape.131.wl_ref, bf16[256,384]{1,0:T(8,128)(2,1)} %constant.124.clone.bh_ref, ...), custom_call_target="tpu_custom_call" | custom-call | flops 7247757312 | bytes 6291456 | tf_op jit(solution)/shard_map/physics/pallas_call | solution.py:219
  117.8 16.0 %all-to-all-done.2.r_ref = f32[8,32,3072]{2,1,0:T(8,128)} async-done(((f32[8,32,3072]{2,1,0:T(8,128)}), f32[8,32,3072]{2,1,0:T(8,128)}, u32[]{:S(2)}, u32[]{:S(2)}) %all-to-all-start.2) | async-done | bytes 3145760 | tf_op jit(solution)/shard_map/all_to_all | solution.py:433
  133.8 4.5 %all-to-all-start.3 = ((f32[8,32,2048]{2,1,0:T(8,128)}), f32[8,32,2048]{2,1,0:T(8,128)}, u32[]{:S(2)}, u32[]{:S(2)}) async-start(f32[8,32,2048]{2,1,0:T(8,128)} %bitcast.41), calls=%async_computation.3 | async-start | bytes 4194304 | tf_op jit(solution)/shard_map/all_to_all | solution.py:433
  138.6 0.7 broadcast_in_dim.13.helm_ref
  139.2 19.5 %element.3 = (f32[96,64,256]{2,1,0:T(8,128)}, bf16[96,3584]{1,0:T(8,128)(2,1)}, bf16[96,3584]{1,0:T(8,128)(2,1)}) custom-call(f32[96,64,256]{2,1,0:T(8,128)} %bitcast.35, f32[8,32,3072]{2,1,0:T(8,128)} %all-to-all-done.2.r_ref, f32[64,64,256]{2,1,0:T(8,128)} %a_ref.5, f32[8,8,256]{2,1,0:T(8,128)} %bitcast.43, f32[32,128]{1,0:T(8,128)} %broadcast_in_dim.13.helm_ref), custom_call_target="tpu_custom_call" | custom-call | flops 100663296 | bytes 12582912 | tf_op jit(solution)/shard_map/element/pallas_call | solution.py:317
  158.8 0.5 broadcast_in_dim.30.refs_2_
  159.3 0.6 copy-done.2
  160.1 6.3 %assemble.2.refs_5_ = f32[96,3584]{1,0:T(8,128)S(1)} custom-call(bf16[96,3584]{1,0:T(8,128)(2,1)S(1)} %copy-done.2, bf16[96,3584]{1,0:T(8,128)(2,1)S(1)} %copy-done.3, s32[3584,128]{1,0:T(8,128)S(1)} %broadcast_in_dim.30.refs_2_), custom_call_target="tpu_custom_call" | custom-call | flops 4932501504 | bytes 4587520 | tf_op jit(solution)/shard_map/assemble/pallas_call | solution.py:360
  166.4 4.1 %all-to-all-start.4 = ((f32[8,32,1024]{2,1,0:T(8,128)}), f32[8,32,1024]{2,1,0:T(8,128)S(1)}, u32[]{:S(2)}, u32[]{:S(2)}) async-start(f32[8,32,1024]{2,1,0:T(8,128)} %bitcast.42), calls=%async_computation.4 | async-start | bytes 2097152 | tf_op jit(solution)/shard_map/all_to_all | solution.py:433
  170.6 14.2 %element.4 = (f32[96,64,256]{2,1,0:T(8,128)}, bf16[64,3584]{1,0:T(8,128)(2,1)}, bf16[64,3584]{1,0:T(8,128)(2,1)}) custom-call(f32[96,64,256]{2,1,0:T(8,128)} %bitcast.36, f32[8,32,2048]{2,1,0:T(8,128)} %all-to-all-done.3.r_ref, f32[64,64,256]{2,1,0:T(8,128)} %a_ref.5, f32[8,8,256]{2,1,0:T(8,128)} %bitcast.44, ...), custom_call_target="tpu_custom_call", output_to_operand_aliasing={{0}: (5, {})} | custom-call | flops 67108864 | bytes 8388608 | tf_op jit(solution)/shard_map/element/pallas_call | solution.py:317
  184.8 1.1 all-to-all-done.4.r_ref
  186.0 1.0 copy-done.8
  186.9 8.7 %element.5 = (f32[96,64,256]{2,1,0:T(8,128)}, bf16[32,3584]{1,0:T(8,128)(2,1)}, bf16[32,3584]{1,0:T(8,128)(2,1)}) custom-call(f32[96,64,256]{2,1,0:T(8,128)} %bitcast.37, f32[8,32,1024]{2,1,0:T(8,128)} %copy-done.8, f32[64,64,256]{2,1,0:T(8,128)} %a_ref.5, f32[8,8,256]{2,1,0:T(8,128)} %bitcast.45, ...), custom_call_target="tpu_custom_call", output_to_operand_aliasing={{0}: (5, {})} | custom-call | flops 33554432 | bytes 4194304 | tf_op jit(solution)/shard_map/element/pallas_call | solution.py:317
  195.7 0.5 broadcast_in_dim.32.refs_4_
  196.9 6.6 %assemble.3.x_ref = f32[96,3584]{1,0:T(8,128)S(1)} custom-call(bf16[64,3584]{1,0:T(8,128)(2,1)S(1)} %copy-done.4, bf16[32,3584]{1,0:T(8,128)(2,1)S(1)} %copy-done.6, bf16[64,3584]{1,0:T(8,128)(2,1)S(1)} %copy-done.5, bf16[32,3584]{1,0:T(8,128)(2,1)S(1)} %copy-done.7, s32[3584,128]{1,0:T(8,128)S(1)} %broadcast_in_dim.32.refs_4_, f32[96,3584]{1,0:T(8,128)S(1)} %assemble.2.refs_5_), custom_call_target="tpu_custom_call" | custom-call | flops 4932501504 | bytes 4587520 | tf_op jit(solution)/shard_map/assemble/pallas_call | solution.py:360
  203.6 4.1 %collective-permute-start = (f32[96,384]{1,0:T(8,128)S(1)}, f32[96,384]{1,0:T(8,128)S(1)}, u32[]{:S(2)}, u32[]{:S(2)}) collective-permute-start(f32[96,384]{1,0:T(8,128)S(1)} %slice.96), channel_id=1, source_target_pairs={{0,1},{1,2},{2,3},{4,5},{5,6},{6,7},{8,9},{9,10},{10,11},{12,13},{... | collective-permute-start | bytes 442376 | tf_op jit(solution)/shard_map/ppermute | solution.py:492
  207.7 1.3 collective-permute-start.1
  209.1 6.3 %coupling.2.refs_0_ = f32[96,3328]{1,0:T(8,128)} custom-call(s32[26,4]{1,0:T(8,128)S(1)} %get-tuple-element.41.cols_ref, s32[10]{0:T(128)S(1)} %copy-done.1, f32[96,3584]{1,0:T(8,128)S(1)} %assemble.3.x_ref, f32[26,4,128,128]{3,2,1,0:T(8,128)S(1)} %bitcast.32), custom_call_target="tpu_custom_call" | custom-call | flops 754974720 | bytes 5242880 | tf_op jit(solution)/shard_map/coupling/pallas_call | solution.py:410
  215.6 0.5 copy-done
  216.0 3.0 %coupling.3 = f32[96,3328]{1,0:T(8,128)} custom-call(s32[26,4]{1,0:T(8,128)S(1)} %get-tuple-element.40.cols_ref, s32[3]{0:T(128)S(1)} %copy-done, f32[96,3840]{1,0:T(8,128)S(1)} %slice_dynamic-update-slice_fusion.2.x_ref, f32[26,4,128,128]{3,2,1,0:T(8,128)S(1)} %bitcast.32, f32[96,3328]{1,0:T(8,128)} %coupling.2.refs_0_), custom_call_target="tpu_custom_call", output_to_operand_aliasing={{}: (4, {})} | custom-call | flops 226492416 | bytes 1572864 | tf_op jit(solution)/shard_map/coupling/pallas_call | solution.py:410
  (70 shorter events, 2.4 us)
Async XLA Ops:
  5.8 43.2 %all-to-all-start = ((f32[8,32,3072]{2,1,0:T(8,128)}), f32[8,32,3072]{2,1,0:T(8,128)}, u32[]{:S(2)}, u32[]{:S(2)}) async-start(f32[8,32,3072]{2,1,0:T(8,128)} %pack.3), calls=%async_computation | async-start | bytes 6291456 | tf_op jit(solution)/shard_map/all_to_all | solution.py:433
  16.1 37.4 %copy-start.13 = (bf16[16,8]{1,0:T(8,128)(2,1)S(1)}, bf16[16,8]{1,0:T(8,128)(2,1)}, u32[]{:S(2)}) copy-start(bf16[16,8]{1,0:T(8,128)(2,1)} %constant.134) | copy-start | bytes 772
  16.1 37.5 %copy-start.12 = (bf16[16,8]{1,0:T(8,128)(2,1)S(1)}, bf16[16,8]{1,0:T(8,128)(2,1)}, u32[]{:S(2)}) copy-start(bf16[16,8]{1,0:T(8,128)(2,1)} %constant.135) | copy-start | bytes 772
  49.0 42.4 %all-to-all-start.1 = ((f32[8,32,3072]{2,1,0:T(8,128)}), f32[8,32,3072]{2,1,0:T(8,128)}, u32[]{:S(2)}, u32[]{:S(2)}) async-start(f32[8,32,3072]{2,1,0:T(8,128)} %pack.2), calls=%async_computation.1 | async-start | bytes 6291456 | tf_op jit(solution)/shard_map/all_to_all | solution.py:433
  54.1 3.3 %copy-start.9 = (f32[4,64,256]{2,1,0:T(8,128)S(1)}, f32[4,64,256]{2,1,0:T(8,128)}, u32[]{:S(2)}) copy-start(f32[4,64,256]{2,1,0:T(8,128)} %param.27) | copy-start | bytes 786436
  91.3 4.7 %copy-start.10 = (s32[256,28]{0,1:T(8,128)S(1)}, s32[256,28]{0,1:T(8,128)}, u32[]{:S(2)}) copy-start(s32[256,28]{0,1:T(8,128)} %param.30) | copy-start | bytes 86020
  91.3 42.5 %all-to-all-start.2 = ((f32[8,32,3072]{2,1,0:T(8,128)}), f32[8,32,3072]{2,1,0:T(8,128)}, u32[]{:S(2)}, u32[]{:S(2)}) async-start(f32[8,32,3072]{2,1,0:T(8,128)} %bitcast.40), calls=%async_computation.2 | async-start | bytes 6291456 | tf_op jit(solution)/shard_map/all_to_all | solution.py:433
  133.8 4.5 %copy-start.14 = (f32[256]{0:T(256)S(1)}, f32[256]{0:T(256)}, u32[]{:S(2)}) copy-start(f32[256]{0:T(256)} %constant.121.clone) | copy-start | bytes 3076
  133.8 32.6 %all-to-all-start.3 = ((f32[8,32,2048]{2,1,0:T(8,128)}), f32[8,32,2048]{2,1,0:T(8,128)}, u32[]{:S(2)}, u32[]{:S(2)}) async-start(f32[8,32,2048]{2,1,0:T(8,128)} %bitcast.41), calls=%async_computation.3 | async-start | bytes 4194304 | tf_op jit(solution)/shard_map/all_to_all | solution.py:433
  158.8 1.1 copy-start.2
  158.8 1.3 copy-start.3
  166.4 4.1 %copy-start.11 = (s32[26,4]{0,1:T(4,128)S(1)}, s32[26,4]{0,1:T(4,128)}, u32[]{:S(2)}) copy-start(s32[26,4]{0,1:T(4,128)} %param.31) | copy-start | bytes 1252
  166.4 19.5 %all-to-all-start.4 = ((f32[8,32,1024]{2,1,0:T(8,128)}), f32[8,32,1024]{2,1,0:T(8,128)S(1)}, u32[]{:S(2)}, u32[]{:S(2)}) async-start(f32[8,32,1024]{2,1,0:T(8,128)} %bitcast.42), calls=%async_computation.4 | async-start | bytes 2097152 | tf_op jit(solution)/shard_map/all_to_all | solution.py:433
  186.0 1.0 copy-start.8
  195.6 1.0 copy-start.4
  195.6 1.2 copy-start.5
  195.6 1.2 copy-start.6
  195.6 1.3 copy-start.7
  195.6 13.4 %slice-start = ((s8[6815744]{0:T(1024)(128)(4,1)}), s8[4194304]{0:T(1024)(128)(4,1)S(1)}, s32[]{:S(2)}) async-start(s8[6815744]{0:T(1024)(128)(4,1)} %bitcast.31), calls=%async_computation.5 | async-start | bytes 8388608
  196.9 12.1 %slice-start.1 = ((s8[6815744]{0:T(1024)(128)(4,1)}), s8[2621440]{0:T(1024)(128)(4,1)S(1)}, s32[]{:S(2)}) async-start(s8[6815744]{0:T(1024)(128)(4,1)} %bitcast.31), calls=%async_computation.6 | async-start | bytes 5242880
  196.9 12.1 %copy-start.1 = (s32[10]{0:T(128)S(1)}, s32[10]{0:T(128)}, u32[]{:S(2)}) copy-start(s32[10]{0:T(128)} %constant.128.clone.at_ref) | copy-start | bytes 124
  203.6 11.8 %collective-permute-start = (f32[96,384]{1,0:T(8,128)S(1)}, f32[96,384]{1,0:T(8,128)S(1)}, u32[]{:S(2)}, u32[]{:S(2)}) collective-permute-start(f32[96,384]{1,0:T(8,128)S(1)} %slice.96), channel_id=1, source_target_pairs={{0,1},{1,2},{2,3},{4,5},{5,6},{6,7},{8,9},{9,10},{10,11},{12,13},{... | collective-permute-start | bytes 442376 | tf_op jit(solution)/shard_map/ppermute | solution.py:492
  207.7 7.8 %collective-permute-start.1 = (f32[96,256]{1,0:T(8,128)S(1)}, f32[96,256]{1,0:T(8,128)S(1)}, u32[]{:S(2)}, u32[]{:S(2)}) collective-permute-start(f32[96,256]{1,0:T(8,128)S(1)} %slice.101), channel_id=1, source_target_pairs={{1,0},{2,1},{3,2},{5,4},{6,5},{7,6},{9,8},{10,9},{11,10},{13,12},{... | collective-permute-start | bytes 294920 | tf_op jit(solution)/shard_map/ppermute | solution.py:493
  215.4 0.7 copy-start

commit v3 on v2

--- a/solution.py
+++ b/solution.py
@@ -97,42 +97,97 @@
     return pltpu.roll(row, shift, 1) if shift else row
 
 
-def pack_kernel(modes, v_ref, o_ref):
+def sublane_groups_swapped(rows):
+    rows = list(rows)
+    line = lax.broadcasted_iota(jnp.int32, (ORDER, LANES), 0)
+    for step in (4, 2, 1):
+        lower = (line & step) == 0
+        for i in range(ORDER):
+            if i & step:
+                continue
+            top, bottom = rows[i], rows[i + step]
+            rows[i] = jnp.where(lower, top, pltpu.roll(bottom, step, 0))
+            rows[i + step] = jnp.where(lower, pltpu.roll(top, ORDER - step, 0), bottom)
+    return rows
+
+
+def partner_order(groups):
+    return [0, 1] + sorted(range(2, groups), key=lambda s: (-bin(s >> 1).count("1"), s & 1, s))
+
+
+def partners_swapped(rows, me):
+    rows = list(rows)
+    bit = 1
+    while bit < len(rows):
+        swap = (jnp.zeros(rows[0].shape, jnp.int32) + (me & bit)) != 0
+        for i in range(len(rows)):
+            if i & bit:
+                continue
+            top, bottom = rows[i], rows[i + bit]
+            rows[i] = jnp.where(swap, bottom, top)
+            rows[i + bit] = jnp.where(swap, top, bottom)
+        bit *= 2
+    return rows
+
+
+def pack_kernel(modes, tiles, me_ref, v_ref, *o_refs):
+    me = me_ref[0]
     for a in range(ORDER):
-        rows = [v_ref[pl.ds(ORDER * a + b, modes, stride=NP), :] for b in range(ORDER)]
-        rows = groups_picked([rolled(row, b) for b, row in enumerate(rows)])
-        for g, row in enumerate(rows):
-            o_ref[g, :, a * LANES : (a + 1) * LANES] = row
-
-
-def pack(v2, chunk, tiles, modes, groups):
+        pieces = []
+        for t in range(tiles):
+            lanes = slice(t * LANES, (t + 1) * LANES)
+            bands = [
+                sublane_groups_swapped([v_ref[u + k, a * ORDER : (a + 1) * ORDER, lanes] for k in range(ORDER)])
+                for u in range(0, modes, ORDER)
+            ]
+            rows = [jnp.concatenate(band, axis=0) for band in zip(*bands)]
+            pieces += groups_picked([rolled(row, b) for b, row in enumerate(rows)])
+        pieces = partners_swapped(pieces, me)
+        for o_ref, s in zip(o_refs, partner_order(len(o_refs))):
+            o_ref[:, a * LANES : (a + 1) * LANES] = pieces[s]
+
+
+def pack(v3, me, chunk, tiles, modes, groups):
     return pl.pallas_call(
-        functools.partial(pack_kernel, modes),
-        out_shape=jax.ShapeDtypeStruct((groups, modes, 3 * COLS), jnp.float32),
-        grid=(3, tiles),
-        in_specs=[pl.BlockSpec((modes * NP, LANES), lambda f, t: (f, chunk * tiles + t))],
-        out_specs=pl.BlockSpec((ORDER, modes, COLS), lambda f, t: (t, 0, f)),
+        functools.partial(pack_kernel, modes, tiles),
+        out_shape=[jax.ShapeDtypeStruct((modes, 3 * COLS), jnp.float32)] * groups,
+        grid_spec=pltpu.PrefetchScalarGridSpec(
+            num_scalar_prefetch=1,
+            grid=(3,),
+            in_specs=[pl.BlockSpec((modes, NP, tiles * LANES), lambda f, m: (f, 0, chunk))],
+            out_specs=[pl.BlockSpec((modes, COLS), lambda f, m: (0, f))] * groups,
+        ),
         compiler_params=pltpu.CompilerParams(vmem_limit_bytes=VMEM_LIMIT),
         cost_estimate=pl.CostEstimate(flops=0, transcendentals=0, bytes_accessed=8 * 3 * tiles * modes * NP * LANES),
         name="pack",
-    )(v2)
-
-
-def physics_kernel(planes, even, odd, counts, fh_ref, fl_ref, wh_ref, wl_ref, bh_ref, bl_ref, m_ref, x_hbm, *refs):
-    outs = refs[: len(counts)]
-    x_ref, y_ref, p_ref, z_ref, s_ref, ah_ref, al_ref, in_sem, out_sem = refs[len(counts) :]
+    )(me, v3)
+
+
+def permuted(pieces):
+    groups = len(pieces)
+    return [
+        lax.ppermute(piece, "fourier", [(i, i ^ s) for i in range(groups)]) if s else piece
+        for s, piece in zip(partner_order(groups), pieces)
+    ]
+
+
+def physics_kernel(planes, even, odd, groups, counts, me_ref, fh_ref, fl_ref, wh_ref, wl_ref, bh_ref, bl_ref, m_ref,
+                   *refs):
+    pieces, outs = refs[:groups], refs[groups : groups + len(counts)]
+    x_ref, y_ref, p_ref, z_ref, s_ref, ah_ref, al_ref, in_sem, out_sem = refs[groups + len(counts) :]
+    modes = K // groups
     width = 3 * COLS
 
-    def arriving(tile):
-        cols = pl.ds(pl.multiple_of(tile * WIDE, WIDE), WIDE)
-        return pltpu.make_async_copy(x_hbm.at[:, cols], x_ref.at[:, cols], in_sem.at[tile])
-
-    for tile in range(width // WIDE):
-        arriving(tile).start()
+    arriving = []
+    for n, partner in enumerate(partner_order(groups)):
+        rows = pl.ds(pl.multiple_of((me_ref[0] ^ partner) * modes, modes), modes)
+        arriving.append(pltpu.make_async_copy(pieces[n], x_ref.at[rows, :], in_sem.at[n]))
+        arriving[n].start()
+    for copy in arriving:
+        copy.wait()
 
     def forward(tile, carry):
         cols = pl.ds(pl.multiple_of(tile * WIDE, WIDE), WIDE)
-        arriving(tile).wait()
         xh, xl = split(x_ref[:, cols])
         fh = fh_ref[...]
         both = dot(fh, xh) + dot(fl_ref[...], xh) + dot(fh, xl)
@@ -200,7 +255,8 @@
         copy.wait()
 
 
-def physics(received, turn, metrics, counts):
+def physics(received, me, turn, metrics, counts):
+    groups = len(received)
     basis, deriv, back, _ = spectral_tables(K)
     planes = basis.shape[0]
     width = 3 * COLS
@@ -217,34 +273,22 @@
     even = ((matrix + flipped) / 2)[:4, :4].astype(np.float32).tolist()
     odd = ((matrix - flipped) / 2)[:4, :4].astype(np.float32).tolist()
     return pl.pallas_call(
-        functools.partial(physics_kernel, planes, even, odd, counts),
+        functools.partial(physics_kernel, planes, even, odd, groups, counts),
         out_shape=[jax.ShapeDtypeStruct((K, count * COLS), jnp.float32) for count in counts],
-        in_specs=[pl.BlockSpec(memory_space=pltpu.VMEM)] * 7 + [pl.BlockSpec(memory_space=pl.ANY)],
+        in_specs=[pl.BlockSpec(memory_space=pltpu.SMEM)]
+        + [pl.BlockSpec(memory_space=pltpu.VMEM)] * 7
+        + [pl.BlockSpec(memory_space=pl.ANY)] * groups,
         out_specs=[pl.BlockSpec(memory_space=pl.ANY)] * len(counts),
         scratch_shapes=[pltpu.VMEM((K, width), jnp.float32)] * 2
         + [pltpu.VMEM((planes, width), jnp.float32)] * 3
         + [pltpu.VMEM((planes, width), jnp.bfloat16)] * 2
-        + [pltpu.SemaphoreType.DMA((width // WIDE,)), pltpu.SemaphoreType.DMA((len(counts),))],
+        + [pltpu.SemaphoreType.DMA((groups,)), pltpu.SemaphoreType.DMA((len(counts),))],
         compiler_params=pltpu.CompilerParams(vmem_limit_bytes=VMEM_LIMIT),
         cost_estimate=pl.CostEstimate(
             flops=6 * planes * width * (3 * K + WIDE), transcendentals=0, bytes_accessed=8 * K * width
         ),
         name="physics",
-    )(fh, fl, wh, wl, bh, bl, metrics, received)
-
-
-def sublane_groups_swapped(rows):
-    rows = list(rows)
-    line = lax.broadcasted_iota(jnp.int32, (ORDER, LANES), 0)
-    for step in (4, 2, 1):
-        lower = (line & step) == 0
-        for i in range(ORDER):
-            if i & step:
-                continue
-            top, bottom = rows[i], rows[i + step]
-            rows[i] = jnp.where(lower, top, pltpu.roll(bottom, step, 0))
-            rows[i + step] = jnp.where(lower, pltpu.roll(top, ORDER - step, 0), bottom)
-    return rows
+    )(me, fh, fl, wh, wl, bh, bl, metrics, *received)
 
 
 def element_kernel(modes, aliased, v_ref, r_ref, a_ref, mass_ref, helm_ref, *refs):
@@ -444,7 +488,6 @@
     tiles = groups // ORDER
     chunks = elems // (tiles * LANES)
 
-    v2 = velocity.reshape(3 * modes * NP, elems)
     v3 = velocity.reshape(3 * modes, NP, elems)
     mass = lumped_mass.reshape(ORDER, ORDER, elems)
     wave = jnp.asarray(spectral_tables(K)[3], jnp.float32)
@@ -457,16 +500,27 @@
     ids = jnp.broadcast_to(ids[:, :, None], ids.shape + (LANES,))
     width = -(-(owned_count + block_size) // ASSEMBLED) * ASSEMBLED
 
-    arrived = []
+    me = jnp.reshape(part, (1,))
+    arrived, source = [], v3
     for chunk in range(chunks):
-        arrived.append(swapped(pack(v2, chunk, tiles, modes, groups), arrived))
+        got = permuted(pack(source, me, chunk, tiles, modes, groups))
+        if chunk + 1 < chunks:
+            source, got[1] = lax.optimization_barrier((v3, got[1]))
+        arrived.append(got)
+
+    for now, later in zip(arrived, arrived[1:]):
+        now[0], later[1] = lax.optimization_barrier((now[0], later[1]))
+
     projected, order = [], []
     for chunk in range(chunks):
         first = (chunk * tiles + part // ORDER) * LANES + (part % ORDER) * SUB
         local_metrics = lax.dynamic_slice_in_dim(metrics, first, SUB, 2).reshape(4 * ORDER, LANES)
         counts = (3,) if chunk + 1 < chunks else (2, 1)
-        pieces = physics(arrived[chunk].reshape(K, 3 * COLS), part % ORDER, local_metrics, counts)
+        pieces = physics(arrived[chunk], me, part % ORDER, local_metrics, counts)
         projected.append([piece.reshape(groups, modes, piece.shape[1]) for piece in pieces])
+        if chunk + 1 < chunks:
+            both = (projected[chunk][0], arrived[chunk + 1])
+            projected[chunk][0], arrived[chunk + 1] = lax.optimization_barrier(both)
         order = [swapped(projected[chunk][0], order)]
         projected[chunk][0] = order[0]
 

time: 220 us -> 206 us (0.936)
  waiting for transfers between devices: 61.1 us -> 40.6 us
  starting transfers between devices: 28.2 us -> 33.4 us
    all_to_all x5 -> x3, waiting for transfers between devices: 61.1 us -> 16.3 us  [swapped(): lax.all_to_all(value, 'fourier', split_axis=0, concat_axis=0, tiled=True)]
    ppermute x0 -> x14, waiting for transfers between devices: none -> 24.3 us  [permuted(): lax.ppermute(piece, 'fourier', [(i, i ^ s) for i in range(groups)])]
    ppermute x0 -> x14, starting transfers between devices: none -> 15.6 us  [permuted(): lax.ppermute(piece, 'fourier', [(i, i ^ s) for i in range(groups)])]
    all_to_all x5 -> x3, starting transfers between devices: 22.8 us -> 13 us  [swapped(): lax.all_to_all(value, 'fourier', split_axis=0, concat_axis=0, tiled=True)]
  transfers between devices with their start and end apart: 7 -> 19, of which waited for: 4 -> 8; matrix products, arithmetic and copies ran while one was open for 3% -> 4% of each run, Pallas kernels for 43% -> 47%
where the time goes in v3:
time: 206 us
  Pallas kernels  120 us (58%)
  waiting for transfers between devices  40.6 us (20%)
  starting transfers between devices  33.4 us (16%)
  local copies, waits for them, and re-layouts  8.86 us (4%)
    pallas_call x2, Pallas kernels, physics(): pl.pallas_call(functools.partial(physics_kernel, planes, even, odd, group...  44.5 us
    pallas_call x3, Pallas kernels, element_stage(): pl.pallas_call(functools.partial(element_kernel, modes, aliased), out_sha...  42.4 us
    ppermute x14, waiting for transfers between devices, permuted(): lax.ppermute(piece, 'fourier', [(i, i ^ s) for i in range(groups)])  24.3 us
    all_to_all x3, waiting for transfers between devices, swapped(): lax.all_to_all(value, 'fourier', split_axis=0, concat_axis=0, tiled=True)  16.3 us
    ppermute x14, starting transfers between devices, permuted(): lax.ppermute(piece, 'fourier', [(i, i ^ s) for i in range(groups)])  15.6 us
    all_to_all x3, starting transfers between devices, swapped(): lax.all_to_all(value, 'fourier', split_axis=0, concat_axis=0, tiled=True)  13 us
    pallas_call x2, Pallas kernels, assemble(): pl.pallas_call(functools.partial(assemble_kernel, len(values), block), ou...  12.9 us
    pallas_call x2, Pallas kernels, pack(): pl.pallas_call(functools.partial(pack_kernel, modes, tiles), out_shape=[j...  10.5 us
  transfers between devices with their start and end apart: 19, of which 8 were waited for; matrix products, arithmetic and copies ran while one was open for 4% of the time, Pallas kernels for 47%

profile of v3, /device:TPU:0, one launch (start us, length us, event | category | flops | bytes accessed | tf_op | source)
XLA Modules:
  0.0 205.7 jit_solution(5521616432465494158)
XLA Ops:
  0.7 5.2 %pack.2 = (f32[32,3072]{1,0:T(8,128)}, f32[32,3072]{1,0:T(8,128)}, f32[32,3072]{1,0:T(8,128)}, f32[32,3072]{1,0:T(8,128)}, f32[32,3072]{1,0:T(8,128)}, /*index=5...) custom-call(s32[1]{0:T(128)} %bitcast.1.me_ref, f32[96,64,256]{2,1,0:T(8,128)} %bitcast.31), custom_call_target="tpu_custom_call" | custom-call | bytes 6291456 | tf_op jit(solution)/shard_map/pack/pallas_call | solution.py:151
  6.4 3.5 %collective-permute-start.2 = (f32[32,3072]{1,0:T(8,128)}, f32[32,3072]{1,0:T(8,128)S(1)}, u32[]{:S(2)}, u32[]{:S(2)}) collective-permute-start(f32[32,3072]{1,0:T(8,128)} %get-tuple-element.54), channel_id=1, source_target_pairs={{0,24},{4,28},{8,16},{12,20},{16,8},{20,12},{24,0},{28,4},{1,25},{... | collective-permute-start | bytes 1179656 | tf_op jit(solution)/shard_map/ppermute | solution.py:169
  9.9 1.7 collective-permute-start.4
  11.6 1.5 collective-permute-start.5
  13.3 5.3 %pack.3 = (f32[32,3072]{1,0:T(8,128)}, f32[32,3072]{1,0:T(8,128)}, f32[32,3072]{1,0:T(8,128)}, f32[32,3072]{1,0:T(8,128)}, f32[32,3072]{1,0:T(8,128)}, /*index=5...) custom-call(s32[1]{0:T(128)} %bitcast.1.me_ref, f32[96,64,256]{2,1,0:T(8,128)} %bitcast.32), custom_call_target="tpu_custom_call" | custom-call | bytes 6291456 | tf_op jit(solution)/shard_map/pack/pallas_call | solution.py:151
  18.9 1.2 collective-permute-done.2.refs_2_
  20.8 7.3 %collective-permute-done.3.refs_3_ = f32[32,3072]{1,0:T(8,128)S(1)} collective-permute-done((f32[32,3072]{1,0:T(8,128)}, f32[32,3072]{1,0:T(8,128)S(1)}, u32[]{:S(2)}, u32[]{:S(2)}) %collective-permute-start.3) | collective-permute-done | bytes 393248 | tf_op jit(solution)/shard_map/ppermute | solution.py:169
  28.1 1.8 collective-permute-start.7
  29.9 1.5 collective-permute-start.10
  31.6 1.6 reshape.125.wh_ref
  33.3 1.7 reshape.126.wl_ref
  35.9 1.6 collective-permute-done.4.refs_4_
  38.1 6.9 %collective-permute-done.6.refs_6_ = f32[32,3072]{1,0:T(8,128)} collective-permute-done((f32[32,3072]{1,0:T(8,128)}, f32[32,3072]{1,0:T(8,128)}, u32[]{:S(2)}, u32[]{:S(2)}) %collective-permute-start.6) | collective-permute-done | bytes 393248 | tf_op jit(solution)/shard_map/ppermute | solution.py:169
  45.8 2.7 %collective-permute-start.8 = (f32[32,3072]{1,0:T(8,128)S(1)}, f32[32,3072]{1,0:T(8,128)}, u32[]{:S(2)}, u32[]{:S(2)}) collective-permute-start(f32[32,3072]{1,0:T(8,128)S(1)} %copy-done.19), channel_id=1, source_target_pairs={{0,24},{4,28},{8,16},{12,20},{16,8},{20,12},{24,0},{28,4},{1,25},{... | collective-permute-start | bytes 1179656 | tf_op jit(solution)/shard_map/ppermute | solution.py:169
  48.5 5.8 %collective-permute-done.10.refs_4_ = f32[32,3072]{1,0:T(8,128)} collective-permute-done((f32[32,3072]{1,0:T(8,128)}, f32[32,3072]{1,0:T(8,128)}, u32[]{:S(2)}, u32[]{:S(2)}) %collective-permute-start.10) | collective-permute-done | bytes 393248 | tf_op jit(solution)/shard_map/ppermute | solution.py:169
  54.6 22.6 %physics.2 = f32[256,3072]{1,0:T(8,128)} custom-call(s32[1]{0:T(128)} %bitcast.1.me_ref, bf16[768,256]{1,0:T(8,128)(2,1)} %constant.122.clone.fh_ref, bf16[768,256]{1,0:T(8,128)(2,1)} %constant.123.clone.fl_ref, bf16[256,256]{1,0:T(8,128)(2,1)} %reshape.125.wh_ref, bf16[256,256]{1,0:T(8,128)(2,1)} %reshape.126.wl_ref, ...), custom_call_target="tpu_custom_call" | custom-call | flops 7247757312 | bytes 6291456 | tf_op jit(solution)/shard_map/physics/pallas_call | solution.py:275
  77.3 1.4 collective-permute-done.9.refs_3_
  78.7 4.5 %all-to-all-start = ((f32[8,32,3072]{2,1,0:T(8,128)}), f32[8,32,3072]{2,1,0:T(8,128)}, u32[]{:S(2)}, u32[]{:S(2)}) async-start(f32[8,32,3072]{2,1,0:T(8,128)} %bitcast.38), calls=%async_computation | async-start | bytes 6291456 | tf_op jit(solution)/shard_map/all_to_all | solution.py:477
  84.0 21.9 %physics.3 = (f32[256,2048]{1,0:T(8,128)}, f32[256,1024]{1,0:T(8,128)}) custom-call(s32[1]{0:T(128)} %bitcast.1.me_ref, bf16[768,256]{1,0:T(8,128)(2,1)} %constant.122.clone.fh_ref, bf16[768,256]{1,0:T(8,128)(2,1)} %constant.123.clone.fl_ref, bf16[256,256]{1,0:T(8,128)(2,1)} %reshape.125.wh_ref, bf16[256,256]{1,0:T(8,128)(2,1)} %reshape.126.wl_ref, ...), custom_call_target="tpu_custom_call" | custom-call | flops 7247757312 | bytes 6291456 | tf_op jit(solution)/shard_map/physics/pallas_call | solution.py:275
  105.9 15.1 %all-to-all-done.r_ref = f32[8,32,3072]{2,1,0:T(8,128)} async-done(((f32[8,32,3072]{2,1,0:T(8,128)}), f32[8,32,3072]{2,1,0:T(8,128)}, u32[]{:S(2)}, u32[]{:S(2)}) %all-to-all-start) | async-done | bytes 3145760 | tf_op jit(solution)/shard_map/all_to_all | solution.py:477
  121.0 4.5 %all-to-all-start.1 = ((f32[8,32,2048]{2,1,0:T(8,128)}), f32[8,32,2048]{2,1,0:T(8,128)}, u32[]{:S(2)}, u32[]{:S(2)}) async-start(f32[8,32,2048]{2,1,0:T(8,128)} %bitcast.39), calls=%async_computation.1 | async-start | bytes 4194304 | tf_op jit(solution)/shard_map/all_to_all | solution.py:477
  126.5 19.5 %element.3 = (f32[96,64,256]{2,1,0:T(8,128)}, bf16[96,3584]{1,0:T(8,128)(2,1)}, bf16[96,3584]{1,0:T(8,128)(2,1)}) custom-call(f32[96,64,256]{2,1,0:T(8,128)} %bitcast.33, f32[8,32,3072]{2,1,0:T(8,128)} %all-to-all-done.r_ref, f32[64,64,256]{2,1,0:T(8,128)} %a_ref.5, f32[8,8,256]{2,1,0:T(8,128)} %bitcast.41, f32[32,128]{1,0:T(8,128)} %broadcast_in_dim.13.helm_ref), custom_call_target="tpu_custom_call" | custom-call | flops 100663296 | bytes 12582912 | tf_op jit(solution)/shard_map/element/pallas_call | solution.py:361
  147.3 6.3 %assemble.2.refs_5_ = f32[96,3584]{1,0:T(8,128)S(1)} custom-call(bf16[96,3584]{1,0:T(8,128)(2,1)S(1)} %copy-done.2, bf16[96,3584]{1,0:T(8,128)(2,1)S(1)} %copy-done.3, s32[3584,128]{1,0:T(8,128)S(1)} %broadcast_in_dim.30.refs_2_), custom_call_target="tpu_custom_call" | custom-call | flops 4932501504 | bytes 4587520 | tf_op jit(solution)/shard_map/assemble/pallas_call | solution.py:404
  153.7 4.1 %all-to-all-start.2 = ((f32[8,32,1024]{2,1,0:T(8,128)}), f32[8,32,1024]{2,1,0:T(8,128)S(1)}, u32[]{:S(2)}, u32[]{:S(2)}) async-start(f32[8,32,1024]{2,1,0:T(8,128)} %bitcast.40), calls=%async_computation.2 | async-start | bytes 2097152 | tf_op jit(solution)/shard_map/all_to_all | solution.py:477
  157.9 14.2 %element.4 = (f32[96,64,256]{2,1,0:T(8,128)}, bf16[64,3584]{1,0:T(8,128)(2,1)}, bf16[64,3584]{1,0:T(8,128)(2,1)}) custom-call(f32[96,64,256]{2,1,0:T(8,128)} %bitcast.34, f32[8,32,2048]{2,1,0:T(8,128)} %all-to-all-done.1.r_ref, f32[64,64,256]{2,1,0:T(8,128)} %a_ref.5, f32[8,8,256]{2,1,0:T(8,128)} %bitcast.42, ...), custom_call_target="tpu_custom_call", output_to_operand_aliasing={{0}: (5, {})} | custom-call | flops 67108864 | bytes 8388608 | tf_op jit(solution)/shard_map/element/pallas_call | solution.py:361
  172.0 1.2 all-to-all-done.2.r_ref
  174.2 8.7 %element.5 = (f32[96,64,256]{2,1,0:T(8,128)}, bf16[32,3584]{1,0:T(8,128)(2,1)}, bf16[32,3584]{1,0:T(8,128)(2,1)}) custom-call(f32[96,64,256]{2,1,0:T(8,128)} %bitcast.35, f32[8,32,1024]{2,1,0:T(8,128)} %copy-done.8, f32[64,64,256]{2,1,0:T(8,128)} %a_ref.5, f32[8,8,256]{2,1,0:T(8,128)} %bitcast.43, ...), custom_call_target="tpu_custom_call", output_to_operand_aliasing={{0}: (5, {})} | custom-call | flops 33554432 | bytes 4194304 | tf_op jit(solution)/shard_map/element/pallas_call | solution.py:361
  184.2 6.6 %assemble.3.x_ref = f32[96,3584]{1,0:T(8,128)S(1)} custom-call(bf16[64,3584]{1,0:T(8,128)(2,1)S(1)} %copy-done.4, bf16[32,3584]{1,0:T(8,128)(2,1)S(1)} %copy-done.6, bf16[64,3584]{1,0:T(8,128)(2,1)S(1)} %copy-done.5, bf16[32,3584]{1,0:T(8,128)(2,1)S(1)} %copy-done.7, s32[3584,128]{1,0:T(8,128)S(1)} %broadcast_in_dim.32.refs_4_, f32[96,3584]{1,0:T(8,128)S(1)} %assemble.2.refs_5_), custom_call_target="tpu_custom_call" | custom-call | flops 4932501504 | bytes 4587520 | tf_op jit(solution)/shard_map/assemble/pallas_call | solution.py:404
  190.8 3.5 %collective-permute-start.14 = (f32[96,384]{1,0:T(8,128)S(1)}, f32[96,384]{1,0:T(8,128)S(1)}, u32[]{:S(2)}, u32[]{:S(2)}) collective-permute-start(f32[96,384]{1,0:T(8,128)S(1)} %slice.96), channel_id=1, source_target_pairs={{0,1},{1,2},{2,3},{4,5},{5,6},{6,7},{8,9},{9,10},{10,11},{12,13},{... | collective-permute-start | bytes 442376 | tf_op jit(solution)/shard_map/ppermute | solution.py:546
  194.3 1.3 collective-permute-start.15
  195.7 6.3 %coupling.2.refs_0_ = f32[96,3328]{1,0:T(8,128)} custom-call(s32[26,4]{1,0:T(8,128)S(1)} %get-tuple-element.95.cols_ref, s32[10]{0:T(128)S(1)} %copy-done.1, f32[96,3584]{1,0:T(8,128)S(1)} %assemble.3.x_ref, f32[26,4,128,128]{3,2,1,0:T(8,128)S(1)} %bitcast.30), custom_call_target="tpu_custom_call" | custom-call | flops 754974720 | bytes 5242880 | tf_op jit(solution)/shard_map/coupling/pallas_call | solution.py:454
  202.7 3.0 %coupling.3 = f32[96,3328]{1,0:T(8,128)} custom-call(s32[26,4]{1,0:T(8,128)S(1)} %get-tuple-element.94.cols_ref, s32[3]{0:T(128)S(1)} %copy-done, f32[96,3840]{1,0:T(8,128)S(1)} %slice_dynamic-update-slice_fusion.2.x_ref, f32[26,4,128,128]{3,2,1,0:T(8,128)S(1)} %bitcast.30, f32[96,3328]{1,0:T(8,128)} %coupling.2.refs_0_), custom_call_target="tpu_custom_call", output_to_operand_aliasing={{}: (4, {})} | custom-call | flops 226492416 | bytes 1572864 | tf_op jit(solution)/shard_map/coupling/pallas_call | solution.py:454
  (116 shorter events, 10.4 us)
Async XLA Ops:
  0.6 12.5 %copy-start.13 = (bf16[16,8]{1,0:T(8,128)(2,1)S(1)}, bf16[16,8]{1,0:T(8,128)(2,1)}, u32[]{:S(2)}) copy-start(bf16[16,8]{1,0:T(8,128)(2,1)} %constant.134) | copy-start | bytes 772
  0.6 12.6 %copy-start.12 = (bf16[16,8]{1,0:T(8,128)(2,1)S(1)}, bf16[16,8]{1,0:T(8,128)(2,1)}, u32[]{:S(2)}) copy-start(bf16[16,8]{1,0:T(8,128)(2,1)} %constant.135) | copy-start | bytes 772
  5.8 7.5 %collective-permute-start = (f32[32,3072]{1,0:T(8,128)}, f32[32,3072]{1,0:T(8,128)S(1)}, u32[]{:S(2)}, u32[]{:S(2)}) collective-permute-start(f32[32,3072]{1,0:T(8,128)} %get-tuple-element.49), channel_id=1, source_target_pairs={{0,4},{4,0},{8,12},{12,8},{16,20},{20,16},{24,28},{28,24},{1,5},{5... | collective-permute-start | bytes 1179656 | tf_op jit(solution)/shard_map/ppermute | solution.py:169
  6.4 13.8 %collective-permute-start.2 = (f32[32,3072]{1,0:T(8,128)}, f32[32,3072]{1,0:T(8,128)S(1)}, u32[]{:S(2)}, u32[]{:S(2)}) collective-permute-start(f32[32,3072]{1,0:T(8,128)} %get-tuple-element.54), channel_id=1, source_target_pairs={{0,24},{4,28},{8,16},{12,20},{16,8},{20,12},{24,0},{28,4},{1,25},{... | collective-permute-start | bytes 1179656 | tf_op jit(solution)/shard_map/ppermute | solution.py:169
  9.9 18.2 %collective-permute-start.3 = (f32[32,3072]{1,0:T(8,128)}, f32[32,3072]{1,0:T(8,128)S(1)}, u32[]{:S(2)}, u32[]{:S(2)}) collective-permute-start(f32[32,3072]{1,0:T(8,128)} %get-tuple-element.55), channel_id=1, source_target_pairs={{0,28},{4,24},{8,20},{12,16},{16,12},{20,8},{24,4},{28,0},{1,29},{... | collective-permute-start | bytes 1179656 | tf_op jit(solution)/shard_map/ppermute | solution.py:169
  9.9 27.6 %collective-permute-start.4 = (f32[32,3072]{1,0:T(8,128)}, f32[32,3072]{1,0:T(8,128)}, u32[]{:S(2)}, u32[]{:S(2)}) collective-permute-start(f32[32,3072]{1,0:T(8,128)} %get-tuple-element.56), channel_id=1, source_target_pairs={{0,8},{4,12},{8,0},{12,4},{16,24},{20,28},{24,16},{28,20},{1,9},{5... | collective-permute-start | bytes 1179656 | tf_op jit(solution)/shard_map/ppermute | solution.py:169
  11.6 26.0 %collective-permute-start.5 = (f32[32,3072]{1,0:T(8,128)}, f32[32,3072]{1,0:T(8,128)}, u32[]{:S(2)}, u32[]{:S(2)}) collective-permute-start(f32[32,3072]{1,0:T(8,128)} %get-tuple-element.57), channel_id=1, source_target_pairs={{0,16},{4,20},{8,24},{12,28},{16,0},{20,4},{24,8},{28,12},{1,17},{... | collective-permute-start | bytes 1179656 | tf_op jit(solution)/shard_map/ppermute | solution.py:169
  13.3 5.3 %copy-start.14 = (f32[32,3072]{1,0:T(8,128)}, f32[32,3072]{1,0:T(8,128)S(1)}, u32[]{:S(2)}) copy-start(f32[32,3072]{1,0:T(8,128)S(1)} %collective-permute-done.refs_1_) | copy-start | bytes 1179652
  18.7 11.2 %collective-permute-start.1 = (f32[32,3072]{1,0:T(8,128)}, f32[32,3072]{1,0:T(8,128)S(1)}, u32[]{:S(2)}, u32[]{:S(2)}) collective-permute-start(f32[32,3072]{1,0:T(8,128)} %get-tuple-element.51), channel_id=1, source_target_pairs={{0,4},{4,0},{8,12},{12,8},{16,20},{20,16},{24,28},{28,24},{1,5},{5... | collective-permute-start | bytes 1179656 | tf_op jit(solution)/shard_map/ppermute | solution.py:169
  20.1 13.1 %copy-start.15 = (f32[32,3072]{1,0:T(8,128)}, f32[32,3072]{1,0:T(8,128)S(1)}, u32[]{:S(2)}) copy-start(f32[32,3072]{1,0:T(8,128)S(1)} %collective-permute-done.2.refs_2_) | copy-start | bytes 1179652
  20.2 24.9 %collective-permute-start.6 = (f32[32,3072]{1,0:T(8,128)}, f32[32,3072]{1,0:T(8,128)}, u32[]{:S(2)}, u32[]{:S(2)}) collective-permute-start(f32[32,3072]{1,0:T(8,128)} %get-tuple-element.58), channel_id=1, source_target_pairs={{0,12},{4,8},{8,4},{12,0},{16,28},{20,24},{24,20},{28,16},{1,13},{... | collective-permute-start | bytes 1179656 | tf_op jit(solution)/shard_map/ppermute | solution.py:169
  28.1 5.1 %copy-start.16 = (f32[32,3072]{1,0:T(8,128)}, f32[32,3072]{1,0:T(8,128)S(1)}, u32[]{:S(2)}) copy-start(f32[32,3072]{1,0:T(8,128)S(1)} %collective-permute-done.3.refs_3_) | copy-start | bytes 1179652
  28.1 17.7 %collective-permute-start.7 = (f32[32,3072]{1,0:T(8,128)}, f32[32,3072]{1,0:T(8,128)}, u32[]{:S(2)}, u32[]{:S(2)}) collective-permute-start(f32[32,3072]{1,0:T(8,128)} %get-tuple-element.59), channel_id=1, source_target_pairs={{0,20},{4,16},{8,28},{12,24},{16,4},{20,0},{24,12},{28,8},{1,21},{... | collective-permute-start | bytes 1179656 | tf_op jit(solution)/shard_map/ppermute | solution.py:169
  29.9 24.5 %collective-permute-start.10 = (f32[32,3072]{1,0:T(8,128)}, f32[32,3072]{1,0:T(8,128)}, u32[]{:S(2)}, u32[]{:S(2)}) collective-permute-start(f32[32,3072]{1,0:T(8,128)} %get-tuple-element.64), channel_id=1, source_target_pairs={{0,8},{4,12},{8,0},{12,4},{16,24},{20,28},{24,16},{28,20},{1,9},{5... | collective-permute-start | bytes 1179656 | tf_op jit(solution)/shard_map/ppermute | solution.py:169
  33.2 12.5 %copy-start.19 = (f32[32,3072]{1,0:T(8,128)S(1)}, f32[32,3072]{1,0:T(8,128)}, u32[]{:S(2)}) copy-start(f32[32,3072]{1,0:T(8,128)} %get-tuple-element.62) | copy-start | bytes 1179652
  33.2 21.1 %copy-start.18 = (f32[32,3072]{1,0:T(8,128)S(1)}, f32[32,3072]{1,0:T(8,128)}, u32[]{:S(2)}) copy-start(f32[32,3072]{1,0:T(8,128)} %get-tuple-element.63) | copy-start | bytes 1179652
  33.3 11.8 %copy-start.20 = (f32[32,3072]{1,0:T(8,128)S(1)}, f32[32,3072]{1,0:T(8,128)}, u32[]{:S(2)}) copy-start(f32[32,3072]{1,0:T(8,128)} %get-tuple-element.67) | copy-start | bytes 1179652
  37.5 39.7 %collective-permute-start.11 = (f32[32,3072]{1,0:T(8,128)}, f32[32,3072]{1,0:T(8,128)S(1)}, u32[]{:S(2)}, u32[]{:S(2)}) collective-permute-start(f32[32,3072]{1,0:T(8,128)} %get-tuple-element.65), channel_id=1, source_target_pairs={{0,16},{4,20},{8,24},{12,28},{16,0},{20,4},{24,8},{28,12},{1,17},{... | collective-permute-start | bytes 1179656 | tf_op jit(solution)/shard_map/ppermute | solution.py:169
  37.6 39.6 %collective-permute-start.12 = (f32[32,3072]{1,0:T(8,128)S(1)}, f32[32,3072]{1,0:T(8,128)S(1)}, u32[]{:S(2)}, u32[]{:S(2)}) collective-permute-start(f32[32,3072]{1,0:T(8,128)S(1)} %copy-done.21), channel_id=1, source_target_pairs={{0,12},{4,8},{8,4},{12,0},{16,28},{20,24},{24,20},{28,16},{1,13},{... | collective-permute-start | bytes 1179656 | tf_op jit(solution)/shard_map/ppermute | solution.py:169
  45.0 32.2 %collective-permute-start.13 = (f32[32,3072]{1,0:T(8,128)S(1)}, f32[32,3072]{1,0:T(8,128)S(1)}, u32[]{:S(2)}, u32[]{:S(2)}) collective-permute-start(f32[32,3072]{1,0:T(8,128)S(1)} %copy-done.20), channel_id=1, source_target_pairs={{0,20},{4,16},{8,28},{12,24},{16,4},{20,0},{24,12},{28,8},{1,21},{... | collective-permute-start | bytes 1179656 | tf_op jit(solution)/shard_map/ppermute | solution.py:169
  45.8 31.5 %collective-permute-start.8 = (f32[32,3072]{1,0:T(8,128)S(1)}, f32[32,3072]{1,0:T(8,128)}, u32[]{:S(2)}, u32[]{:S(2)}) collective-permute-start(f32[32,3072]{1,0:T(8,128)S(1)} %copy-done.19), channel_id=1, source_target_pairs={{0,24},{4,28},{8,16},{12,20},{16,8},{20,12},{24,0},{28,4},{1,25},{... | collective-permute-start | bytes 1179656 | tf_op jit(solution)/shard_map/ppermute | solution.py:169
  54.4 24.3 %collective-permute-start.9 = (f32[32,3072]{1,0:T(8,128)S(1)}, f32[32,3072]{1,0:T(8,128)}, u32[]{:S(2)}, u32[]{:S(2)}) collective-permute-start(f32[32,3072]{1,0:T(8,128)S(1)} %copy-done.18), channel_id=1, source_target_pairs={{0,28},{4,24},{8,20},{12,16},{16,12},{20,8},{24,4},{28,0},{1,29},{... | collective-permute-start | bytes 1179656 | tf_op jit(solution)/shard_map/ppermute | solution.py:169
  78.7 4.6 %copy-start.10 = (s32[256,28]{0,1:T(8,128)S(1)}, s32[256,28]{0,1:T(8,128)}, u32[]{:S(2)}) copy-start(s32[256,28]{0,1:T(8,128)} %param.30) | copy-start | bytes 86020
  78.7 42.4 %all-to-all-start = ((f32[8,32,3072]{2,1,0:T(8,128)}), f32[8,32,3072]{2,1,0:T(8,128)}, u32[]{:S(2)}, u32[]{:S(2)}) async-start(f32[8,32,3072]{2,1,0:T(8,128)} %bitcast.38), calls=%async_computation | async-start | bytes 6291456 | tf_op jit(solution)/shard_map/all_to_all | solution.py:477
  121.0 4.5 %copy-start.25 = (f32[256]{0:T(256)S(1)}, f32[256]{0:T(256)}, u32[]{:S(2)}) copy-start(f32[256]{0:T(256)} %constant.121.clone) | copy-start | bytes 3076
  121.0 32.6 %all-to-all-start.1 = ((f32[8,32,2048]{2,1,0:T(8,128)}), f32[8,32,2048]{2,1,0:T(8,128)}, u32[]{:S(2)}, u32[]{:S(2)}) async-start(f32[8,32,2048]{2,1,0:T(8,128)} %bitcast.39), calls=%async_computation.1 | async-start | bytes 4194304 | tf_op jit(solution)/shard_map/all_to_all | solution.py:477
  153.7 19.5 %all-to-all-start.2 = ((f32[8,32,1024]{2,1,0:T(8,128)}), f32[8,32,1024]{2,1,0:T(8,128)S(1)}, u32[]{:S(2)}, u32[]{:S(2)}) async-start(f32[8,32,1024]{2,1,0:T(8,128)} %bitcast.40), calls=%async_computation.2 | async-start | bytes 2097152 | tf_op jit(solution)/shard_map/all_to_all | solution.py:477
  182.9 12.8 %slice-start = ((s8[6815744]{0:T(1024)(128)(4,1)}), s8[4194304]{0:T(1024)(128)(4,1)S(1)}, s32[]{:S(2)}) async-start(s8[6815744]{0:T(1024)(128)(4,1)} %bitcast.29), calls=%async_computation.3 | async-start | bytes 8388608
  184.1 11.5 %slice-start.1 = ((s8[6815744]{0:T(1024)(128)(4,1)}), s8[2621440]{0:T(1024)(128)(4,1)S(1)}, s32[]{:S(2)}) async-start(s8[6815744]{0:T(1024)(128)(4,1)} %bitcast.29), calls=%async_computation.4 | async-start | bytes 5242880
  184.1 11.5 %copy-start.1 = (s32[10]{0:T(128)S(1)}, s32[10]{0:T(128)}, u32[]{:S(2)}) copy-start(s32[10]{0:T(128)} %constant.128.clone.at_ref) | copy-start | bytes 124
  190.8 11.2 %collective-permute-start.14 = (f32[96,384]{1,0:T(8,128)S(1)}, f32[96,384]{1,0:T(8,128)S(1)}, u32[]{:S(2)}, u32[]{:S(2)}) collective-permute-start(f32[96,384]{1,0:T(8,128)S(1)} %slice.96), channel_id=1, source_target_pairs={{0,1},{1,2},{2,3},{4,5},{5,6},{6,7},{8,9},{9,10},{10,11},{12,13},{... | collective-permute-start | bytes 442376 | tf_op jit(solution)/shard_map/ppermute | solution.py:546
  194.3 7.8 %collective-permute-start.15 = (f32[96,256]{1,0:T(8,128)S(1)}, f32[96,256]{1,0:T(8,128)S(1)}, u32[]{:S(2)}, u32[]{:S(2)}) collective-permute-start(f32[96,256]{1,0:T(8,128)S(1)} %slice.101), channel_id=1, source_target_pairs={{1,0},{2,1},{3,2},{5,4},{6,5},{7,6},{9,8},{10,9},{11,10},{13,12},{... | collective-permute-start | bytes 294920 | tf_op jit(solution)/shard_map/ppermute | solution.py:547
  (15 other events, 28.1 us)

commit v4 on v3

--- a/solution.py
+++ b/solution.py
@@ -370,7 +370,7 @@
         ),
         scratch_shapes=[pltpu.VMEM((NP, modes, LANES), jnp.float32)],
         input_output_aliases={5: 0} if aliased else {},
-        compiler_params=pltpu.CompilerParams(vmem_limit_bytes=VMEM_LIMIT),
+        compiler_params=pltpu.CompilerParams(vmem_limit_bytes=50 << 20),
         cost_estimate=pl.CostEstimate(
             flops=2 * count * tiles * modes * NP * NP * LANES, transcendentals=0,
             bytes_accessed=4 * 4 * count * tiles * modes * NP * LANES,
@@ -415,11 +415,38 @@
     )(*args)
 
 
-def coupling_kernel(pair, cols_ref, at_ref, x_ref, b_ref, *refs):
+def split_blocks_kernel(b_ref, o_ref):
+    for q in range(b_ref.shape[0]):
+        for s in range(b_ref.shape[1]):
+            rows = slice(s * LANES, (s + 1) * LANES)
+            high, low = split(b_ref[q, s].T)
+            o_ref[q, rows, :LANES] = high
+            o_ref[q, rows, LANES:] = low
+
+
+def split_blocks(blocks):
+    count, slots, size, _ = blocks.shape
+    pair = 2
+    return pl.pallas_call(
+        split_blocks_kernel,
+        out_shape=jax.ShapeDtypeStruct((count, slots * size, 2 * size), jnp.bfloat16),
+        grid=(count // pair,),
+        in_specs=[pl.BlockSpec((pair, slots, size, size), lambda n: (n, 0, 0, 0))],
+        out_specs=pl.BlockSpec((pair, slots * size, 2 * size), lambda n: (n, 0, 0)),
+        compiler_params=pltpu.CompilerParams(vmem_limit_bytes=32 << 20),
+        cost_estimate=pl.CostEstimate(
+            flops=0, transcendentals=0, bytes_accessed=8 * count * slots * size * size
+        ),
+        name="split_blocks",
+    )(blocks)
+
+
+def coupling_kernel(cols_ref, at_ref, x_ref, w_ref, *refs):
     o_ref, both_ref = refs[-2:]
     step = pl.program_id(0)
     rows = x_ref.shape[0]
-    slots = b_ref.shape[1]
+    group = w_ref.shape[0]
+    slots = w_ref.shape[1] // LANES
 
     @pl.when(step == 0)
     def _():
@@ -427,45 +454,40 @@
         both_ref[:rows] = high
         both_ref[rows:] = low
 
-    for q in range(pair):
-        r = at_ref[step] * pair + q
-        total = jnp.zeros((rows, LANES), jnp.float32)
-        for s in range(0, slots, 2):
-            picks = [pl.ds(pl.multiple_of(cols_ref[r, s + h] * LANES, LANES), LANES) for h in range(2)]
-            values = jnp.concatenate([both_ref[:, at] for at in picks], axis=1)
-            bh, bl = split(jnp.concatenate([b_ref[q, s + h] for h in range(2)], axis=1))
-            first = dot_nt(values, bh)
-            total = total + first[:rows] + first[rows:] + dot_nt(values[:rows], bl)
-        o_ref[:, q * LANES : (q + 1) * LANES] = total
-
-
-def coupling(extended, local_cols, blocks, order, previous):
+    for q in range(group):
+        r = at_ref[step] * group + q
+        picks = [pl.ds(pl.multiple_of(cols_ref[r, s] * LANES, LANES), LANES) for s in range(slots)]
+        total = dot(jnp.concatenate([both_ref[:, at] for at in picks], axis=1), w_ref[q])
+        total = total[:rows] + total[rows:]
+        o_ref[:, q * LANES : (q + 1) * LANES] = total[:, :LANES] + total[:, LANES:]
+
+
+def coupling(extended, local_cols, weights, order, group, previous):
     rows = extended.shape[0]
-    count, slots, size, _ = blocks.shape
-    pair = 2
+    count, depth, both = weights.shape
     in_specs = [
         pl.BlockSpec(extended.shape, lambda n, c, at: (0, 0)),
-        pl.BlockSpec((pair, slots, size, size), lambda n, c, at: (at[n], 0, 0, 0)),
+        pl.BlockSpec((group, depth, both), lambda n, c, at: (at[n], 0, 0)),
     ]
-    args = [extended, blocks]
+    args = [extended, weights]
     if previous is not None:
         in_specs.append(pl.BlockSpec(memory_space=pl.ANY))
         args.append(previous)
     return pl.pallas_call(
-        functools.partial(coupling_kernel, pair),
-        out_shape=jax.ShapeDtypeStruct((rows, count * size), jnp.float32),
+        coupling_kernel,
+        out_shape=jax.ShapeDtypeStruct((rows, count * LANES), jnp.float32),
         grid_spec=pltpu.PrefetchScalarGridSpec(
             num_scalar_prefetch=2,
             grid=(len(order),),
             in_specs=in_specs,
-            out_specs=pl.BlockSpec((rows, pair * size), lambda n, c, at: (0, at[n])),
+            out_specs=pl.BlockSpec((rows, group * LANES), lambda n, c, at: (0, at[n])),
             scratch_shapes=[pltpu.VMEM((2 * rows, extended.shape[1]), jnp.bfloat16)],
         ),
         input_output_aliases={4: 0} if previous is not None else {},
         compiler_params=pltpu.CompilerParams(vmem_limit_bytes=32 << 20),
         cost_estimate=pl.CostEstimate(
-            flops=6 * rows * slots * size * size * pair * len(order), transcendentals=0,
-            bytes_accessed=4 * slots * size * size * pair * len(order),
+            flops=4 * rows * depth * both * group * len(order), transcendentals=0,
+            bytes_accessed=2 * depth * both * group * len(order),
         ),
         name="coupling",
     )(local_cols, jnp.asarray(order, jnp.int32), *args)
@@ -521,6 +543,10 @@
         if chunk + 1 < chunks:
             both = (projected[chunk][0], arrived[chunk + 1])
             projected[chunk][0], arrived[chunk + 1] = lax.optimization_barrier(both)
+        else:
+            weights, projected[chunk] = lax.optimization_barrier((schur_blocks, projected[chunk]))
+            early = (projected[chunk][0], split_blocks(weights))
+            projected[chunk][0], weights = lax.optimization_barrier(early)
         order = [swapped(projected[chunk][0], order)]
         projected[chunk][0] = order[0]
 
@@ -551,9 +577,12 @@
         [from_below[:, :reach], start, sums[:, block_size:owned_count], after, from_above[:, block_size:]], axis=1
     )
     local_cols = block_cols - slab * block_rows
-    pairs = block_rows // 2
-    boundary_out = coupling(sums, local_cols, schur_blocks, range(2, pairs - 1), None)
-    boundary_out = coupling(extended, local_cols + HB, schur_blocks, (0, 1, pairs - 1), boundary_out)
+    inner = range(2 * HB, block_rows - HB)
+    group = max(n for n in (4, 2) if len(inner) % n == 0 and inner.start % n == 0)
+    inner = range(inner.start // group, inner.stop // group)
+    outer = (*range(HB), block_rows // HB - 1)
+    boundary_out = coupling(sums, local_cols, weights, inner, group, None)
+    boundary_out = coupling(extended, local_cols + HB, weights, outer, HB, boundary_out)
     return (out.reshape(velocity.shape), boundary_out.reshape(3, modes, owned_count))
 
 

time: 206 us -> 202 us (0.981)
  waiting for transfers between devices: 40.6 us -> 32.1 us
  local copies, waits for them, and re-layouts: 8.86 us -> 14.4 us
    all_to_all x3, waiting for transfers between devices: 16.3 us -> 6.66 us  [swapped(): lax.all_to_all(value, 'fourier', split_axis=0, concat_axis=0, tiled=True)]
    unnamed x63 -> x67, local copies, waits for them, and re-layouts: 3.27 us -> 9.36 us
    pallas_call x2 -> x3, Pallas kernels: 9.34 us -> 9.86 us  [the longest x2 7.08 us: coupling(): pl.pallas_call(coupling_kernel, out_shape=jax.ShapeDtypeStruct((rows, cou...]
  transfers between devices with their start and end apart: 19 -> 19, of which waited for: 8 -> 8; matrix products, arithmetic and copies ran while one was open for 4% -> 3% of each run, Pallas kernels for 47% -> 48%
where the time goes in v4:
time: 202 us
  Pallas kernels  119 us (59%)
  starting transfers between devices  32.7 us (16%)
  waiting for transfers between devices  32.1 us (16%)
  local copies, waits for them, and re-layouts  14.4 us (7%)
    pallas_call x2, Pallas kernels, physics(): pl.pallas_call(functools.partial(physics_kernel, planes, even, odd, group...  44.5 us
    pallas_call x3, Pallas kernels, element_stage(): pl.pallas_call(functools.partial(element_kernel, modes, aliased), out_sha...  41.4 us
    ppermute x14, waiting for transfers between devices, permuted(): lax.ppermute(piece, 'fourier', [(i, i ^ s) for i in range(groups)])  24.3 us
    ppermute x14, starting transfers between devices, permuted(): lax.ppermute(piece, 'fourier', [(i, i ^ s) for i in range(groups)])  15.6 us
    pallas_call x2, Pallas kernels, assemble(): pl.pallas_call(functools.partial(assemble_kernel, len(values), block), ou...  12.9 us
    all_to_all x3, starting transfers between devices, swapped(): lax.all_to_all(value, 'fourier', split_axis=0, concat_axis=0, tiled=True)  12.3 us
    pallas_call x2, Pallas kernels, pack(): pl.pallas_call(functools.partial(pack_kernel, modes, tiles), out_shape=[j...  10.5 us
    unnamed x67, local copies, waits for them, and re-layouts  9.36 us
  transfers between devices with their start and end apart: 19, of which 8 were waited for; matrix products, arithmetic and copies ran while one was open for 3% of the time, Pallas kernels for 48%

profile of v4, /device:TPU:0, one launch (start us, length us, event | category | flops | bytes accessed | tf_op | source)
XLA Modules:
  0.0 201.5 jit_solution(4539402861186707995)
XLA Ops:
  0.7 5.1 %pack.2 = (f32[32,3072]{1,0:T(8,128)}, f32[32,3072]{1,0:T(8,128)}, f32[32,3072]{1,0:T(8,128)}, f32[32,3072]{1,0:T(8,128)}, f32[32,3072]{1,0:T(8,128)}, /*index=5...) custom-call(s32[1]{0:T(128)} %bitcast.1.me_ref, f32[96,64,256]{2,1,0:T(8,128)} %bitcast.34), custom_call_target="tpu_custom_call" | custom-call | bytes 6291456 | tf_op jit(solution)/shard_map/pack/pallas_call | solution.py:151
  6.3 3.5 %collective-permute-start.2 = (f32[32,3072]{1,0:T(8,128)}, f32[32,3072]{1,0:T(8,128)S(1)}, u32[]{:S(2)}, u32[]{:S(2)}) collective-permute-start(f32[32,3072]{1,0:T(8,128)} %get-tuple-element.59), channel_id=1, source_target_pairs={{0,24},{4,28},{8,16},{12,20},{16,8},{20,12},{24,0},{28,4},{1,25},{... | collective-permute-start | bytes 1179656 | tf_op jit(solution)/shard_map/ppermute | solution.py:169
  9.9 1.7 collective-permute-start.4
  11.6 1.5 collective-permute-start.5
  13.3 5.3 %pack.3 = (f32[32,3072]{1,0:T(8,128)}, f32[32,3072]{1,0:T(8,128)}, f32[32,3072]{1,0:T(8,128)}, f32[32,3072]{1,0:T(8,128)}, f32[32,3072]{1,0:T(8,128)}, /*index=5...) custom-call(s32[1]{0:T(128)} %bitcast.1.me_ref, f32[96,64,256]{2,1,0:T(8,128)} %bitcast.35), custom_call_target="tpu_custom_call" | custom-call | bytes 6291456 | tf_op jit(solution)/shard_map/pack/pallas_call | solution.py:151
  20.8 7.3 %collective-permute-done.3.refs_3_ = f32[32,3072]{1,0:T(8,128)S(1)} collective-permute-done((f32[32,3072]{1,0:T(8,128)}, f32[32,3072]{1,0:T(8,128)S(1)}, u32[]{:S(2)}, u32[]{:S(2)}) %collective-permute-start.3) | collective-permute-done | bytes 393248 | tf_op jit(solution)/shard_map/ppermute | solution.py:169
  28.1 1.8 collective-permute-start.7
  29.9 1.5 collective-permute-start.10
  31.6 1.7 reshape.125.wh_ref
  33.3 1.7 reshape.126.wl_ref
  35.9 1.6 collective-permute-done.4.refs_4_
  38.1 6.9 %collective-permute-done.6.refs_6_ = f32[32,3072]{1,0:T(8,128)} collective-permute-done((f32[32,3072]{1,0:T(8,128)}, f32[32,3072]{1,0:T(8,128)}, u32[]{:S(2)}, u32[]{:S(2)}) %collective-permute-start.6) | collective-permute-done | bytes 393248 | tf_op jit(solution)/shard_map/ppermute | solution.py:169
  45.7 2.7 %collective-permute-start.8 = (f32[32,3072]{1,0:T(8,128)S(1)}, f32[32,3072]{1,0:T(8,128)}, u32[]{:S(2)}, u32[]{:S(2)}) collective-permute-start(f32[32,3072]{1,0:T(8,128)S(1)} %copy-done.21), channel_id=1, source_target_pairs={{0,24},{4,28},{8,16},{12,20},{16,8},{20,12},{24,0},{28,4},{1,25},{... | collective-permute-start | bytes 1179656 | tf_op jit(solution)/shard_map/ppermute | solution.py:169
  48.5 5.8 %collective-permute-done.10.refs_4_ = f32[32,3072]{1,0:T(8,128)} collective-permute-done((f32[32,3072]{1,0:T(8,128)}, f32[32,3072]{1,0:T(8,128)}, u32[]{:S(2)}, u32[]{:S(2)}) %collective-permute-start.10) | collective-permute-done | bytes 393248 | tf_op jit(solution)/shard_map/ppermute | solution.py:169
  54.6 22.6 %physics.2 = f32[256,3072]{1,0:T(8,128)} custom-call(s32[1]{0:T(128)} %bitcast.1.me_ref, bf16[768,256]{1,0:T(8,128)(2,1)} %constant.122.clone.fh_ref, bf16[768,256]{1,0:T(8,128)(2,1)} %constant.123.clone.fl_ref, bf16[256,256]{1,0:T(8,128)(2,1)} %reshape.125.wh_ref, bf16[256,256]{1,0:T(8,128)(2,1)} %reshape.126.wl_ref, ...), custom_call_target="tpu_custom_call" | custom-call | flops 7247757312 | bytes 6291456 | tf_op jit(solution)/shard_map/physics/pallas_call | solution.py:275
  77.3 1.4 collective-permute-done.9.refs_3_
  78.7 4.5 %all-to-all-start = ((f32[8,32,3072]{2,1,0:T(8,128)}), f32[8,32,3072]{2,1,0:T(8,128)}, u32[]{:S(2)}, u32[]{:S(2)}) async-start(f32[8,32,3072]{2,1,0:T(8,128)} %bitcast.41), calls=%async_computation | async-start | bytes 6291456 | tf_op jit(solution)/shard_map/all_to_all | solution.py:499
  84.0 21.9 %physics.3 = (f32[256,2048]{1,0:T(8,128)}, f32[256,1024]{1,0:T(8,128)}) custom-call(s32[1]{0:T(128)} %bitcast.1.me_ref, bf16[768,256]{1,0:T(8,128)(2,1)} %constant.122.clone.fh_ref, bf16[768,256]{1,0:T(8,128)(2,1)} %constant.123.clone.fl_ref, bf16[256,256]{1,0:T(8,128)(2,1)} %reshape.125.wh_ref, bf16[256,256]{1,0:T(8,128)(2,1)} %reshape.126.wl_ref, ...), custom_call_target="tpu_custom_call" | custom-call | flops 7247757312 | bytes 6291456 | tf_op jit(solution)/shard_map/physics/pallas_call | solution.py:275
  105.9 2.9 %copy-done.1 = f32[26,4,128,128]{3,2,1,0:T(8,128)S(1)} copy-done((f32[26,4,128,128]{3,2,1,0:T(8,128)S(1)}, f32[26,4,128,128]{3,2,1,0:T(8,128)}, u32[]{:S(2)}) %copy-start.1) | copy-done | bytes 6815768
  108.8 2.8 %split_blocks.1.w_ref = bf16[26,512,256]{2,1,0:T(8,128)(2,1)S(1)} custom-call(f32[26,4,128,128]{3,2,1,0:T(8,128)S(1)} %copy-done.1), custom_call_target="tpu_custom_call" | custom-call | bytes 13631488 | tf_op jit(solution)/shard_map/split_blocks/pallas_call | solution.py:430
  111.6 2.8 %copy-done = bf16[26,512,256]{2,1,0:T(8,128)(2,1)} copy-done((bf16[26,512,256]{2,1,0:T(8,128)(2,1)}, bf16[26,512,256]{2,1,0:T(8,128)(2,1)S(1)}, u32[]{:S(2)}) %copy-start) | copy-done | bytes 6815768
  114.4 6.6 %all-to-all-done.r_ref = f32[8,32,3072]{2,1,0:T(8,128)} async-done(((f32[8,32,3072]{2,1,0:T(8,128)}), f32[8,32,3072]{2,1,0:T(8,128)}, u32[]{:S(2)}, u32[]{:S(2)}) %all-to-all-start) | async-done | bytes 3145760 | tf_op jit(solution)/shard_map/all_to_all | solution.py:499
  121.0 3.6 %all-to-all-start.1 = ((f32[8,32,2048]{2,1,0:T(8,128)}), f32[8,32,2048]{2,1,0:T(8,128)S(1)}, u32[]{:S(2)}, u32[]{:S(2)}) async-start(f32[8,32,2048]{2,1,0:T(8,128)} %bitcast.42), calls=%async_computation.1 | async-start | bytes 4194304 | tf_op jit(solution)/shard_map/all_to_all | solution.py:499
  125.0 19.4 %element.3 = (f32[96,64,256]{2,1,0:T(8,128)}, bf16[96,3584]{1,0:T(8,128)(2,1)S(1)}, bf16[96,3584]{1,0:T(8,128)(2,1)S(1)}) custom-call(f32[96,64,256]{2,1,0:T(8,128)} %bitcast.36, f32[8,32,3072]{2,1,0:T(8,128)} %all-to-all-done.r_ref, f32[64,64,256]{2,1,0:T(8,128)} %a_ref.5, f32[8,8,256]{2,1,0:T(8,128)S(1)} %bitcast.31, f32[32,128]{1,0:T(8,128)S(1)} %broadcast_in_dim.13.helm_ref), custom_call_target="tpu_custom_call" | custom-call | flops 100663296 | bytes 12582912 | tf_op jit(solution)/shard_map/element/pallas_call | solution.py:361
  144.9 6.3 %assemble.2.refs_5_ = f32[96,3584]{1,0:T(8,128)S(1)} custom-call(bf16[96,3584]{1,0:T(8,128)(2,1)S(1)} %get-tuple-element.85.refs_0_, bf16[96,3584]{1,0:T(8,128)(2,1)S(1)} %get-tuple-element.86.refs_1_, s32[3584,128]{1,0:T(8,128)S(1)} %broadcast_in_dim.30.refs_2_), custom_call_target="tpu_custom_call" | custom-call | flops 4932501504 | bytes 4587520 | tf_op jit(solution)/shard_map/assemble/pallas_call | solution.py:404
  152.4 4.3 %all-to-all-start.2 = ((f32[8,32,1024]{2,1,0:T(8,128)}), f32[8,32,1024]{2,1,0:T(8,128)S(1)}, u32[]{:S(2)}, u32[]{:S(2)}) async-start(f32[8,32,1024]{2,1,0:T(8,128)} %bitcast.43), calls=%async_computation.2 | async-start | bytes 2097152 | tf_op jit(solution)/shard_map/all_to_all | solution.py:499
  156.8 13.7 %element.4 = (f32[96,64,256]{2,1,0:T(8,128)}, bf16[64,3584]{1,0:T(8,128)(2,1)S(1)}, bf16[64,3584]{1,0:T(8,128)(2,1)S(1)}) custom-call(f32[96,64,256]{2,1,0:T(8,128)} %bitcast.37, f32[8,32,2048]{2,1,0:T(8,128)S(1)} %all-to-all-done.1.r_ref, f32[64,64,256]{2,1,0:T(8,128)} %a_ref.5, f32[8,8,256]{2,1,0:T(8,128)S(1)} %bitcast.32, ...), custom_call_target="tpu_custom_call", output_to_operand_aliasing={{0}: (5, {})} | custom-call | flops 67108864 | bytes 8388608 | tf_op jit(solution)/shard_map/element/pallas_call | solution.py:361
  172.1 8.3 %element.5 = (f32[96,64,256]{2,1,0:T(8,128)}, bf16[32,3584]{1,0:T(8,128)(2,1)S(1)}, bf16[32,3584]{1,0:T(8,128)(2,1)S(1)}) custom-call(f32[96,64,256]{2,1,0:T(8,128)} %bitcast.38, f32[8,32,1024]{2,1,0:T(8,128)S(1)} %all-to-all-done.2.r_ref, f32[64,64,256]{2,1,0:T(8,128)} %a_ref.5, f32[8,8,256]{2,1,0:T(8,128)S(1)} %bitcast.33, ...), custom_call_target="tpu_custom_call", output_to_operand_aliasing={{0}: (5, {})} | custom-call | flops 33554432 | bytes 4194304 | tf_op jit(solution)/shard_map/element/pallas_call | solution.py:361
  181.6 6.6 %assemble.3.x_ref = f32[96,3584]{1,0:T(8,128)S(1)} custom-call(bf16[64,3584]{1,0:T(8,128)(2,1)S(1)} %copy-done.6, bf16[32,3584]{1,0:T(8,128)(2,1)S(1)} %get-tuple-element.97.refs_1_, bf16[64,3584]{1,0:T(8,128)(2,1)S(1)} %copy-done.8, bf16[32,3584]{1,0:T(8,128)(2,1)S(1)} %get-tuple-element.99.refs_3_, s32[3584,128]{1,0:T(8,128)S(1)} %broadcast_in_dim.32.refs_4_, ...), custom_call_target="tpu_custom_call" | custom-call | flops 4932501504 | bytes 4587520 | tf_op jit(solution)/shard_map/assemble/pallas_call | solution.py:404
  188.3 3.5 %collective-permute-start.14 = (f32[96,384]{1,0:T(8,128)S(1)}, f32[96,384]{1,0:T(8,128)S(1)}, u32[]{:S(2)}, u32[]{:S(2)}) collective-permute-start(f32[96,384]{1,0:T(8,128)S(1)} %slice.96), channel_id=1, source_target_pairs={{0,1},{1,2},{2,3},{4,5},{5,6},{6,7},{8,9},{9,10},{10,11},{12,13},{... | collective-permute-start | bytes 442376 | tf_op jit(solution)/shard_map/ppermute | solution.py:572
  193.1 4.2 %coupling.2.refs_0_ = f32[96,3328]{1,0:T(8,128)} custom-call(s32[26,4]{1,0:T(8,128)S(1)} %get-tuple-element.105.cols_ref, s32[5]{0:T(128)S(1)} %copy-done.4, f32[96,3584]{1,0:T(8,128)S(1)} %assemble.3.x_ref, bf16[26,512,256]{2,1,0:T(8,128)(2,1)S(1)} %bitcast.30), custom_call_target="tpu_custom_call" | custom-call | flops 1006632960 | bytes 5242880 | tf_op jit(solution)/shard_map/coupling/pallas_call | solution.py:476
  198.6 2.9 %coupling.3 = f32[96,3328]{1,0:T(8,128)} custom-call(s32[26,4]{1,0:T(8,128)S(1)} %get-tuple-element.104.cols_ref, s32[3]{0:T(128)S(1)} %copy-done.3, f32[96,3840]{1,0:T(8,128)S(1)} %slice_dynamic-update-slice_fusion.2.x_ref, bf16[26,512,256]{2,1,0:T(8,128)(2,1)S(1)} %bitcast.30, f32[96,3328]{1,0:T(8,128)} %coupling.2.refs_0_), custom_call_target="tpu_custom_call", output_to_operand_aliasing={{}: (4, {})} | custom-call | flops 301989888 | bytes 1572864 | tf_op jit(solution)/shard_map/coupling/pallas_call | solution.py:476
  (121 shorter events, 13.9 us)
Async XLA Ops:
  0.6 12.5 %copy-start.15 = (bf16[16,8]{1,0:T(8,128)(2,1)S(1)}, bf16[16,8]{1,0:T(8,128)(2,1)}, u32[]{:S(2)}) copy-start(bf16[16,8]{1,0:T(8,128)(2,1)} %constant.134) | copy-start | bytes 772
  0.6 12.6 %copy-start.14 = (bf16[16,8]{1,0:T(8,128)(2,1)S(1)}, bf16[16,8]{1,0:T(8,128)(2,1)}, u32[]{:S(2)}) copy-start(bf16[16,8]{1,0:T(8,128)(2,1)} %constant.135) | copy-start | bytes 772
  5.8 7.5 %collective-permute-start = (f32[32,3072]{1,0:T(8,128)}, f32[32,3072]{1,0:T(8,128)S(1)}, u32[]{:S(2)}, u32[]{:S(2)}) collective-permute-start(f32[32,3072]{1,0:T(8,128)} %get-tuple-element.54), channel_id=1, source_target_pairs={{0,4},{4,0},{8,12},{12,8},{16,20},{20,16},{24,28},{28,24},{1,5},{5... | collective-permute-start | bytes 1179656 | tf_op jit(solution)/shard_map/ppermute | solution.py:169
  6.3 13.8 %collective-permute-start.2 = (f32[32,3072]{1,0:T(8,128)}, f32[32,3072]{1,0:T(8,128)S(1)}, u32[]{:S(2)}, u32[]{:S(2)}) collective-permute-start(f32[32,3072]{1,0:T(8,128)} %get-tuple-element.59), channel_id=1, source_target_pairs={{0,24},{4,28},{8,16},{12,20},{16,8},{20,12},{24,0},{28,4},{1,25},{... | collective-permute-start | bytes 1179656 | tf_op jit(solution)/shard_map/ppermute | solution.py:169
  9.8 18.2 %collective-permute-start.3 = (f32[32,3072]{1,0:T(8,128)}, f32[32,3072]{1,0:T(8,128)S(1)}, u32[]{:S(2)}, u32[]{:S(2)}) collective-permute-start(f32[32,3072]{1,0:T(8,128)} %get-tuple-element.60), channel_id=1, source_target_pairs={{0,28},{4,24},{8,20},{12,16},{16,12},{20,8},{24,4},{28,0},{1,29},{... | collective-permute-start | bytes 1179656 | tf_op jit(solution)/shard_map/ppermute | solution.py:169
  9.9 27.6 %collective-permute-start.4 = (f32[32,3072]{1,0:T(8,128)}, f32[32,3072]{1,0:T(8,128)}, u32[]{:S(2)}, u32[]{:S(2)}) collective-permute-start(f32[32,3072]{1,0:T(8,128)} %get-tuple-element.61), channel_id=1, source_target_pairs={{0,8},{4,12},{8,0},{12,4},{16,24},{20,28},{24,16},{28,20},{1,9},{5... | collective-permute-start | bytes 1179656 | tf_op jit(solution)/shard_map/ppermute | solution.py:169
  11.6 26.0 %collective-permute-start.5 = (f32[32,3072]{1,0:T(8,128)}, f32[32,3072]{1,0:T(8,128)}, u32[]{:S(2)}, u32[]{:S(2)}) collective-permute-start(f32[32,3072]{1,0:T(8,128)} %get-tuple-element.62), channel_id=1, source_target_pairs={{0,16},{4,20},{8,24},{12,28},{16,0},{20,4},{24,8},{28,12},{1,17},{... | collective-permute-start | bytes 1179656 | tf_op jit(solution)/shard_map/ppermute | solution.py:169
  13.3 5.3 %copy-start.16 = (f32[32,3072]{1,0:T(8,128)}, f32[32,3072]{1,0:T(8,128)S(1)}, u32[]{:S(2)}) copy-start(f32[32,3072]{1,0:T(8,128)S(1)} %collective-permute-done.refs_1_) | copy-start | bytes 1179652
  18.6 11.2 %collective-permute-start.1 = (f32[32,3072]{1,0:T(8,128)}, f32[32,3072]{1,0:T(8,128)S(1)}, u32[]{:S(2)}, u32[]{:S(2)}) collective-permute-start(f32[32,3072]{1,0:T(8,128)} %get-tuple-element.56), channel_id=1, source_target_pairs={{0,4},{4,0},{8,12},{12,8},{16,20},{20,16},{24,28},{28,24},{1,5},{5... | collective-permute-start | bytes 1179656 | tf_op jit(solution)/shard_map/ppermute | solution.py:169
  20.1 13.1 %copy-start.17 = (f32[32,3072]{1,0:T(8,128)}, f32[32,3072]{1,0:T(8,128)S(1)}, u32[]{:S(2)}) copy-start(f32[32,3072]{1,0:T(8,128)S(1)} %collective-permute-done.2.refs_2_) | copy-start | bytes 1179652
  20.1 24.9 %collective-permute-start.6 = (f32[32,3072]{1,0:T(8,128)}, f32[32,3072]{1,0:T(8,128)}, u32[]{:S(2)}, u32[]{:S(2)}) collective-permute-start(f32[32,3072]{1,0:T(8,128)} %get-tuple-element.63), channel_id=1, source_target_pairs={{0,12},{4,8},{8,4},{12,0},{16,28},{20,24},{24,20},{28,16},{1,13},{... | collective-permute-start | bytes 1179656 | tf_op jit(solution)/shard_map/ppermute | solution.py:169
  28.1 17.7 %collective-permute-start.7 = (f32[32,3072]{1,0:T(8,128)}, f32[32,3072]{1,0:T(8,128)}, u32[]{:S(2)}, u32[]{:S(2)}) collective-permute-start(f32[32,3072]{1,0:T(8,128)} %get-tuple-element.64), channel_id=1, source_target_pairs={{0,20},{4,16},{8,28},{12,24},{16,4},{20,0},{24,12},{28,8},{1,21},{... | collective-permute-start | bytes 1179656 | tf_op jit(solution)/shard_map/ppermute | solution.py:169
  29.9 24.5 %collective-permute-start.10 = (f32[32,3072]{1,0:T(8,128)}, f32[32,3072]{1,0:T(8,128)}, u32[]{:S(2)}, u32[]{:S(2)}) collective-permute-start(f32[32,3072]{1,0:T(8,128)} %get-tuple-element.69), channel_id=1, source_target_pairs={{0,8},{4,12},{8,0},{12,4},{16,24},{20,28},{24,16},{28,20},{1,9},{5... | collective-permute-start | bytes 1179656 | tf_op jit(solution)/shard_map/ppermute | solution.py:169
  33.2 12.5 %copy-start.21 = (f32[32,3072]{1,0:T(8,128)S(1)}, f32[32,3072]{1,0:T(8,128)}, u32[]{:S(2)}) copy-start(f32[32,3072]{1,0:T(8,128)} %get-tuple-element.67) | copy-start | bytes 1179652
  33.2 21.1 %copy-start.20 = (f32[32,3072]{1,0:T(8,128)S(1)}, f32[32,3072]{1,0:T(8,128)}, u32[]{:S(2)}) copy-start(f32[32,3072]{1,0:T(8,128)} %get-tuple-element.68) | copy-start | bytes 1179652
  33.3 11.8 %copy-start.22 = (f32[32,3072]{1,0:T(8,128)S(1)}, f32[32,3072]{1,0:T(8,128)}, u32[]{:S(2)}) copy-start(f32[32,3072]{1,0:T(8,128)} %get-tuple-element.72) | copy-start | bytes 1179652
  37.5 39.7 %collective-permute-start.11 = (f32[32,3072]{1,0:T(8,128)}, f32[32,3072]{1,0:T(8,128)S(1)}, u32[]{:S(2)}, u32[]{:S(2)}) collective-permute-start(f32[32,3072]{1,0:T(8,128)} %get-tuple-element.70), channel_id=1, source_target_pairs={{0,16},{4,20},{8,24},{12,28},{16,0},{20,4},{24,8},{28,12},{1,17},{... | collective-permute-start | bytes 1179656 | tf_op jit(solution)/shard_map/ppermute | solution.py:169
  37.6 39.6 %collective-permute-start.12 = (f32[32,3072]{1,0:T(8,128)S(1)}, f32[32,3072]{1,0:T(8,128)S(1)}, u32[]{:S(2)}, u32[]{:S(2)}) collective-permute-start(f32[32,3072]{1,0:T(8,128)S(1)} %copy-done.23), channel_id=1, source_target_pairs={{0,12},{4,8},{8,4},{12,0},{16,28},{20,24},{24,20},{28,16},{1,13},{... | collective-permute-start | bytes 1179656 | tf_op jit(solution)/shard_map/ppermute | solution.py:169
  45.0 32.2 %collective-permute-start.13 = (f32[32,3072]{1,0:T(8,128)S(1)}, f32[32,3072]{1,0:T(8,128)S(1)}, u32[]{:S(2)}, u32[]{:S(2)}) collective-permute-start(f32[32,3072]{1,0:T(8,128)S(1)} %copy-done.22), channel_id=1, source_target_pairs={{0,20},{4,16},{8,28},{12,24},{16,4},{20,0},{24,12},{28,8},{1,21},{... | collective-permute-start | bytes 1179656 | tf_op jit(solution)/shard_map/ppermute | solution.py:169
  45.7 31.5 %collective-permute-start.8 = (f32[32,3072]{1,0:T(8,128)S(1)}, f32[32,3072]{1,0:T(8,128)}, u32[]{:S(2)}, u32[]{:S(2)}) collective-permute-start(f32[32,3072]{1,0:T(8,128)S(1)} %copy-done.21), channel_id=1, source_target_pairs={{0,24},{4,28},{8,16},{12,20},{16,8},{20,12},{24,0},{28,4},{1,25},{... | collective-permute-start | bytes 1179656 | tf_op jit(solution)/shard_map/ppermute | solution.py:169
  54.3 24.3 %collective-permute-start.9 = (f32[32,3072]{1,0:T(8,128)S(1)}, f32[32,3072]{1,0:T(8,128)}, u32[]{:S(2)}, u32[]{:S(2)}) collective-permute-start(f32[32,3072]{1,0:T(8,128)S(1)} %copy-done.20), channel_id=1, source_target_pairs={{0,28},{4,24},{8,20},{12,16},{16,12},{20,8},{24,4},{28,0},{1,29},{... | collective-permute-start | bytes 1179656 | tf_op jit(solution)/shard_map/ppermute | solution.py:169
  78.7 42.4 %all-to-all-start = ((f32[8,32,3072]{2,1,0:T(8,128)}), f32[8,32,3072]{2,1,0:T(8,128)}, u32[]{:S(2)}, u32[]{:S(2)}) async-start(f32[8,32,3072]{2,1,0:T(8,128)} %bitcast.41), calls=%async_computation | async-start | bytes 6291456 | tf_op jit(solution)/shard_map/all_to_all | solution.py:499
  114.4 10.3 %copy-start.27 = (f32[256]{0:T(256)S(1)}, f32[256]{0:T(256)}, u32[]{:S(2)}) copy-start(f32[256]{0:T(256)} %constant.121.clone) | copy-start | bytes 3076
  114.4 10.6 %copy-start.2 = (f32[64,256]{1,0:T(8,128)S(1)}, f32[64,256]{1,0:T(8,128)}, u32[]{:S(2)}) copy-start(f32[64,256]{1,0:T(8,128)} %param.28) | copy-start | bytes 196612
  121.0 31.4 %all-to-all-start.1 = ((f32[8,32,2048]{2,1,0:T(8,128)}), f32[8,32,2048]{2,1,0:T(8,128)S(1)}, u32[]{:S(2)}, u32[]{:S(2)}) async-start(f32[8,32,2048]{2,1,0:T(8,128)} %bitcast.42), calls=%async_computation.1 | async-start | bytes 4194304 | tf_op jit(solution)/shard_map/all_to_all | solution.py:499
  152.4 19.7 %all-to-all-start.2 = ((f32[8,32,1024]{2,1,0:T(8,128)}), f32[8,32,1024]{2,1,0:T(8,128)S(1)}, u32[]{:S(2)}, u32[]{:S(2)}) async-start(f32[8,32,1024]{2,1,0:T(8,128)} %bitcast.43), calls=%async_computation.2 | async-start | bytes 2097152 | tf_op jit(solution)/shard_map/all_to_all | solution.py:499
  172.1 8.9 %copy-start.10 = (f32[96,3584]{1,0:T(8,128)S(1)}, f32[96,3584]{1,0:T(8,128)}, u32[]{:S(2)}) copy-start(f32[96,3584]{1,0:T(8,128)} %copy-done.9) | copy-start | bytes 4128772
  180.5 12.6 %slice-start = ((s8[6815744]{0:T(1024)(128)(4,1)}), s8[4194304]{0:T(1024)(128)(4,1)S(1)}, s32[]{:S(2)}) async-start(s8[6815744]{0:T(1024)(128)(4,1)} %bitcast.29), calls=%async_computation.3 | async-start | bytes 8388608
  181.6 11.5 %slice-start.1 = ((s8[6815744]{0:T(1024)(128)(4,1)}), s8[2621440]{0:T(1024)(128)(4,1)S(1)}, s32[]{:S(2)}) async-start(s8[6815744]{0:T(1024)(128)(4,1)} %bitcast.29), calls=%async_computation.4 | async-start | bytes 5242880
  181.6 11.5 %copy-start.4 = (s32[5]{0:T(128)S(1)}, s32[5]{0:T(128)}, u32[]{:S(2)}) copy-start(s32[5]{0:T(128)} %constant.128.clone.at_ref) | copy-start | bytes 64
  188.3 9.1 %collective-permute-start.14 = (f32[96,384]{1,0:T(8,128)S(1)}, f32[96,384]{1,0:T(8,128)S(1)}, u32[]{:S(2)}, u32[]{:S(2)}) collective-permute-start(f32[96,384]{1,0:T(8,128)S(1)} %slice.96), channel_id=1, source_target_pairs={{0,1},{1,2},{2,3},{4,5},{5,6},{6,7},{8,9},{9,10},{10,11},{12,13},{... | collective-permute-start | bytes 442376 | tf_op jit(solution)/shard_map/ppermute | solution.py:572
  191.8 6.8 %collective-permute-start.15 = (f32[96,256]{1,0:T(8,128)S(1)}, f32[96,256]{1,0:T(8,128)S(1)}, u32[]{:S(2)}, u32[]{:S(2)}) collective-permute-start(f32[96,256]{1,0:T(8,128)S(1)} %slice.101), channel_id=1, source_target_pairs={{1,0},{2,1},{3,2},{5,4},{6,5},{7,6},{9,8},{10,9},{11,10},{13,12},{... | collective-permute-start | bytes 294920 | tf_op jit(solution)/shard_map/ppermute | solution.py:573
  (17 other events, 41.2 us)

commit v5 on v4

--- a/solution.py
+++ b/solution.py
@@ -18,7 +18,7 @@
 COLS = NP * SUB
 PERIM = 28
 VMEM_LIMIT = 61 << 20
-ASSEMBLED = 512
+ASSEMBLED = 1792
 
 
 gauss_nodes = [

time: 202 us -> 200 us (0.990)
  no operation moved by 1% of the time
where the time goes in v5:
time: 200 us
  Pallas kernels  117 us (58%)
  starting transfers between devices  32.7 us (16%)
  waiting for transfers between devices  32.1 us (16%)
  local copies, waits for them, and re-layouts  14.4 us (7%)
    pallas_call x2, Pallas kernels, physics(): pl.pallas_call(functools.partial(physics_kernel, planes, even, odd, group...  44.5 us
    pallas_call x3, Pallas kernels, element_stage(): pl.pallas_call(functools.partial(element_kernel, modes, aliased), out_sha...  41.4 us
    ppermute x14, waiting for transfers between devices, permuted(): lax.ppermute(piece, 'fourier', [(i, i ^ s) for i in range(groups)])  24.3 us
    ppermute x14, starting transfers between devices, permuted(): lax.ppermute(piece, 'fourier', [(i, i ^ s) for i in range(groups)])  15.6 us
    all_to_all x3, starting transfers between devices, swapped(): lax.all_to_all(value, 'fourier', split_axis=0, concat_axis=0, tiled=True)  12.3 us
    pallas_call x2, Pallas kernels, assemble(): pl.pallas_call(functools.partial(assemble_kernel, len(values), block), ou...  11 us
    pallas_call x2, Pallas kernels, pack(): pl.pallas_call(functools.partial(pack_kernel, modes, tiles), out_shape=[j...  10.5 us
    unnamed x67, local copies, waits for them, and re-layouts  9.36 us
  transfers between devices with their start and end apart: 19, of which 8 were waited for; matrix products, arithmetic and copies ran while one was open for 3% of the time, Pallas kernels for 48%

profile of v5, /device:TPU:0, one launch (start us, length us, event | category | flops | bytes accessed | tf_op | source)
XLA Modules:
  0.0 199.6 jit_solution(13747369115934312044)
XLA Ops:
  0.7 5.1 %pack.2 = (f32[32,3072]{1,0:T(8,128)}, f32[32,3072]{1,0:T(8,128)}, f32[32,3072]{1,0:T(8,128)}, f32[32,3072]{1,0:T(8,128)}, f32[32,3072]{1,0:T(8,128)}, /*index=5...) custom-call(s32[1]{0:T(128)} %bitcast.1.me_ref, f32[96,64,256]{2,1,0:T(8,128)} %bitcast.34), custom_call_target="tpu_custom_call" | custom-call | bytes 6291456 | tf_op jit(solution)/shard_map/pack/pallas_call | solution.py:151
  6.3 3.5 %collective-permute-start.2 = (f32[32,3072]{1,0:T(8,128)}, f32[32,3072]{1,0:T(8,128)S(1)}, u32[]{:S(2)}, u32[]{:S(2)}) collective-permute-start(f32[32,3072]{1,0:T(8,128)} %get-tuple-element.59), channel_id=1, source_target_pairs={{0,24},{4,28},{8,16},{12,20},{16,8},{20,12},{24,0},{28,4},{1,25},{... | collective-permute-start | bytes 1179656 | tf_op jit(solution)/shard_map/ppermute | solution.py:169
  9.9 1.7 collective-permute-start.4
  11.6 1.5 collective-permute-start.5
  13.3 5.3 %pack.3 = (f32[32,3072]{1,0:T(8,128)}, f32[32,3072]{1,0:T(8,128)}, f32[32,3072]{1,0:T(8,128)}, f32[32,3072]{1,0:T(8,128)}, f32[32,3072]{1,0:T(8,128)}, /*index=5...) custom-call(s32[1]{0:T(128)} %bitcast.1.me_ref, f32[96,64,256]{2,1,0:T(8,128)} %bitcast.35), custom_call_target="tpu_custom_call" | custom-call | bytes 6291456 | tf_op jit(solution)/shard_map/pack/pallas_call | solution.py:151
  20.8 7.3 %collective-permute-done.3.refs_3_ = f32[32,3072]{1,0:T(8,128)S(1)} collective-permute-done((f32[32,3072]{1,0:T(8,128)}, f32[32,3072]{1,0:T(8,128)S(1)}, u32[]{:S(2)}, u32[]{:S(2)}) %collective-permute-start.3) | collective-permute-done | bytes 393248 | tf_op jit(solution)/shard_map/ppermute | solution.py:169
  28.1 1.8 collective-permute-start.7
  29.9 1.5 collective-permute-start.10
  31.6 1.7 reshape.125.wh_ref
  33.3 1.7 reshape.126.wl_ref
  35.9 1.6 collective-permute-done.4.refs_4_
  38.1 6.9 %collective-permute-done.6.refs_6_ = f32[32,3072]{1,0:T(8,128)} collective-permute-done((f32[32,3072]{1,0:T(8,128)}, f32[32,3072]{1,0:T(8,128)}, u32[]{:S(2)}, u32[]{:S(2)}) %collective-permute-start.6) | collective-permute-done | bytes 393248 | tf_op jit(solution)/shard_map/ppermute | solution.py:169
  45.7 2.7 %collective-permute-start.8 = (f32[32,3072]{1,0:T(8,128)S(1)}, f32[32,3072]{1,0:T(8,128)}, u32[]{:S(2)}, u32[]{:S(2)}) collective-permute-start(f32[32,3072]{1,0:T(8,128)S(1)} %copy-done.21), channel_id=1, source_target_pairs={{0,24},{4,28},{8,16},{12,20},{16,8},{20,12},{24,0},{28,4},{1,25},{... | collective-permute-start | bytes 1179656 | tf_op jit(solution)/shard_map/ppermute | solution.py:169
  48.5 5.8 %collective-permute-done.10.refs_4_ = f32[32,3072]{1,0:T(8,128)} collective-permute-done((f32[32,3072]{1,0:T(8,128)}, f32[32,3072]{1,0:T(8,128)}, u32[]{:S(2)}, u32[]{:S(2)}) %collective-permute-start.10) | collective-permute-done | bytes 393248 | tf_op jit(solution)/shard_map/ppermute | solution.py:169
  54.6 22.6 %physics.2 = f32[256,3072]{1,0:T(8,128)} custom-call(s32[1]{0:T(128)} %bitcast.1.me_ref, bf16[768,256]{1,0:T(8,128)(2,1)} %constant.122.clone.fh_ref, bf16[768,256]{1,0:T(8,128)(2,1)} %constant.123.clone.fl_ref, bf16[256,256]{1,0:T(8,128)(2,1)} %reshape.125.wh_ref, bf16[256,256]{1,0:T(8,128)(2,1)} %reshape.126.wl_ref, ...), custom_call_target="tpu_custom_call" | custom-call | flops 7247757312 | bytes 6291456 | tf_op jit(solution)/shard_map/physics/pallas_call | solution.py:275
  77.3 1.4 collective-permute-done.9.refs_3_
  78.7 4.5 %all-to-all-start = ((f32[8,32,3072]{2,1,0:T(8,128)}), f32[8,32,3072]{2,1,0:T(8,128)}, u32[]{:S(2)}, u32[]{:S(2)}) async-start(f32[8,32,3072]{2,1,0:T(8,128)} %bitcast.41), calls=%async_computation | async-start | bytes 6291456 | tf_op jit(solution)/shard_map/all_to_all | solution.py:499
  84.0 21.9 %physics.3 = (f32[256,2048]{1,0:T(8,128)}, f32[256,1024]{1,0:T(8,128)}) custom-call(s32[1]{0:T(128)} %bitcast.1.me_ref, bf16[768,256]{1,0:T(8,128)(2,1)} %constant.122.clone.fh_ref, bf16[768,256]{1,0:T(8,128)(2,1)} %constant.123.clone.fl_ref, bf16[256,256]{1,0:T(8,128)(2,1)} %reshape.125.wh_ref, bf16[256,256]{1,0:T(8,128)(2,1)} %reshape.126.wl_ref, ...), custom_call_target="tpu_custom_call" | custom-call | flops 7247757312 | bytes 6291456 | tf_op jit(solution)/shard_map/physics/pallas_call | solution.py:275
  105.9 2.9 %copy-done.1 = f32[26,4,128,128]{3,2,1,0:T(8,128)S(1)} copy-done((f32[26,4,128,128]{3,2,1,0:T(8,128)S(1)}, f32[26,4,128,128]{3,2,1,0:T(8,128)}, u32[]{:S(2)}) %copy-start.1) | copy-done | bytes 6815768
  108.8 2.8 %split_blocks.1.w_ref = bf16[26,512,256]{2,1,0:T(8,128)(2,1)S(1)} custom-call(f32[26,4,128,128]{3,2,1,0:T(8,128)S(1)} %copy-done.1), custom_call_target="tpu_custom_call" | custom-call | bytes 13631488 | tf_op jit(solution)/shard_map/split_blocks/pallas_call | solution.py:430
  111.6 2.8 %copy-done = bf16[26,512,256]{2,1,0:T(8,128)(2,1)} copy-done((bf16[26,512,256]{2,1,0:T(8,128)(2,1)}, bf16[26,512,256]{2,1,0:T(8,128)(2,1)S(1)}, u32[]{:S(2)}) %copy-start) | copy-done | bytes 6815768
  114.4 6.6 %all-to-all-done.r_ref = f32[8,32,3072]{2,1,0:T(8,128)} async-done(((f32[8,32,3072]{2,1,0:T(8,128)}), f32[8,32,3072]{2,1,0:T(8,128)}, u32[]{:S(2)}, u32[]{:S(2)}) %all-to-all-start) | async-done | bytes 3145760 | tf_op jit(solution)/shard_map/all_to_all | solution.py:499
  121.0 3.8 %all-to-all-start.1 = ((f32[8,32,2048]{2,1,0:T(8,128)}), f32[8,32,2048]{2,1,0:T(8,128)S(1)}, u32[]{:S(2)}, u32[]{:S(2)}) async-start(f32[8,32,2048]{2,1,0:T(8,128)} %bitcast.42), calls=%async_computation.1 | async-start | bytes 4194304 | tf_op jit(solution)/shard_map/all_to_all | solution.py:499
  125.2 19.4 %element.3 = (f32[96,64,256]{2,1,0:T(8,128)}, bf16[96,3584]{1,0:T(8,128)(2,1)S(1)}, bf16[96,3584]{1,0:T(8,128)(2,1)S(1)}) custom-call(f32[96,64,256]{2,1,0:T(8,128)} %bitcast.36, f32[8,32,3072]{2,1,0:T(8,128)} %all-to-all-done.r_ref, f32[64,64,256]{2,1,0:T(8,128)} %a_ref.5, f32[8,8,256]{2,1,0:T(8,128)S(1)} %bitcast.31, f32[32,128]{1,0:T(8,128)S(1)} %broadcast_in_dim.13.helm_ref), custom_call_target="tpu_custom_call" | custom-call | flops 100663296 | bytes 12582912 | tf_op jit(solution)/shard_map/element/pallas_call | solution.py:361
  145.1 5.4 %assemble.2.refs_5_ = f32[96,3584]{1,0:T(8,128)S(1)} custom-call(bf16[96,3584]{1,0:T(8,128)(2,1)S(1)} %get-tuple-element.85.refs_0_, bf16[96,3584]{1,0:T(8,128)(2,1)S(1)} %get-tuple-element.86.refs_1_, s32[3584,128]{1,0:T(8,128)S(1)} %broadcast_in_dim.30.refs_2_), custom_call_target="tpu_custom_call" | custom-call | flops 4932501504 | bytes 4587520 | tf_op jit(solution)/shard_map/assemble/pallas_call | solution.py:404
  151.7 4.1 %all-to-all-start.2 = ((f32[8,32,1024]{2,1,0:T(8,128)}), f32[8,32,1024]{2,1,0:T(8,128)S(1)}, u32[]{:S(2)}, u32[]{:S(2)}) async-start(f32[8,32,1024]{2,1,0:T(8,128)} %bitcast.43), calls=%async_computation.2 | async-start | bytes 2097152 | tf_op jit(solution)/shard_map/all_to_all | solution.py:499
  155.9 13.7 %element.4 = (f32[96,64,256]{2,1,0:T(8,128)}, bf16[64,3584]{1,0:T(8,128)(2,1)S(1)}, bf16[64,3584]{1,0:T(8,128)(2,1)S(1)}) custom-call(f32[96,64,256]{2,1,0:T(8,128)} %bitcast.37, f32[8,32,2048]{2,1,0:T(8,128)S(1)} %all-to-all-done.1.r_ref, f32[64,64,256]{2,1,0:T(8,128)} %a_ref.5, f32[8,8,256]{2,1,0:T(8,128)S(1)} %bitcast.32, ...), custom_call_target="tpu_custom_call", output_to_operand_aliasing={{0}: (5, {})} | custom-call | flops 67108864 | bytes 8388608 | tf_op jit(solution)/shard_map/element/pallas_call | solution.py:361
  171.2 8.3 %element.5 = (f32[96,64,256]{2,1,0:T(8,128)}, bf16[32,3584]{1,0:T(8,128)(2,1)S(1)}, bf16[32,3584]{1,0:T(8,128)(2,1)S(1)}) custom-call(f32[96,64,256]{2,1,0:T(8,128)} %bitcast.38, f32[8,32,1024]{2,1,0:T(8,128)S(1)} %all-to-all-done.2.r_ref, f32[64,64,256]{2,1,0:T(8,128)} %a_ref.5, f32[8,8,256]{2,1,0:T(8,128)S(1)} %bitcast.33, ...), custom_call_target="tpu_custom_call", output_to_operand_aliasing={{0}: (5, {})} | custom-call | flops 33554432 | bytes 4194304 | tf_op jit(solution)/shard_map/element/pallas_call | solution.py:361
  180.7 5.6 %assemble.3.x_ref = f32[96,3584]{1,0:T(8,128)S(1)} custom-call(bf16[64,3584]{1,0:T(8,128)(2,1)S(1)} %copy-done.6, bf16[32,3584]{1,0:T(8,128)(2,1)S(1)} %get-tuple-element.97.refs_1_, bf16[64,3584]{1,0:T(8,128)(2,1)S(1)} %copy-done.8, bf16[32,3584]{1,0:T(8,128)(2,1)S(1)} %get-tuple-element.99.refs_3_, s32[3584,128]{1,0:T(8,128)S(1)} %broadcast_in_dim.32.refs_4_, ...), custom_call_target="tpu_custom_call" | custom-call | flops 4932501504 | bytes 4587520 | tf_op jit(solution)/shard_map/assemble/pallas_call | solution.py:404
  186.3 3.5 %collective-permute-start.14 = (f32[96,384]{1,0:T(8,128)S(1)}, f32[96,384]{1,0:T(8,128)S(1)}, u32[]{:S(2)}, u32[]{:S(2)}) collective-permute-start(f32[96,384]{1,0:T(8,128)S(1)} %slice.96), channel_id=1, source_target_pairs={{0,1},{1,2},{2,3},{4,5},{5,6},{6,7},{8,9},{9,10},{10,11},{12,13},{... | collective-permute-start | bytes 442376 | tf_op jit(solution)/shard_map/ppermute | solution.py:572
  191.2 4.2 %coupling.2.refs_0_ = f32[96,3328]{1,0:T(8,128)} custom-call(s32[26,4]{1,0:T(8,128)S(1)} %get-tuple-element.105.cols_ref, s32[5]{0:T(128)S(1)} %copy-done.4, f32[96,3584]{1,0:T(8,128)S(1)} %assemble.3.x_ref, bf16[26,512,256]{2,1,0:T(8,128)(2,1)S(1)} %bitcast.30), custom_call_target="tpu_custom_call" | custom-call | flops 1006632960 | bytes 5242880 | tf_op jit(solution)/shard_map/coupling/pallas_call | solution.py:476
  196.7 2.9 %coupling.3 = f32[96,3328]{1,0:T(8,128)} custom-call(s32[26,4]{1,0:T(8,128)S(1)} %get-tuple-element.104.cols_ref, s32[3]{0:T(128)S(1)} %copy-done.3, f32[96,3840]{1,0:T(8,128)S(1)} %slice_dynamic-update-slice_fusion.2.x_ref, bf16[26,512,256]{2,1,0:T(8,128)(2,1)S(1)} %bitcast.30, f32[96,3328]{1,0:T(8,128)} %coupling.2.refs_0_), custom_call_target="tpu_custom_call", output_to_operand_aliasing={{}: (4, {})} | custom-call | flops 301989888 | bytes 1572864 | tf_op jit(solution)/shard_map/coupling/pallas_call | solution.py:476
  (121 shorter events, 13.9 us)
Async XLA Ops:
  0.6 12.5 %copy-start.15 = (bf16[16,8]{1,0:T(8,128)(2,1)S(1)}, bf16[16,8]{1,0:T(8,128)(2,1)}, u32[]{:S(2)}) copy-start(bf16[16,8]{1,0:T(8,128)(2,1)} %constant.134) | copy-start | bytes 772
  0.6 12.6 %copy-start.14 = (bf16[16,8]{1,0:T(8,128)(2,1)S(1)}, bf16[16,8]{1,0:T(8,128)(2,1)}, u32[]{:S(2)}) copy-start(bf16[16,8]{1,0:T(8,128)(2,1)} %constant.135) | copy-start | bytes 772
  5.8 7.5 %collective-permute-start = (f32[32,3072]{1,0:T(8,128)}, f32[32,3072]{1,0:T(8,128)S(1)}, u32[]{:S(2)}, u32[]{:S(2)}) collective-permute-start(f32[32,3072]{1,0:T(8,128)} %get-tuple-element.54), channel_id=1, source_target_pairs={{0,4},{4,0},{8,12},{12,8},{16,20},{20,16},{24,28},{28,24},{1,5},{5... | collective-permute-start | bytes 1179656 | tf_op jit(solution)/shard_map/ppermute | solution.py:169
  6.3 13.8 %collective-permute-start.2 = (f32[32,3072]{1,0:T(8,128)}, f32[32,3072]{1,0:T(8,128)S(1)}, u32[]{:S(2)}, u32[]{:S(2)}) collective-permute-start(f32[32,3072]{1,0:T(8,128)} %get-tuple-element.59), channel_id=1, source_target_pairs={{0,24},{4,28},{8,16},{12,20},{16,8},{20,12},{24,0},{28,4},{1,25},{... | collective-permute-start | bytes 1179656 | tf_op jit(solution)/shard_map/ppermute | solution.py:169
  9.8 18.2 %collective-permute-start.3 = (f32[32,3072]{1,0:T(8,128)}, f32[32,3072]{1,0:T(8,128)S(1)}, u32[]{:S(2)}, u32[]{:S(2)}) collective-permute-start(f32[32,3072]{1,0:T(8,128)} %get-tuple-element.60), channel_id=1, source_target_pairs={{0,28},{4,24},{8,20},{12,16},{16,12},{20,8},{24,4},{28,0},{1,29},{... | collective-permute-start | bytes 1179656 | tf_op jit(solution)/shard_map/ppermute | solution.py:169
  9.9 27.6 %collective-permute-start.4 = (f32[32,3072]{1,0:T(8,128)}, f32[32,3072]{1,0:T(8,128)}, u32[]{:S(2)}, u32[]{:S(2)}) collective-permute-start(f32[32,3072]{1,0:T(8,128)} %get-tuple-element.61), channel_id=1, source_target_pairs={{0,8},{4,12},{8,0},{12,4},{16,24},{20,28},{24,16},{28,20},{1,9},{5... | collective-permute-start | bytes 1179656 | tf_op jit(solution)/shard_map/ppermute | solution.py:169
  11.6 26.0 %collective-permute-start.5 = (f32[32,3072]{1,0:T(8,128)}, f32[32,3072]{1,0:T(8,128)}, u32[]{:S(2)}, u32[]{:S(2)}) collective-permute-start(f32[32,3072]{1,0:T(8,128)} %get-tuple-element.62), channel_id=1, source_target_pairs={{0,16},{4,20},{8,24},{12,28},{16,0},{20,4},{24,8},{28,12},{1,17},{... | collective-permute-start | bytes 1179656 | tf_op jit(solution)/shard_map/ppermute | solution.py:169
  13.3 5.3 %copy-start.16 = (f32[32,3072]{1,0:T(8,128)}, f32[32,3072]{1,0:T(8,128)S(1)}, u32[]{:S(2)}) copy-start(f32[32,3072]{1,0:T(8,128)S(1)} %collective-permute-done.refs_1_) | copy-start | bytes 1179652
  18.6 11.2 %collective-permute-start.1 = (f32[32,3072]{1,0:T(8,128)}, f32[32,3072]{1,0:T(8,128)S(1)}, u32[]{:S(2)}, u32[]{:S(2)}) collective-permute-start(f32[32,3072]{1,0:T(8,128)} %get-tuple-element.56), channel_id=1, source_target_pairs={{0,4},{4,0},{8,12},{12,8},{16,20},{20,16},{24,28},{28,24},{1,5},{5... | collective-permute-start | bytes 1179656 | tf_op jit(solution)/shard_map/ppermute | solution.py:169
  20.1 13.1 %copy-start.17 = (f32[32,3072]{1,0:T(8,128)}, f32[32,3072]{1,0:T(8,128)S(1)}, u32[]{:S(2)}) copy-start(f32[32,3072]{1,0:T(8,128)S(1)} %collective-permute-done.2.refs_2_) | copy-start | bytes 1179652
  20.1 24.9 %collective-permute-start.6 = (f32[32,3072]{1,0:T(8,128)}, f32[32,3072]{1,0:T(8,128)}, u32[]{:S(2)}, u32[]{:S(2)}) collective-permute-start(f32[32,3072]{1,0:T(8,128)} %get-tuple-element.63), channel_id=1, source_target_pairs={{0,12},{4,8},{8,4},{12,0},{16,28},{20,24},{24,20},{28,16},{1,13},{... | collective-permute-start | bytes 1179656 | tf_op jit(solution)/shard_map/ppermute | solution.py:169
  28.1 17.7 %collective-permute-start.7 = (f32[32,3072]{1,0:T(8,128)}, f32[32,3072]{1,0:T(8,128)}, u32[]{:S(2)}, u32[]{:S(2)}) collective-permute-start(f32[32,3072]{1,0:T(8,128)} %get-tuple-element.64), channel_id=1, source_target_pairs={{0,20},{4,16},{8,28},{12,24},{16,4},{20,0},{24,12},{28,8},{1,21},{... | collective-permute-start | bytes 1179656 | tf_op jit(solution)/shard_map/ppermute | solution.py:169
  29.9 24.5 %collective-permute-start.10 = (f32[32,3072]{1,0:T(8,128)}, f32[32,3072]{1,0:T(8,128)}, u32[]{:S(2)}, u32[]{:S(2)}) collective-permute-start(f32[32,3072]{1,0:T(8,128)} %get-tuple-element.69), channel_id=1, source_target_pairs={{0,8},{4,12},{8,0},{12,4},{16,24},{20,28},{24,16},{28,20},{1,9},{5... | collective-permute-start | bytes 1179656 | tf_op jit(solution)/shard_map/ppermute | solution.py:169
  33.2 12.5 %copy-start.21 = (f32[32,3072]{1,0:T(8,128)S(1)}, f32[32,3072]{1,0:T(8,128)}, u32[]{:S(2)}) copy-start(f32[32,3072]{1,0:T(8,128)} %get-tuple-element.67) | copy-start | bytes 1179652
  33.2 21.1 %copy-start.20 = (f32[32,3072]{1,0:T(8,128)S(1)}, f32[32,3072]{1,0:T(8,128)}, u32[]{:S(2)}) copy-start(f32[32,3072]{1,0:T(8,128)} %get-tuple-element.68) | copy-start | bytes 1179652
  33.3 11.8 %copy-start.22 = (f32[32,3072]{1,0:T(8,128)S(1)}, f32[32,3072]{1,0:T(8,128)}, u32[]{:S(2)}) copy-start(f32[32,3072]{1,0:T(8,128)} %get-tuple-element.72) | copy-start | bytes 1179652
  37.5 39.7 %collective-permute-start.11 = (f32[32,3072]{1,0:T(8,128)}, f32[32,3072]{1,0:T(8,128)S(1)}, u32[]{:S(2)}, u32[]{:S(2)}) collective-permute-start(f32[32,3072]{1,0:T(8,128)} %get-tuple-element.70), channel_id=1, source_target_pairs={{0,16},{4,20},{8,24},{12,28},{16,0},{20,4},{24,8},{28,12},{1,17},{... | collective-permute-start | bytes 1179656 | tf_op jit(solution)/shard_map/ppermute | solution.py:169
  37.6 39.6 %collective-permute-start.12 = (f32[32,3072]{1,0:T(8,128)S(1)}, f32[32,3072]{1,0:T(8,128)S(1)}, u32[]{:S(2)}, u32[]{:S(2)}) collective-permute-start(f32[32,3072]{1,0:T(8,128)S(1)} %copy-done.23), channel_id=1, source_target_pairs={{0,12},{4,8},{8,4},{12,0},{16,28},{20,24},{24,20},{28,16},{1,13},{... | collective-permute-start | bytes 1179656 | tf_op jit(solution)/shard_map/ppermute | solution.py:169
  45.0 32.2 %collective-permute-start.13 = (f32[32,3072]{1,0:T(8,128)S(1)}, f32[32,3072]{1,0:T(8,128)S(1)}, u32[]{:S(2)}, u32[]{:S(2)}) collective-permute-start(f32[32,3072]{1,0:T(8,128)S(1)} %copy-done.22), channel_id=1, source_target_pairs={{0,20},{4,16},{8,28},{12,24},{16,4},{20,0},{24,12},{28,8},{1,21},{... | collective-permute-start | bytes 1179656 | tf_op jit(solution)/shard_map/ppermute | solution.py:169
  45.7 31.5 %collective-permute-start.8 = (f32[32,3072]{1,0:T(8,128)S(1)}, f32[32,3072]{1,0:T(8,128)}, u32[]{:S(2)}, u32[]{:S(2)}) collective-permute-start(f32[32,3072]{1,0:T(8,128)S(1)} %copy-done.21), channel_id=1, source_target_pairs={{0,24},{4,28},{8,16},{12,20},{16,8},{20,12},{24,0},{28,4},{1,25},{... | collective-permute-start | bytes 1179656 | tf_op jit(solution)/shard_map/ppermute | solution.py:169
  54.3 24.3 %collective-permute-start.9 = (f32[32,3072]{1,0:T(8,128)S(1)}, f32[32,3072]{1,0:T(8,128)}, u32[]{:S(2)}, u32[]{:S(2)}) collective-permute-start(f32[32,3072]{1,0:T(8,128)S(1)} %copy-done.20), channel_id=1, source_target_pairs={{0,28},{4,24},{8,20},{12,16},{16,12},{20,8},{24,4},{28,0},{1,29},{... | collective-permute-start | bytes 1179656 | tf_op jit(solution)/shard_map/ppermute | solution.py:169
  78.7 42.4 %all-to-all-start = ((f32[8,32,3072]{2,1,0:T(8,128)}), f32[8,32,3072]{2,1,0:T(8,128)}, u32[]{:S(2)}, u32[]{:S(2)}) async-start(f32[8,32,3072]{2,1,0:T(8,128)} %bitcast.41), calls=%async_computation | async-start | bytes 6291456 | tf_op jit(solution)/shard_map/all_to_all | solution.py:499
  114.4 10.5 %copy-start.27 = (f32[256]{0:T(256)S(1)}, f32[256]{0:T(256)}, u32[]{:S(2)}) copy-start(f32[256]{0:T(256)} %constant.121.clone) | copy-start | bytes 3076
  114.4 10.8 %copy-start.2 = (f32[64,256]{1,0:T(8,128)S(1)}, f32[64,256]{1,0:T(8,128)}, u32[]{:S(2)}) copy-start(f32[64,256]{1,0:T(8,128)} %param.28) | copy-start | bytes 196612
  121.0 30.7 %all-to-all-start.1 = ((f32[8,32,2048]{2,1,0:T(8,128)}), f32[8,32,2048]{2,1,0:T(8,128)S(1)}, u32[]{:S(2)}, u32[]{:S(2)}) async-start(f32[8,32,2048]{2,1,0:T(8,128)} %bitcast.42), calls=%async_computation.1 | async-start | bytes 4194304 | tf_op jit(solution)/shard_map/all_to_all | solution.py:499
  151.7 19.5 %all-to-all-start.2 = ((f32[8,32,1024]{2,1,0:T(8,128)}), f32[8,32,1024]{2,1,0:T(8,128)S(1)}, u32[]{:S(2)}, u32[]{:S(2)}) async-start(f32[8,32,1024]{2,1,0:T(8,128)} %bitcast.43), calls=%async_computation.2 | async-start | bytes 2097152 | tf_op jit(solution)/shard_map/all_to_all | solution.py:499
  171.2 8.9 %copy-start.10 = (f32[96,3584]{1,0:T(8,128)S(1)}, f32[96,3584]{1,0:T(8,128)}, u32[]{:S(2)}) copy-start(f32[96,3584]{1,0:T(8,128)} %copy-done.9) | copy-start | bytes 4128772
  179.6 11.6 %slice-start = ((s8[6815744]{0:T(1024)(128)(4,1)}), s8[4194304]{0:T(1024)(128)(4,1)S(1)}, s32[]{:S(2)}) async-start(s8[6815744]{0:T(1024)(128)(4,1)} %bitcast.29), calls=%async_computation.3 | async-start | bytes 8388608
  180.7 10.5 %slice-start.1 = ((s8[6815744]{0:T(1024)(128)(4,1)}), s8[2621440]{0:T(1024)(128)(4,1)S(1)}, s32[]{:S(2)}) async-start(s8[6815744]{0:T(1024)(128)(4,1)} %bitcast.29), calls=%async_computation.4 | async-start | bytes 5242880
  180.7 10.5 %copy-start.4 = (s32[5]{0:T(128)S(1)}, s32[5]{0:T(128)}, u32[]{:S(2)}) copy-start(s32[5]{0:T(128)} %constant.128.clone.at_ref) | copy-start | bytes 64
  186.3 9.1 %collective-permute-start.14 = (f32[96,384]{1,0:T(8,128)S(1)}, f32[96,384]{1,0:T(8,128)S(1)}, u32[]{:S(2)}, u32[]{:S(2)}) collective-permute-start(f32[96,384]{1,0:T(8,128)S(1)} %slice.96), channel_id=1, source_target_pairs={{0,1},{1,2},{2,3},{4,5},{5,6},{6,7},{8,9},{9,10},{10,11},{12,13},{... | collective-permute-start | bytes 442376 | tf_op jit(solution)/shard_map/ppermute | solution.py:572
  189.9 6.8 %collective-permute-start.15 = (f32[96,256]{1,0:T(8,128)S(1)}, f32[96,256]{1,0:T(8,128)S(1)}, u32[]{:S(2)}, u32[]{:S(2)}) collective-permute-start(f32[96,256]{1,0:T(8,128)S(1)} %slice.101), channel_id=1, source_target_pairs={{1,0},{2,1},{3,2},{5,4},{6,5},{7,6},{9,8},{10,9},{11,10},{13,12},{... | collective-permute-start | bytes 294920 | tf_op jit(solution)/shard_map/ppermute | solution.py:573
  (17 other events, 41.1 us)
